TPU v7x, 512 devices: a whole 4x8x8 slice. The times are simulated.
512 devices in a mesh: panel: 2 (over z_hi), colat: 16 (over z_lo, x), lon: 16 (over y, core).
Axes of the slice: x: 4, y: 8, z: 8 (z_hi: 2, z_lo: 4; z = z_hi * 4 + z_lo), core: 2. Of those that a mesh axis runs over, the one named last changes fastest.
Arguments:
- fields_now: float32 [4, 2, 256, 512, 128], P(None, 'panel', 'colat', 'lon'), may hold values from -6 to 6
- diffusivity: float32 [2, 256, 512, 128], P('panel', 'colat', 'lon'), may hold values from 0.5 to 2
- viscosity: float32 [2, 256, 512, 128], P('panel', 'colat', 'lon'), may hold values from 0.5 to 2
- donor_row: int32 [2, 16, 16, 12], P('panel', 'colat', 'lon'), may hold values from 0 to 16
- donor_column: int32 [2, 16, 16, 12], P('panel', 'colat', 'lon'), may hold values from 0 to 32
- donor_offset: float32 [2, 16, 16, 2, 12], P('panel', 'colat', 'lon'), may hold values from 0 to 1
- rim_angle: float32 [2, 16, 16, 12], P('panel', 'colat', 'lon'), may hold values from -3.140625 to 3.140625
Outputs:
- advanced: float32 [4, 2, 256, 512, 128], P(None, 'panel', 'colat', 'lon')
All inputs are finite; a program needn't handle non-finite values.
Results may differ from a plain program's by a relative error of at most 0.00002.
Values sent between devices are 32-bit elements; how exact they have to be, the bound alone decides.
A program may use at most 64 MiB of HBM per device.

v0:
```python
import jax
import jax.numpy as jnp
from jax import lax
from jax.sharding import PartitionSpec as P

TIME_STEP = 0.05
BUOYANCY = 1.0


def with_halo(x, sides, width):
    for axis, dim in sides:
        count, length = (lax.axis_size(axis), x.shape[dim])
        up = [(i, (i + 1) % count) for i in range(count - 1)]
        down = [(j, i) for i, j in up]
        last = lax.slice_in_dim(x, length - width, length, axis=dim)
        leading = lax.slice_in_dim(x, 0, width, axis=dim)
        before = lax.ppermute(last, axis, up)
        after = lax.ppermute(leading, axis, down)
        x = jnp.concatenate([before, x, after], axis=dim)
    return x


def swapped(block, axis, stride):
    count = lax.axis_size(axis)
    route = []
    for low in range(count):
        high = low | 1 << stride
        if high != low and high < count:
            route += [(low, high), (high, low)]
    return lax.ppermute(block, axis, route)


def gradient(stencil):
    return (8.0 * (stencil[3] - stencil[1]) - (stencil[4] - stencil[0])) / 12.0


def curvature(stencil):
    return (16.0 * (stencil[3] + stencil[1]) - (stencil[4] + stencil[0]) - 30.0 * stencil[2]) / 12.0


def advance(padded, thermal, viscous):
    height = padded.shape[1] - 4
    breadth = padded.shape[2] - 4
    center = padded[:, 2 : 2 + height, 2 : 2 + breadth]
    radial_len = center.shape[3]
    radial_pad = jnp.pad(center, ((0, 0), (0, 0), (0, 0), (2, 2)))
    along_lat = [padded[:, offset : offset + height, 2 : 2 + breadth] for offset in range(5)]
    along_lon = [padded[:, 2 : 2 + height, offset : offset + breadth] for offset in range(5)]
    along_rad = [radial_pad[..., offset : offset + radial_len] for offset in range(5)]
    laplace = curvature(along_rad) + curvature(along_lat) + curvature(along_lon)
    transport = (
        center[1:2] * gradient(along_rad)
        + center[2:3] * gradient(along_lat)
        + center[3:4] * gradient(along_lon)
    )
    diffusion = jnp.stack([thermal, viscous, viscous, viscous])
    change = diffusion * laplace - transport
    change = change.at[1].add(BUOYANCY * center[0])
    return center + TIME_STEP * change


def local(fields_now, diffusivity, viscosity, donor_row, donor_column, donor_offset, rim_angle):
    fields = fields_now[:, 0]
    thermal = diffusivity[0]
    viscous = viscosity[0]
    height = fields.shape[1]
    breadth = fields.shape[2]
    radial_len = fields.shape[3]
    colat_pos = lax.axis_index("colat")
    lon_pos = lax.axis_index("lon")
    colat_count = lax.axis_size("colat")
    lon_count = lax.axis_size("lon")
    row_share = 4 * breadth // colat_count
    padded = with_halo(fields, (("colat", 1), ("lon", 2)), 2)
    fresh = advance(padded, thermal, viscous)
    extended = with_halo(fresh, (("colat", 1), ("lon", 2)), 1)
    width = breadth + 2
    flattened = extended.reshape(4, (height + 2) * width, radial_len)
    anchor = donor_row.reshape(-1) * width + donor_column.reshape(-1)

    def corner(offset):
        return jnp.take(flattened, anchor + offset, axis=1)

    frac_row = donor_offset[0, 0, 0, 0][None, :, None]
    frac_lon = donor_offset[0, 0, 0, 1][None, :, None]
    blended = (1.0 - frac_row) * (
        (1.0 - frac_lon) * corner(0) + frac_lon * corner(1)
    ) + frac_row * ((1.0 - frac_lon) * corner(width) + frac_lon * corner(width + 1))
    angles = rim_angle.reshape(-1)
    cosine = jnp.cos(angles)[:, None]
    sine_part = jnp.sin(angles)[:, None]
    turned_lat = cosine * blended[2] - sine_part * blended[3]
    turned_lon = sine_part * blended[2] + cosine * blended[3]
    blended = jnp.stack([blended[0], blended[1], turned_lat, turned_lon])
    arrived = swapped(blended, "panel", 0)
    row_full = lax.all_gather(arrived[:, 0:row_share], "colat", axis=1, tiled=True)
    col_full = lax.all_gather(arrived[:, row_share:], "lon", axis=1, tiled=True)
    col_blocks = col_full.reshape(4, 4, height, radial_len)
    west_strip = jnp.transpose(
        jnp.stack([col_blocks[:, 0], col_blocks[:, 2]], axis=1), (0, 2, 1, 3)
    )
    east_strip = jnp.transpose(
        jnp.stack([col_blocks[:, 3], col_blocks[:, 1]], axis=1), (0, 2, 1, 3)
    )
    fresh = fresh.at[:, :, 0:2].set(jnp.where(lon_pos == 0, west_strip, fresh[:, :, 0:2]))
    fresh = fresh.at[:, :, breadth - 2 :].set(
        jnp.where(lon_pos == lon_count - 1, east_strip, fresh[:, :, breadth - 2 :])
    )
    row_blocks = row_full.reshape(4, 4, breadth, radial_len)
    north_strip = jnp.stack([row_blocks[:, 0], row_blocks[:, 2]], axis=1)
    south_strip = jnp.stack([row_blocks[:, 3], row_blocks[:, 1]], axis=1)
    fresh = fresh.at[:, 0:2].set(jnp.where(colat_pos == 0, north_strip, fresh[:, 0:2]))
    fresh = fresh.at[:, height - 2 :].set(
        jnp.where(colat_pos == colat_count - 1, south_strip, fresh[:, height - 2 :])
    )
    return fresh[:, None]


def solution(mesh):
    placed = (
        P(None, "panel", "colat", "lon", None),
        P("panel", "colat", "lon", None),
        P("panel", "colat", "lon", None),
        P("panel", "colat", "lon", None),
        P("panel", "colat", "lon", None),
        P("panel", "colat", "lon", None, None),
        P("panel", "colat", "lon", None),
    )
    return jax.shard_map(
        local,
        mesh=mesh,
        in_specs=placed,
        out_specs=P(None, "panel", "colat", "lon", None),
        check_vma=False,
    )
```

profile of v0, /device:TPU:8, one launch (start us, length us, event | category | flops | bytes accessed | tf_op | source)
XLA Modules:
  0.0 119.7 jit_solution(8745832736168921647)
XLA Ops:
  0.0 1.9 %copy.67 = f32[4,1,16,32,128]{4,2,3,0,1:T(8,128)S(1)} copy(f32[4,1,16,32,128]{4,3,2,1,0:T(8,128)} %param.19) | data formatting | bytes 2097152 | tf_op args[0]
  1.9 0.1 fusion.16
  2.0 1.3 %collective-permute-start = (f32[4,2,32,128]{3,1,2,0:T(2,128)S(1)}, f32[4,2,32,128]{3,1,2,0:T(2,128)S(1)}, u32[]{:S(2)}, u32[]{:S(2)}) collective-permute-start(f32[4,2,32,128]{3,1,2,0:T(2,128)S(1)} %get-tuple-element.87), channel_id=1, source_target_pairs={{16,0},{32,16},{48,32},{64,48},{80,64},{96,80},{112,96},{128,112},... | collective-permute-start | bytes 393224 | tf_op jit(solution)/shard_map/ppermute | solution.py:18
  3.3 0.0 copy-start.1
  3.4 4.7 %collective-permute-start.1 = (f32[4,2,32,128]{3,1,2,0:T(2,128)S(1)}, f32[4,2,32,128]{3,1,2,0:T(2,128)S(1)}, u32[]{:S(2)}, u32[]{:S(2)}) collective-permute-start(f32[4,2,32,128]{3,1,2,0:T(2,128)S(1)} %get-tuple-element.86), channel_id=1, source_target_pairs={{0,16},{16,32},{32,48},{48,64},{64,80},{80,96},{96,112},{112,128},... | collective-permute-start | bytes 393224 | tf_op jit(solution)/shard_map/ppermute | solution.py:17
  8.1 0.1 fusion.15
  8.2 0.0 copy-start.6
  8.3 0.2 copy.42
  8.4 0.2 copy.43
  8.6 0.2 copy.44
  8.8 0.2 copy.38
  9.0 0.2 copy.39
  9.2 1.3 %collective-permute-done.1 = f32[4,2,32,128]{3,1,2,0:T(2,128)S(1)} collective-permute-done((f32[4,2,32,128]{3,1,2,0:T(2,128)S(1)}, f32[4,2,32,128]{3,1,2,0:T(2,128)S(1)}, u32[]{:S(2)}, u32[]{:S(2)}) %collective-permute-start.1) | collective-permute-done | bytes 131104 | tf_op jit(solution)/shard_map/ppermute | solution.py:17
  10.6 1.9 %collective-permute-start.2 = (f32[4,20,2,128]{3,1,2,0:T(8,128)S(1)}, f32[4,20,2,128]{3,1,2,0:T(8,128)S(1)}, u32[]{:S(2)}, u32[]{:S(2)}) collective-permute-start(f32[4,20,2,128]{3,1,2,0:T(8,128)S(1)} %get-tuple-element.76), channel_id=1, source_target_pairs={{1,0},{2,1},{3,2},{4,3},{5,4},{6,5},{7,6},{8,7},{9,8},{10,9},{11,1... | collective-permute-start | bytes 245768 | tf_op jit(solution)/shard_map/ppermute | solution.py:18
  12.5 2.4 %collective-permute-start.3 = (f32[4,20,2,128]{3,1,2,0:T(8,128)S(1)}, f32[4,20,2,128]{3,1,2,0:T(8,128)S(1)}, u32[]{:S(2)}, u32[]{:S(2)}) collective-permute-start(f32[4,20,2,128]{3,1,2,0:T(8,128)S(1)} %get-tuple-element.77), channel_id=1, source_target_pairs={{0,1},{1,2},{2,3},{3,4},{4,5},{5,6},{6,7},{7,8},{8,9},{9,10},{10,1... | collective-permute-start | bytes 245768 | tf_op jit(solution)/shard_map/ppermute | solution.py:17
  15.0 7.7 %collective-permute-done.3 = f32[4,20,2,128]{3,1,2,0:T(8,128)S(1)} collective-permute-done((f32[4,20,2,128]{3,1,2,0:T(8,128)S(1)}, f32[4,20,2,128]{3,1,2,0:T(8,128)S(1)}, u32[]{:S(2)}, u32[]{:S(2)}) %collective-permute-start.3) | collective-permute-done | bytes 81952 | tf_op jit(solution)/shard_map/ppermute | solution.py:17
  22.6 0.3 pad_maximum_fusion
  22.9 2.5 %fusion.2 = f32[4,16,32,128]{3,1,2,0:T(8,128)S(1)} fusion(f32[1,16,32,128]{3,1,2,0:T(8,128)S(1)} %copy.39, f32[1,16,32,128]{3,1,2,0:T(8,128)S(1)} %copy.38, f32[4,20,34,128]{3,1,2,0:T(8,128)S(1)} %get-tuple-element.75, f32[4,20,34,128]{3,1,2,0:T(8,128)S(1)} %get-tuple-element.74, f32[4,2,32,128]{3,1,2,0:T(2,128)S(1)} %collective-permute-done, ...), kind=kLoop, calls=%fused_computation.20 | loop fusion | flops 11796480 | bytes 7864320 | tf_op jit(solution)/shard_map/sub | solution.py:57
  25.4 0.2 fusion.3
  25.7 0.7 multiply_add_fusion
  26.3 0.1 fusion.14
  26.4 4.4 %collective-permute-start.4 = (f32[4,1,32,128]{3,1,2,0:T(1,128)S(1)}, f32[4,1,32,128]{3,1,2,0:T(1,128)S(1)}, u32[]{:S(2)}, u32[]{:S(2)}) collective-permute-start(f32[4,1,32,128]{3,1,2,0:T(1,128)S(1)} %get-tuple-element.80), channel_id=1, source_target_pairs={{0,16},{16,32},{32,48},{48,64},{64,80},{80,96},{96,112},{112,128},... | collective-permute-start | bytes 196616 | tf_op jit(solution)/shard_map/ppermute | solution.py:17
  30.8 1.3 %collective-permute-start.5 = (f32[4,1,32,128]{3,1,2,0:T(1,128)S(1)}, f32[4,1,32,128]{3,1,2,0:T(1,128)S(1)}, u32[]{:S(2)}, u32[]{:S(2)}) collective-permute-start(f32[4,1,32,128]{3,1,2,0:T(1,128)S(1)} %get-tuple-element.81), channel_id=1, source_target_pairs={{16,0},{32,16},{48,32},{64,48},{80,64},{96,80},{112,96},{128,112},... | collective-permute-start | bytes 196616 | tf_op jit(solution)/shard_map/ppermute | solution.py:18
  32.1 0.6 collective-permute-done.4
  32.7 4.3 %collective-permute-done.5 = f32[4,1,32,128]{3,1,2,0:T(1,128)S(1)} collective-permute-done((f32[4,1,32,128]{3,1,2,0:T(1,128)S(1)}, f32[4,1,32,128]{3,1,2,0:T(1,128)S(1)}, u32[]{:S(2)}, u32[]{:S(2)}) %collective-permute-start.5) | collective-permute-done | bytes 65568 | tf_op jit(solution)/shard_map/ppermute | solution.py:18
  37.0 1.9 %collective-permute-start.6 = (f32[4,18,1,128]{3,1,2,0:T(8,128)S(1)}, f32[4,18,1,128]{3,1,2,0:T(8,128)S(1)}, u32[]{:S(2)}, u32[]{:S(2)}) collective-permute-start(f32[4,18,1,128]{3,1,2,0:T(8,128)S(1)} %get-tuple-element.78), channel_id=1, source_target_pairs={{0,1},{1,2},{2,3},{3,4},{4,5},{5,6},{6,7},{7,8},{8,9},{9,10},{10,1... | collective-permute-start | bytes 110600 | tf_op jit(solution)/shard_map/ppermute | solution.py:17
  38.9 3.6 %collective-permute-start.7 = (f32[4,18,1,128]{3,1,2,0:T(8,128)S(1)}, f32[4,18,1,128]{3,1,2,0:T(8,128)S(1)}, u32[]{:S(2)}, u32[]{:S(2)}) collective-permute-start(f32[4,18,1,128]{3,1,2,0:T(8,128)S(1)} %get-tuple-element.79), channel_id=1, source_target_pairs={{1,0},{2,1},{3,2},{4,3},{5,4},{6,5},{7,6},{8,7},{9,8},{10,9},{11,1... | collective-permute-start | bytes 110600 | tf_op jit(solution)/shard_map/ppermute | solution.py:18
  42.6 1.7 %collective-permute-done.7 = f32[4,18,1,128]{3,1,2,0:T(8,128)S(1)} collective-permute-done((f32[4,18,1,128]{3,1,2,0:T(8,128)S(1)}, f32[4,18,1,128]{3,1,2,0:T(8,128)S(1)}, u32[]{:S(2)}, u32[]{:S(2)}) %collective-permute-start.7) | collective-permute-done | bytes 36896 | tf_op jit(solution)/shard_map/ppermute | solution.py:18
  44.3 0.3 pad_maximum_fusion.1
  44.6 0.5 copy.46
  45.0 0.6 gather_fusion.2
  45.6 0.6 gather_fusion.3
  46.2 0.6 gather_fusion.1
  46.8 0.6 gather_fusion
  47.4 0.2 fusion.11
  47.6 0.1 multiply_subtract_fusion
  47.7 6.7 %collective-permute-start.8 = (f32[4,12,128]{2,0,1:T(4,128)S(1)}, f32[4,12,128]{2,0,1:T(4,128)S(1)}, u32[]{:S(2)}, u32[]{:S(2)}) collective-permute-start(f32[4,12,128]{2,0,1:T(4,128)S(1)} %pad_maximum_fusion.10), channel_id=1, source_target_pairs={{0,256},{256,0},{1,257},{257,1},{2,258},{258,2},{3,259},{259,3},{4... | collective-permute-start | bytes 73736 | tf_op jit(solution)/shard_map/ppermute | solution.py:30
  54.4 3.1 %collective-permute-done.8 = f32[4,12,128]{2,0,1:T(4,128)S(1)} collective-permute-done((f32[4,12,128]{2,0,1:T(4,128)S(1)}, f32[4,12,128]{2,0,1:T(4,128)S(1)}, u32[]{:S(2)}, u32[]{:S(2)}) %collective-permute-start.8) | collective-permute-done | bytes 24608 | tf_op jit(solution)/shard_map/ppermute | solution.py:30
  57.5 17.1 %all_gather.6 = f32[4,64,128]{2,0,1:T(4,128)S(1)} all-gather(f32[4,4,128]{2,0,1:T(4,128)S(1)} %slice.349), channel_id=1, replica_groups=mesh['panel'=2,'colat'=16,'lon'=16] {'lon'}, dimensions={1}, use_global_device_ids=true | all-gather | bytes 139264 | tf_op jit(solution)/shard_map/all_gather | solution.py:97
  74.6 42.9 %all_gather.7 = f32[4,128,128]{2,0,1:T(4,128)S(1)} all-gather(f32[4,8,128]{2,0,1:T(4,128)S(1)} %slice.356), channel_id=1, replica_groups=mesh['panel'=2,'colat'=16,'lon'=16] {'colat'}, dimensions={1}, use_global_device_ids=true | all-gather | bytes 278528 | tf_op jit(solution)/shard_map/all_gather | solution.py:96
  117.6 0.1 copy.57
  117.6 0.1 copy.58
  117.8 0.2 fusion.6
  118.0 0.1 copy.72
  118.0 0.1 copy.59
  118.1 0.1 copy.60
  118.2 0.2 fusion.5
  118.4 1.3 %copy.53 = f32[4,1,16,32,128]{4,3,2,1,0:T(8,128)} copy(f32[4,1,16,32,128]{4,2,3,0,1:T(8,128)S(1)} %fusion.5) | data formatting | bytes 2097152 | tf_op jit(solution)/shard_map/scatter | solution.py:113
  (35 shorter events, 0.3 us)
Async XLA Ops:
  0.0 8.1 %copy-start = (f32[4,1,16,32,128]{4,3,2,1,0:T(8,128)S(1)}, f32[4,1,16,32,128]{4,3,2,1,0:T(8,128)}, u32[]{:S(2)}) copy-start(f32[4,1,16,32,128]{4,3,2,1,0:T(8,128)} %param.19) | copy-start | bytes 3145732
  1.9 6.3 %copy-start.3 = (f32[1,1,1,2,12]{4,3,2,1,0:T(2,128)S(1)}, f32[1,1,1,2,12]{4,3,2,1,0:T(2,128)}, u32[]{:S(2)}) copy-start(f32[1,1,1,2,12]{4,3,2,1,0:T(2,128)} %param.24) | copy-start | bytes 292
  2.0 7.2 %collective-permute-start = (f32[4,2,32,128]{3,1,2,0:T(2,128)S(1)}, f32[4,2,32,128]{3,1,2,0:T(2,128)S(1)}, u32[]{:S(2)}, u32[]{:S(2)}) collective-permute-start(f32[4,2,32,128]{3,1,2,0:T(2,128)S(1)} %get-tuple-element.87), channel_id=1, source_target_pairs={{16,0},{32,16},{48,32},{64,48},{80,64},{96,80},{112,96},{128,112},... | collective-permute-start | bytes 393224 | tf_op jit(solution)/shard_map/ppermute | solution.py:18
  3.3 5.4 %copy-start.1 = (f32[1,16,32,128]{3,2,1,0:T(8,128)S(1)}, f32[1,16,32,128]{3,2,1,0:T(8,128)}, u32[]{:S(2)}) copy-start(f32[1,16,32,128]{3,2,1,0:T(8,128)} %param.20) | copy-start | bytes 786436
  3.4 5.6 %copy-start.2 = (f32[1,16,32,128]{3,2,1,0:T(8,128)S(1)}, f32[1,16,32,128]{3,2,1,0:T(8,128)}, u32[]{:S(2)}) copy-start(f32[1,16,32,128]{3,2,1,0:T(8,128)} %param.21) | copy-start | bytes 786436
  3.4 7.2 %collective-permute-start.1 = (f32[4,2,32,128]{3,1,2,0:T(2,128)S(1)}, f32[4,2,32,128]{3,1,2,0:T(2,128)S(1)}, u32[]{:S(2)}, u32[]{:S(2)}) collective-permute-start(f32[4,2,32,128]{3,1,2,0:T(2,128)S(1)} %get-tuple-element.86), channel_id=1, source_target_pairs={{0,16},{16,32},{32,48},{48,64},{64,80},{80,96},{96,112},{112,128},... | collective-permute-start | bytes 393224 | tf_op jit(solution)/shard_map/ppermute | solution.py:17
  8.2 0.9 copy-start.4
  8.2 0.9 copy-start.5
  8.2 0.9 copy-start.6
  10.6 4.4 %collective-permute-start.2 = (f32[4,20,2,128]{3,1,2,0:T(8,128)S(1)}, f32[4,20,2,128]{3,1,2,0:T(8,128)S(1)}, u32[]{:S(2)}, u32[]{:S(2)}) collective-permute-start(f32[4,20,2,128]{3,1,2,0:T(8,128)S(1)} %get-tuple-element.76), channel_id=1, source_target_pairs={{1,0},{2,1},{3,2},{4,3},{5,4},{6,5},{7,6},{8,7},{9,8},{10,9},{11,1... | collective-permute-start | bytes 245768 | tf_op jit(solution)/shard_map/ppermute | solution.py:18
  12.5 10.1 %collective-permute-start.3 = (f32[4,20,2,128]{3,1,2,0:T(8,128)S(1)}, f32[4,20,2,128]{3,1,2,0:T(8,128)S(1)}, u32[]{:S(2)}, u32[]{:S(2)}) collective-permute-start(f32[4,20,2,128]{3,1,2,0:T(8,128)S(1)} %get-tuple-element.77), channel_id=1, source_target_pairs={{0,1},{1,2},{2,3},{3,4},{4,5},{5,6},{6,7},{7,8},{8,9},{9,10},{10,1... | collective-permute-start | bytes 245768 | tf_op jit(solution)/shard_map/ppermute | solution.py:17
  26.4 6.2 %collective-permute-start.4 = (f32[4,1,32,128]{3,1,2,0:T(1,128)S(1)}, f32[4,1,32,128]{3,1,2,0:T(1,128)S(1)}, u32[]{:S(2)}, u32[]{:S(2)}) collective-permute-start(f32[4,1,32,128]{3,1,2,0:T(1,128)S(1)} %get-tuple-element.80), channel_id=1, source_target_pairs={{0,16},{16,32},{32,48},{48,64},{64,80},{80,96},{96,112},{112,128},... | collective-permute-start | bytes 196616 | tf_op jit(solution)/shard_map/ppermute | solution.py:17
  30.8 6.2 %collective-permute-start.5 = (f32[4,1,32,128]{3,1,2,0:T(1,128)S(1)}, f32[4,1,32,128]{3,1,2,0:T(1,128)S(1)}, u32[]{:S(2)}, u32[]{:S(2)}) collective-permute-start(f32[4,1,32,128]{3,1,2,0:T(1,128)S(1)} %get-tuple-element.81), channel_id=1, source_target_pairs={{16,0},{32,16},{48,32},{64,48},{80,64},{96,80},{112,96},{128,112},... | collective-permute-start | bytes 196616 | tf_op jit(solution)/shard_map/ppermute | solution.py:18
  37.0 5.6 %collective-permute-start.6 = (f32[4,18,1,128]{3,1,2,0:T(8,128)S(1)}, f32[4,18,1,128]{3,1,2,0:T(8,128)S(1)}, u32[]{:S(2)}, u32[]{:S(2)}) collective-permute-start(f32[4,18,1,128]{3,1,2,0:T(8,128)S(1)} %get-tuple-element.78), channel_id=1, source_target_pairs={{0,1},{1,2},{2,3},{3,4},{4,5},{5,6},{6,7},{7,8},{8,9},{9,10},{10,1... | collective-permute-start | bytes 110600 | tf_op jit(solution)/shard_map/ppermute | solution.py:17
  38.9 5.4 %collective-permute-start.7 = (f32[4,18,1,128]{3,1,2,0:T(8,128)S(1)}, f32[4,18,1,128]{3,1,2,0:T(8,128)S(1)}, u32[]{:S(2)}, u32[]{:S(2)}) collective-permute-start(f32[4,18,1,128]{3,1,2,0:T(8,128)S(1)} %get-tuple-element.79), channel_id=1, source_target_pairs={{1,0},{2,1},{3,2},{4,3},{5,4},{6,5},{7,6},{8,7},{9,8},{10,9},{11,1... | collective-permute-start | bytes 110600 | tf_op jit(solution)/shard_map/ppermute | solution.py:18
  47.7 9.8 %collective-permute-start.8 = (f32[4,12,128]{2,0,1:T(4,128)S(1)}, f32[4,12,128]{2,0,1:T(4,128)S(1)}, u32[]{:S(2)}, u32[]{:S(2)}) collective-permute-start(f32[4,12,128]{2,0,1:T(4,128)S(1)} %pad_maximum_fusion.10), channel_id=1, source_target_pairs={{0,256},{256,0},{1,257},{257,1},{2,258},{258,2},{3,259},{259,3},{4... | collective-permute-start | bytes 73736 | tf_op jit(solution)/shard_map/ppermute | solution.py:30
where the time goes:
time: 120 us
  blocking collectives  60 us (50%)
  starting transfers between devices  28.2 us (24%)
  waiting for transfers between devices  18.6 us (16%)
  local copies, waits for them, and re-layouts  7.47 us (6%)
  other arithmetic  4.91 us (4%)
    all_gather x1, blocking collectives, local(): lax.all_gather(arrived[:, 0:row_share], 'colat', axis=1, tiled=True)  42.9 us
    all_gather x1, blocking collectives, local(): col_full = lax.all_gather(arrived[:, row_share:], 'lon', axis=1, tiled=True)  17.1 us
    ppermute x4, starting transfers between devices, with_halo(): before = lax.ppermute(last, axis, up)  13.4 us
    ppermute x4, waiting for transfers between devices, with_halo(): before = lax.ppermute(last, axis, up)  9.57 us
    ppermute x4, starting transfers between devices, with_halo(): after = lax.ppermute(leading, axis, down)  8.15 us
    ppermute x1, starting transfers between devices, swapped(): return lax.ppermute(block, axis, route)  6.72 us
    ppermute x4, waiting for transfers between devices, with_halo(): after = lax.ppermute(leading, axis, down)  5.98 us
    ppermute x1, waiting for transfers between devices, swapped(): return lax.ppermute(block, axis, route)  3.06 us
  transfers between devices with their start and end apart: 9, of which 6 were waited for; matrix products, arithmetic and copies ran while one was open for 1% of the time, Pallas kernels for 0%

commit v1 on v0

--- a/solution.py
+++ b/solution.py
@@ -2,6 +2,10 @@
 import jax.numpy as jnp
 from jax import lax
 from jax.sharding import PartitionSpec as P
+from jax.experimental import pallas as pl
+from jax.experimental.pallas import tpu as pltpu
+
+MESH = pl.DeviceIdType.MESH
 
 TIME_STEP = 0.05
 BUOYANCY = 1.0
@@ -28,6 +32,113 @@
         if high != low and high < count:
             route += [(low, high), (high, low)]
     return lax.ppermute(block, axis, route)
+
+
+def rim_kernel(row_ref, col_ref, row_out, col_out, send_sem, row_sem, col_sem):
+    panel = lax.axis_index("panel")
+    colat = lax.axis_index("colat")
+    lon = lax.axis_index("lon")
+    colat_count = lax.axis_size("colat")
+    lon_count = lax.axis_size("lon")
+    row_types = row_out.shape[0] // 2
+    col_types = col_out.shape[0] // 2
+    other = 1 - panel
+
+    def route(share, per_type, count):
+        kind = share // per_type
+        edge = (kind % 2) * (count - 1)
+        slot = (kind // 2) * per_type + share % per_type
+        return edge, slot
+
+    row_edge, row_slot = route(colat, row_types, colat_count)
+    col_edge, col_slot = route(lon, col_types, lon_count)
+    row_dest = (other, row_edge, lon)
+    col_dest = (other, colat, col_edge)
+    at_row_edge = jnp.logical_or(colat == 0, colat == colat_count - 1)
+    at_col_edge = jnp.logical_or(lon == 0, lon == lon_count - 1)
+    parity_row = (colat // (colat_count - 1)).astype(jnp.int32)
+    parity_col = (lon // (lon_count - 1)).astype(jnp.int32)
+
+    def row_sender(slot):
+        kind = 2 * (slot // row_types) + parity_row
+        return (other, kind * row_types + slot % row_types, lon)
+
+    def col_sender(slot):
+        kind = 2 * (slot // col_types) + parity_col
+        return (other, colat, kind * col_types + slot % col_types)
+
+    barrier = pltpu.get_barrier_semaphore()
+    pl.semaphore_signal(barrier, 1, device_id=row_dest, device_id_type=MESH)
+    pl.semaphore_signal(barrier, 1, device_id=col_dest, device_id_type=MESH)
+
+    @pl.when(at_row_edge)
+    def _():
+        for slot in range(2 * row_types):
+            pl.semaphore_signal(barrier, 1, device_id=row_sender(slot), device_id_type=MESH)
+
+    @pl.when(at_col_edge)
+    def _():
+        for slot in range(2 * col_types):
+            pl.semaphore_signal(barrier, 1, device_id=col_sender(slot), device_id_type=MESH)
+
+    expected = (
+        2
+        + at_row_edge.astype(jnp.int32) * (2 * row_types)
+        + at_col_edge.astype(jnp.int32) * (2 * col_types)
+    )
+    pl.semaphore_wait(barrier, expected)
+
+    row_copy = pltpu.make_async_remote_copy(
+        row_ref, row_out.at[row_slot], send_sem.at[0], row_sem.at[row_slot],
+        device_id=row_dest, device_id_type=MESH,
+    )
+    col_copy = pltpu.make_async_remote_copy(
+        col_ref, col_out.at[col_slot], send_sem.at[1], col_sem.at[col_slot],
+        device_id=col_dest, device_id_type=MESH,
+    )
+    row_copy.start()
+    col_copy.start()
+    row_copy.wait_send()
+    col_copy.wait_send()
+
+    @pl.when(at_row_edge)
+    def _():
+        for slot in range(2 * row_types):
+            pltpu.make_async_remote_copy(
+                row_ref, row_out.at[slot], send_sem.at[0], row_sem.at[slot],
+                device_id=row_sender(slot), device_id_type=MESH,
+            ).wait_recv()
+
+    @pl.when(at_col_edge)
+    def _():
+        for slot in range(2 * col_types):
+            pltpu.make_async_remote_copy(
+                col_ref, col_out.at[slot], send_sem.at[1], col_sem.at[slot],
+                device_id=col_sender(slot), device_id_type=MESH,
+            ).wait_recv()
+
+
+def rim_exchange(rows, cols):
+    colat_count = lax.axis_size("colat")
+    lon_count = lax.axis_size("lon")
+    row_types = colat_count // 4
+    col_types = lon_count // 4
+    vmem = pl.BlockSpec(memory_space=pltpu.VMEM)
+    return pl.pallas_call(
+        rim_kernel,
+        out_shape=(
+            jax.ShapeDtypeStruct((2 * row_types,) + rows.shape, rows.dtype),
+            jax.ShapeDtypeStruct((2 * col_types,) + cols.shape, cols.dtype),
+        ),
+        in_specs=[vmem, vmem],
+        out_specs=(vmem, vmem),
+        scratch_shapes=[
+            pltpu.SemaphoreType.DMA((2,)),
+            pltpu.SemaphoreType.DMA((2 * row_types,)),
+            pltpu.SemaphoreType.DMA((2 * col_types,)),
+        ],
+        compiler_params=pltpu.CompilerParams(collective_id=0, has_side_effects=True),
+    )(rows, cols)
 
 
 def gradient(stencil):
@@ -92,23 +203,20 @@
     turned_lat = cosine * blended[2] - sine_part * blended[3]
     turned_lon = sine_part * blended[2] + cosine * blended[3]
     blended = jnp.stack([blended[0], blended[1], turned_lat, turned_lon])
-    arrived = swapped(blended, "panel", 0)
-    row_full = lax.all_gather(arrived[:, 0:row_share], "colat", axis=1, tiled=True)
-    col_full = lax.all_gather(arrived[:, row_share:], "lon", axis=1, tiled=True)
-    col_blocks = col_full.reshape(4, 4, height, radial_len)
-    west_strip = jnp.transpose(
-        jnp.stack([col_blocks[:, 0], col_blocks[:, 2]], axis=1), (0, 2, 1, 3)
-    )
-    east_strip = jnp.transpose(
-        jnp.stack([col_blocks[:, 3], col_blocks[:, 1]], axis=1), (0, 2, 1, 3)
-    )
+    row_buf, col_buf = rim_exchange(blended[:, 0:row_share], blended[:, row_share:])
+    col_share = blended.shape[1] - row_share
+    col_strip = col_buf.reshape(2, col_buf.shape[0] // 2, 4, col_share, radial_len)
+    col_strip = jnp.transpose(col_strip, (2, 0, 1, 3, 4)).reshape(4, 2, height, radial_len)
+    west_strip = jnp.transpose(col_strip, (0, 2, 1, 3))
+    east_strip = jnp.stack([col_strip[:, 1], col_strip[:, 0]], axis=2)
     fresh = fresh.at[:, :, 0:2].set(jnp.where(lon_pos == 0, west_strip, fresh[:, :, 0:2]))
     fresh = fresh.at[:, :, breadth - 2 :].set(
         jnp.where(lon_pos == lon_count - 1, east_strip, fresh[:, :, breadth - 2 :])
     )
-    row_blocks = row_full.reshape(4, 4, breadth, radial_len)
-    north_strip = jnp.stack([row_blocks[:, 0], row_blocks[:, 2]], axis=1)
-    south_strip = jnp.stack([row_blocks[:, 3], row_blocks[:, 1]], axis=1)
+    row_strip = row_buf.reshape(2, row_buf.shape[0] // 2, 4, row_share, radial_len)
+    row_strip = jnp.transpose(row_strip, (2, 0, 1, 3, 4)).reshape(4, 2, breadth, radial_len)
+    north_strip = row_strip
+    south_strip = jnp.stack([row_strip[:, 1], row_strip[:, 0]], axis=1)
     fresh = fresh.at[:, 0:2].set(jnp.where(colat_pos == 0, north_strip, fresh[:, 0:2]))
     fresh = fresh.at[:, height - 2 :].set(
         jnp.where(colat_pos == colat_count - 1, south_strip, fresh[:, height - 2 :])

time: 120 us -> 74.6 us (0.62)
  the two profiles are of different devices: /device:TPU:8 before, /device:TPU:6 now
where the time goes in v1:
time: 74.6 us; the launch traced here: 74.1 us
  starting transfers between devices  24.1 us (32%)
  Pallas kernels  21.6 us (29%)
  waiting for transfers between devices  13.5 us (18%)
  local copies, waits for them, and re-layouts  7.41 us (10%)
  other arithmetic  7.08 us (9%)
    pallas_call x1, Pallas kernels, rim_exchange(): pl.pallas_call(rim_kernel, out_shape=(jax.ShapeDtypeStruct((2 * row_types...  21.6 us
    ppermute x4, starting transfers between devices, with_halo(): before = lax.ppermute(last, axis, up)  16.9 us
    ppermute x4, waiting for transfers between devices, with_halo(): after = lax.ppermute(leading, axis, down)  11.5 us
    ppermute x4, starting transfers between devices, with_halo(): after = lax.ppermute(leading, axis, down)  7.24 us
    gather x4, local copies, waits for them, and re-layouts, corner(): return jnp.take(flattened, anchor + offset, axis=1)  2.31 us
    sub x1, other arithmetic, advance(): change = diffusion * laplace - transport  2.3 us
    ppermute x4, waiting for transfers between devices, with_halo(): before = lax.ppermute(last, axis, up)  2 us
  transfers between devices with their start and end apart: 8, of which 4 were waited for; matrix products, arithmetic and copies ran while one was open for 2% of the time, Pallas kernels for 0%

profile of v1, /device:TPU:6, one launch (start us, length us, event | category | flops | bytes accessed | tf_op | source)
XLA Modules:
  0.0 74.1 jit_solution(8939233012056183733)
XLA Ops:
  0.0 0.0 copy-start.4
  0.0 0.0 copy-start.6
  0.0 1.1 %fusion.15 = (f32[4,2,32,128]{3,2,1,0:T(8,128)S(1)}, f32[4,2,32,128]{3,2,1,0:T(8,128)S(1)}) fusion(f32[4,16,32,128]{3,2,1,0:T(8,128)} %bitcast.91), kind=kLoop, calls=%fused_computation.84 | loop fusion | bytes 524288 | tf_op jit(solution)/shard_map/slice | solution.py:19
  1.1 2.7 %collective-permute-start = (f32[4,2,32,128]{3,2,1,0:T(8,128)S(1)}, f32[4,2,32,128]{3,2,1,0:T(8,128)S(1)}, u32[]{:S(2)}, u32[]{:S(2)}) collective-permute-start(f32[4,2,32,128]{3,2,1,0:T(8,128)S(1)} %get-tuple-element.90), channel_id=1, source_target_pairs={{16,0},{32,16},{48,32},{64,48},{80,64},{96,80},{112,96},{128,112},... | collective-permute-start | bytes 393224 | tf_op jit(solution)/shard_map/ppermute | solution.py:22
  3.9 5.2 %collective-permute-start.1 = (f32[4,2,32,128]{3,2,1,0:T(8,128)S(1)}, f32[4,2,32,128]{3,2,1,0:T(8,128)S(1)}, u32[]{:S(2)}, u32[]{:S(2)}) collective-permute-start(f32[4,2,32,128]{3,2,1,0:T(8,128)S(1)} %get-tuple-element.89), channel_id=1, source_target_pairs={{0,16},{16,32},{32,48},{48,64},{64,80},{80,96},{96,112},{112,128},... | collective-permute-start | bytes 393224 | tf_op jit(solution)/shard_map/ppermute | solution.py:21
  9.1 1.2 %multiply_bitcast_fusion.2 = (f32[16,32,128]{2,1,0:T(8,128)S(1)}, f32[16,32,128]{2,1,0:T(8,128)S(1)}, f32[16,32,128]{2,1,0:T(8,128)S(1)}) fusion(f32[4,1,16,32,128]{4,3,2,1,0:T(8,128)} %param.19), kind=kLoop, calls=%fused_computation.26 | loop fusion | flops 196608 | bytes 1572864 | tf_op jit(solution)/shard_map/mul | solution.py:163
  10.3 0.0 copy-done.3
  10.4 0.0 collective-permute-done
  10.4 1.1 %collective-permute-done.1 = f32[4,2,32,128]{3,2,1,0:T(8,128)S(1)} collective-permute-done((f32[4,2,32,128]{3,2,1,0:T(8,128)S(1)}, f32[4,2,32,128]{3,2,1,0:T(8,128)S(1)}, u32[]{:S(2)}, u32[]{:S(2)}) %collective-permute-start.1) | collective-permute-done | bytes 131104 | tf_op jit(solution)/shard_map/ppermute | solution.py:21
  11.6 0.1 pad_maximum_fusion.6
  11.6 1.3 %collective-permute-start.2 = (f32[4,20,2,128]{3,2,1,0:T(2,128)S(1)}, f32[4,20,2,128]{3,2,1,0:T(2,128)S(1)}, u32[]{:S(2)}, u32[]{:S(2)}) collective-permute-start(f32[4,20,2,128]{3,2,1,0:T(2,128)S(1)} %get-tuple-element.80), channel_id=1, source_target_pairs={{1,0},{2,1},{3,2},{4,3},{5,4},{6,5},{7,6},{8,7},{9,8},{10,9},{11,1... | collective-permute-start | bytes 245768 | tf_op jit(solution)/shard_map/ppermute | solution.py:22
  12.9 3.0 %collective-permute-start.3 = (f32[4,20,2,128]{3,2,1,0:T(2,128)S(1)}, f32[4,20,2,128]{3,2,1,0:T(2,128)S(1)}, u32[]{:S(2)}, u32[]{:S(2)}) collective-permute-start(f32[4,20,2,128]{3,2,1,0:T(2,128)S(1)} %get-tuple-element.81), channel_id=1, source_target_pairs={{0,1},{1,2},{2,3},{3,4},{4,5},{5,6},{6,7},{7,8},{8,9},{9,10},{10,1... | collective-permute-start | bytes 245768 | tf_op jit(solution)/shard_map/ppermute | solution.py:21
  16.0 0.0 copy-start.1
  16.0 0.0 copy-start.2
  16.0 0.0 collective-permute-done.2
  16.0 0.9 %collective-permute-done.3 = f32[4,20,2,128]{3,2,1,0:T(2,128)S(1)} collective-permute-done((f32[4,20,2,128]{3,2,1,0:T(2,128)S(1)}, f32[4,20,2,128]{3,2,1,0:T(2,128)S(1)}, u32[]{:S(2)}, u32[]{:S(2)}) %collective-permute-start.3) | collective-permute-done | bytes 81952 | tf_op jit(solution)/shard_map/ppermute | solution.py:21
  16.9 0.3 pad_maximum_fusion
  17.2 2.3 %fusion.2 = f32[4,16,32,128]{3,2,1,0:T(8,128)S(1)} fusion(f32[1,16,32,128]{3,2,1,0:T(8,128)S(1)} %copy-done.1, f32[1,16,32,128]{3,2,1,0:T(8,128)S(1)} %copy-done.2, f32[4,20,34,128]{3,2,1,0:T(8,128)S(1)} %get-tuple-element.79, f32[4,20,34,128]{3,2,1,0:T(8,128)S(1)} %get-tuple-element.78, f32[4,2,32,128]{3,2,1,0:T(8,128)S(1)} %collective-permute-done, ...), kind=kLoop, calls=%fused_computation.20 | loop fusion | flops 11796480 | bytes 7864320 | tf_op jit(solution)/shard_map/sub | solution.py:168
  19.5 0.1 fusion.3
  19.6 0.2 multiply_add_fusion
  19.8 6.5 %collective-permute-start.4 = (f32[4,1,32,128]{3,2,1,0:T(8,128)S(1)}, f32[4,1,32,128]{3,2,1,0:T(8,128)S(1)}, u32[]{:S(2)}, u32[]{:S(2)}) collective-permute-start(f32[4,1,32,128]{3,2,1,0:T(8,128)S(1)} %get-tuple-element.84), channel_id=1, source_target_pairs={{0,16},{16,32},{32,48},{48,64},{64,80},{80,96},{96,112},{112,128},... | collective-permute-start | bytes 196616 | tf_op jit(solution)/shard_map/ppermute | solution.py:21
  26.3 1.9 %collective-permute-start.5 = (f32[4,1,32,128]{3,2,1,0:T(8,128)S(1)}, f32[4,1,32,128]{3,2,1,0:T(8,128)S(1)}, u32[]{:S(2)}, u32[]{:S(2)}) collective-permute-start(f32[4,1,32,128]{3,2,1,0:T(8,128)S(1)} %get-tuple-element.85), channel_id=1, source_target_pairs={{16,0},{32,16},{48,32},{64,48},{80,64},{96,80},{112,96},{128,112},... | collective-permute-start | bytes 196616 | tf_op jit(solution)/shard_map/ppermute | solution.py:22
  28.3 0.0 collective-permute-done.4
  28.3 6.6 %collective-permute-done.5 = f32[4,1,32,128]{3,2,1,0:T(8,128)S(1)} collective-permute-done((f32[4,1,32,128]{3,2,1,0:T(8,128)S(1)}, f32[4,1,32,128]{3,2,1,0:T(8,128)S(1)}, u32[]{:S(2)}, u32[]{:S(2)}) %collective-permute-start.5) | collective-permute-done | bytes 65568 | tf_op jit(solution)/shard_map/ppermute | solution.py:22
  34.8 0.1 pad_maximum_fusion.10
  34.9 2.2 %collective-permute-start.6 = (f32[4,18,1,128]{3,2,1,0:T(1,128)S(1)}, f32[4,18,1,128]{3,2,1,0:T(1,128)S(1)}, u32[]{:S(2)}, u32[]{:S(2)}) collective-permute-start(f32[4,18,1,128]{3,2,1,0:T(1,128)S(1)} %get-tuple-element.82), channel_id=1, source_target_pairs={{0,1},{1,2},{2,3},{3,4},{4,5},{5,6},{6,7},{7,8},{8,9},{9,10},{10,1... | collective-permute-start | bytes 110600 | tf_op jit(solution)/shard_map/ppermute | solution.py:21
  37.1 1.3 %collective-permute-start.7 = (f32[4,18,1,128]{3,2,1,0:T(1,128)S(1)}, f32[4,18,1,128]{3,2,1,0:T(1,128)S(1)}, u32[]{:S(2)}, u32[]{:S(2)}) collective-permute-start(f32[4,18,1,128]{3,2,1,0:T(1,128)S(1)} %get-tuple-element.83), channel_id=1, source_target_pairs={{1,0},{2,1},{3,2},{4,3},{5,4},{6,5},{7,6},{8,7},{9,8},{10,9},{11,1... | collective-permute-start | bytes 110600 | tf_op jit(solution)/shard_map/ppermute | solution.py:22
  38.4 0.0 collective-permute-done.6
  38.4 4.9 %collective-permute-done.7 = f32[4,18,1,128]{3,2,1,0:T(1,128)S(1)} collective-permute-done((f32[4,18,1,128]{3,2,1,0:T(1,128)S(1)}, f32[4,18,1,128]{3,2,1,0:T(1,128)S(1)}, u32[]{:S(2)}, u32[]{:S(2)}) %collective-permute-start.7) | collective-permute-done | bytes 36896 | tf_op jit(solution)/shard_map/ppermute | solution.py:22
  43.3 0.2 pad_maximum_fusion.1
  43.5 0.5 copy.13
  44.0 0.6 gather_fusion.2
  44.6 0.6 gather_fusion.3
  45.2 0.6 gather_fusion.1
  45.8 0.6 gather_fusion
  46.4 0.1 fusion.11
  46.5 0.1 multiply_subtract_fusion
  46.5 0.6 pad_maximum_fusion.12.col_ref
  47.2 0.6 slice.333.row_ref
  47.8 21.6 %shard_map.73 = (f32[8,4,8,128]{3,2,1,0:T(8,128)}, f32[8,4,4,128]{3,2,1,0:T(4,128)}) custom-call(f32[4,8,128]{2,1,0:T(8,128)} %slice.333.row_ref, f32[4,4,128]{2,1,0:T(4,128)} %pad_maximum_fusion.12.col_ref), custom_call_target="tpu_custom_call" | custom-call | tf_op jit(solution)/shard_map/pallas_call | solution.py:127
  69.4 0.9 %copy.18 = f32[4,2,4,4,128]{4,1,3,2,0:T(2,128)S(1)} copy(f32[4,2,4,4,128]{4,3,0,2,1:T(4,128)} %bitcast.107) | data formatting | bytes 131072 | tf_op jit(solution)/shard_map/transpose | solution.py:209
  70.3 0.1 fusion.17
  70.3 0.9 %copy.40 = f32[4,2,4,8,128]{4,3,2,1,0:T(8,128)S(1)} copy(f32[4,2,4,8,128]{4,3,0,2,1:T(8,128)} %bitcast.102) | data formatting | bytes 262144 | tf_op jit(solution)/shard_map/transpose | solution.py:217
  71.3 0.1 fusion.8
  71.4 0.1 fusion.7
  71.5 0.9 %fusion.6 = f32[4,16,32,128]{3,2,1,0:T(8,128)S(1)} fusion(f32[4,16,32,128]{3,2,1,0:T(8,128)S(1)} %fusion.7, pred[]{:T(512)S(6)} %eq.14, f32[4,2,4,8,128]{4,3,0,2,1:T(8,128)} %bitcast.103), kind=kLoop, calls=%fused_computation.31 | loop fusion | flops 32768 | bytes 393217 | tf_op jit(solution)/shard_map/scatter | solution.py:220
  72.4 1.0 %copy.45 = f32[4,1,16,32,128]{4,3,2,1,0:T(8,128)} copy(f32[4,1,16,32,128]{4,3,2,1,0:T(8,128)S(1)} %bitcast.95) | data formatting | bytes 2097152
  73.4 0.7 fusion.5
  (23 shorter events, 0.1 us)
Async XLA Ops:
  0.0 11.6 %copy-start = (f32[4,1,16,32,128]{4,3,2,1,0:T(8,128)S(1)}, f32[4,1,16,32,128]{4,3,2,1,0:T(8,128)}, u32[]{:S(2)}) copy-start(f32[4,1,16,32,128]{4,3,2,1,0:T(8,128)} %param.19) | copy-start | bytes 3145732
  0.0 10.3 %copy-start.3 = (f32[1,1,1,2,12]{4,3,2,1,0:T(2,128)S(1)}, f32[1,1,1,2,12]{4,3,2,1,0:T(2,128)}, u32[]{:S(2)}) copy-start(f32[1,1,1,2,12]{4,3,2,1,0:T(2,128)} %param.24) | copy-start | bytes 292
  0.0 10.3 %copy-start.5 = (s32[1,1,1,12]{3,2,1,0:T(1,128)S(1)}, s32[1,1,1,12]{3,2,1,0:T(1,128)}, u32[]{:S(2)}) copy-start(s32[1,1,1,12]{3,2,1,0:T(1,128)} %param.22) | copy-start | bytes 148
  0.0 10.3 %copy-start.4 = (s32[1,1,1,12]{3,2,1,0:T(1,128)S(1)}, s32[1,1,1,12]{3,2,1,0:T(1,128)}, u32[]{:S(2)}) copy-start(s32[1,1,1,12]{3,2,1,0:T(1,128)} %param.23) | copy-start | bytes 148
  0.0 10.3 %copy-start.6 = (f32[1,1,1,12]{3,2,1,0:T(1,128)S(1)}, f32[1,1,1,12]{3,2,1,0:T(1,128)}, u32[]{:S(2)}) copy-start(f32[1,1,1,12]{3,2,1,0:T(1,128)} %param.25) | copy-start | bytes 148
  1.1 9.3 %collective-permute-start = (f32[4,2,32,128]{3,2,1,0:T(8,128)S(1)}, f32[4,2,32,128]{3,2,1,0:T(8,128)S(1)}, u32[]{:S(2)}, u32[]{:S(2)}) collective-permute-start(f32[4,2,32,128]{3,2,1,0:T(8,128)S(1)} %get-tuple-element.90), channel_id=1, source_target_pairs={{16,0},{32,16},{48,32},{64,48},{80,64},{96,80},{112,96},{128,112},... | collective-permute-start | bytes 393224 | tf_op jit(solution)/shard_map/ppermute | solution.py:22
  3.9 7.7 %collective-permute-start.1 = (f32[4,2,32,128]{3,2,1,0:T(8,128)S(1)}, f32[4,2,32,128]{3,2,1,0:T(8,128)S(1)}, u32[]{:S(2)}, u32[]{:S(2)}) collective-permute-start(f32[4,2,32,128]{3,2,1,0:T(8,128)S(1)} %get-tuple-element.89), channel_id=1, source_target_pairs={{0,16},{16,32},{32,48},{48,64},{64,80},{80,96},{96,112},{112,128},... | collective-permute-start | bytes 393224 | tf_op jit(solution)/shard_map/ppermute | solution.py:21
  11.6 4.4 %collective-permute-start.2 = (f32[4,20,2,128]{3,2,1,0:T(2,128)S(1)}, f32[4,20,2,128]{3,2,1,0:T(2,128)S(1)}, u32[]{:S(2)}, u32[]{:S(2)}) collective-permute-start(f32[4,20,2,128]{3,2,1,0:T(2,128)S(1)} %get-tuple-element.80), channel_id=1, source_target_pairs={{1,0},{2,1},{3,2},{4,3},{5,4},{6,5},{7,6},{8,7},{9,8},{10,9},{11,1... | collective-permute-start | bytes 245768 | tf_op jit(solution)/shard_map/ppermute | solution.py:22
  12.9 3.9 %collective-permute-start.3 = (f32[4,20,2,128]{3,2,1,0:T(2,128)S(1)}, f32[4,20,2,128]{3,2,1,0:T(2,128)S(1)}, u32[]{:S(2)}, u32[]{:S(2)}) collective-permute-start(f32[4,20,2,128]{3,2,1,0:T(2,128)S(1)} %get-tuple-element.81), channel_id=1, source_target_pairs={{0,1},{1,2},{2,3},{3,4},{4,5},{5,6},{6,7},{7,8},{8,9},{9,10},{10,1... | collective-permute-start | bytes 245768 | tf_op jit(solution)/shard_map/ppermute | solution.py:21
  16.0 1.2 %copy-start.1 = (f32[1,16,32,128]{3,2,1,0:T(8,128)S(1)}, f32[1,16,32,128]{3,2,1,0:T(8,128)}, u32[]{:S(2)}) copy-start(f32[1,16,32,128]{3,2,1,0:T(8,128)} %param.21) | copy-start | bytes 786436
  16.0 1.2 %copy-start.2 = (f32[1,16,32,128]{3,2,1,0:T(8,128)S(1)}, f32[1,16,32,128]{3,2,1,0:T(8,128)}, u32[]{:S(2)}) copy-start(f32[1,16,32,128]{3,2,1,0:T(8,128)} %param.20) | copy-start | bytes 786436
  19.8 8.4 %collective-permute-start.4 = (f32[4,1,32,128]{3,2,1,0:T(8,128)S(1)}, f32[4,1,32,128]{3,2,1,0:T(8,128)S(1)}, u32[]{:S(2)}, u32[]{:S(2)}) collective-permute-start(f32[4,1,32,128]{3,2,1,0:T(8,128)S(1)} %get-tuple-element.84), channel_id=1, source_target_pairs={{0,16},{16,32},{32,48},{48,64},{64,80},{80,96},{96,112},{112,128},... | collective-permute-start | bytes 196616 | tf_op jit(solution)/shard_map/ppermute | solution.py:21
  26.3 8.5 %collective-permute-start.5 = (f32[4,1,32,128]{3,2,1,0:T(8,128)S(1)}, f32[4,1,32,128]{3,2,1,0:T(8,128)S(1)}, u32[]{:S(2)}, u32[]{:S(2)}) collective-permute-start(f32[4,1,32,128]{3,2,1,0:T(8,128)S(1)} %get-tuple-element.85), channel_id=1, source_target_pairs={{16,0},{32,16},{48,32},{64,48},{80,64},{96,80},{112,96},{128,112},... | collective-permute-start | bytes 196616 | tf_op jit(solution)/shard_map/ppermute | solution.py:22
  34.9 3.5 %collective-permute-start.6 = (f32[4,18,1,128]{3,2,1,0:T(1,128)S(1)}, f32[4,18,1,128]{3,2,1,0:T(1,128)S(1)}, u32[]{:S(2)}, u32[]{:S(2)}) collective-permute-start(f32[4,18,1,128]{3,2,1,0:T(1,128)S(1)} %get-tuple-element.82), channel_id=1, source_target_pairs={{0,1},{1,2},{2,3},{3,4},{4,5},{5,6},{6,7},{7,8},{8,9},{9,10},{10,1... | collective-permute-start | bytes 110600 | tf_op jit(solution)/shard_map/ppermute | solution.py:21
  37.1 6.2 %collective-permute-start.7 = (f32[4,18,1,128]{3,2,1,0:T(1,128)S(1)}, f32[4,18,1,128]{3,2,1,0:T(1,128)S(1)}, u32[]{:S(2)}, u32[]{:S(2)}) collective-permute-start(f32[4,18,1,128]{3,2,1,0:T(1,128)S(1)} %get-tuple-element.83), channel_id=1, source_target_pairs={{1,0},{2,1},{3,2},{4,3},{5,4},{6,5},{7,6},{8,7},{9,8},{10,9},{11,1... | collective-permute-start | bytes 110600 | tf_op jit(solution)/shard_map/ppermute | solution.py:22

commit v2 on v1

--- a/solution.py
+++ b/solution.py
@@ -141,6 +141,122 @@
     )(rows, cols)
 
 
+DIRECTIONS = ((-1, -1), (-1, 0), (-1, 1), (0, -1), (0, 1), (1, -1), (1, 0), (1, 1))
+
+
+def halo_kernel(*refs):
+    count = len(DIRECTIONS)
+    sends = refs[0 : 2 * count]
+    recvs = refs[2 * count : 4 * count]
+    send_sem, recv_sem = refs[4 * count :]
+    panel = lax.axis_index("panel")
+    colat = lax.axis_index("colat")
+    lon = lax.axis_index("lon")
+    colat_count = lax.axis_size("colat")
+    lon_count = lax.axis_size("lon")
+
+    def present(step):
+        row = colat + step[0]
+        col = lon + step[1]
+        inside = jnp.logical_and(row >= 0, row < colat_count)
+        return jnp.logical_and(inside, jnp.logical_and(col >= 0, col < lon_count))
+
+    def copies(index, part):
+        step = DIRECTIONS[index]
+        target = (panel, colat + step[0], lon + step[1])
+        back = count - 1 - index
+        return pltpu.make_async_remote_copy(
+            sends[2 * index + part], recvs[2 * back + part],
+            send_sem.at[index, part], recv_sem.at[back, part],
+            device_id=target, device_id_type=MESH,
+        )
+
+    def arriving(index, part):
+        step = DIRECTIONS[index]
+        source = (panel, colat + step[0], lon + step[1])
+        return pltpu.make_async_remote_copy(
+            sends[2 * index + part], recvs[2 * index + part],
+            send_sem.at[index, part], recv_sem.at[index, part],
+            device_id=source, device_id_type=MESH,
+        )
+
+    barrier = pltpu.get_barrier_semaphore()
+    expected = jnp.int32(0)
+    for index, step in enumerate(DIRECTIONS):
+        exists = present(step)
+        expected = expected + exists.astype(jnp.int32)
+
+        @pl.when(exists)
+        def _():
+            pl.semaphore_signal(
+                barrier, 1, device_id=(panel, colat + step[0], lon + step[1]),
+                device_id_type=MESH,
+            )
+
+    pl.semaphore_wait(barrier, expected)
+    for index, step in enumerate(DIRECTIONS):
+
+        @pl.when(present(step))
+        def _():
+            copies(index, 0).start()
+            copies(index, 1).start()
+
+    for index, step in enumerate(DIRECTIONS):
+
+        @pl.when(present(step))
+        def _():
+            copies(index, 0).wait_send()
+            copies(index, 1).wait_send()
+            arriving(index, 0).wait_recv()
+            arriving(index, 1).wait_recv()
+
+
+def halo_exchange(fields, coefs, width):
+    height, breadth = fields.shape[1], fields.shape[2]
+    sends = []
+    shapes = []
+    for step in DIRECTIONS:
+        for block, depth in ((fields, width), (coefs, 1)):
+            rows = slice(0, depth) if step[0] < 0 else slice(height - depth, height) if step[0] > 0 else slice(0, height)
+            cols = slice(0, depth) if step[1] < 0 else slice(breadth - depth, breadth) if step[1] > 0 else slice(0, breadth)
+            piece = block[:, rows, cols]
+            sends.append(piece)
+            shapes.append(jax.ShapeDtypeStruct(piece.shape, piece.dtype))
+    vmem = pl.BlockSpec(memory_space=pltpu.VMEM)
+    count = len(DIRECTIONS)
+    recvs = pl.pallas_call(
+        halo_kernel,
+        out_shape=tuple(shapes),
+        in_specs=[vmem] * len(sends),
+        out_specs=tuple([vmem] * len(sends)),
+        scratch_shapes=[
+            pltpu.SemaphoreType.DMA((count, 2)),
+            pltpu.SemaphoreType.DMA((count, 2)),
+        ],
+        compiler_params=pltpu.CompilerParams(collective_id=1, has_side_effects=True),
+    )(*sends)
+    colat = lax.axis_index("colat")
+    lon = lax.axis_index("lon")
+    colat_count = lax.axis_size("colat")
+    lon_count = lax.axis_size("lon")
+    padded = []
+    for part, block in enumerate((fields, coefs)):
+        pieces = {}
+        for index, step in enumerate(DIRECTIONS):
+            row = colat + step[0]
+            col = lon + step[1]
+            exists = (row >= 0) & (row < colat_count) & (col >= 0) & (col < lon_count)
+            got = recvs[2 * index + part]
+            pieces[step] = jnp.where(exists, got, jnp.zeros_like(got))
+        pieces[(0, 0)] = block
+        bands = [
+            jnp.concatenate([pieces[(r, -1)], pieces[(r, 0)], pieces[(r, 1)]], axis=2)
+            for r in (-1, 0, 1)
+        ]
+        padded.append(jnp.concatenate(bands, axis=1))
+    return padded
+
+
 def gradient(stencil):
     return (8.0 * (stencil[3] - stencil[1]) - (stencil[4] - stencil[0])) / 12.0
 
@@ -182,9 +298,17 @@
     colat_count = lax.axis_size("colat")
     lon_count = lax.axis_size("lon")
     row_share = 4 * breadth // colat_count
-    padded = with_halo(fields, (("colat", 1), ("lon", 2)), 2)
-    fresh = advance(padded, thermal, viscous)
-    extended = with_halo(fresh, (("colat", 1), ("lon", 2)), 1)
+    coefs = jnp.concatenate([thermal[None], viscous[None]], axis=0)
+    padded, coef_ext = halo_exchange(fields, coefs, 3)
+    fresh_ext = advance(padded, coef_ext[0], coef_ext[1])
+    row_ids = lax.broadcasted_iota(jnp.int32, (height + 2, breadth + 2), 0) + colat_pos * height - 1
+    col_ids = lax.broadcasted_iota(jnp.int32, (height + 2, breadth + 2), 1) + lon_pos * breadth - 1
+    in_panel = (
+        (row_ids >= 0) & (row_ids < colat_count * height)
+        & (col_ids >= 0) & (col_ids < lon_count * breadth)
+    )
+    extended = jnp.where(in_panel[None, :, :, None], fresh_ext, 0.0)
+    fresh = fresh_ext[:, 1 : 1 + height, 1 : 1 + breadth]
     width = breadth + 2
     flattened = extended.reshape(4, (height + 2) * width, radial_len)
     anchor = donor_row.reshape(-1) * width + donor_column.reshape(-1)

time: 74.6 us -> 61.3 us (0.82)
  starting transfers between devices: 24.1 us -> 0 us
  waiting for transfers between devices: 13.5 us -> 0 us
  Pallas kernels: 21.6 us -> 32.2 us
  local copies, waits for them, and re-layouts: 7.41 us -> 15.6 us
  other arithmetic: 7.08 us -> 12.4 us
    ppermute x8 -> x0, starting transfers between devices: 24.1 us -> none  [the longest x4 16.9 us: with_halo(): before = lax.ppermute(last, axis, up)]
    pallas_call x0 -> x1, Pallas kernels: none -> 13.6 us  [halo_exchange(): pl.pallas_call(halo_kernel, out_shape=tuple(shapes), in_specs=[vmem] * le...]
    ppermute x8 -> x0, waiting for transfers between devices: 13.5 us -> none  [the longest x4 11.5 us: with_halo(): after = lax.ppermute(leading, axis, down)]
    select_n x0 -> x10, other arithmetic: none -> 4.41 us  [the longest x8 2.9 us: halo_exchange(): pieces[step] = jnp.where(exists, got, jnp.zeros_like(got))]
    slice x2 -> x8, local copies, waits for them, and re-layouts: 1.09 us -> 5.3 us  [the longest x6 5.02 us: halo_exchange(): piece = block[:, rows, cols]]
    pallas_call x1, Pallas kernels: 21.6 us -> 18.6 us  [rim_exchange(): pl.pallas_call(rim_kernel, out_shape=(jax.ShapeDtypeStruct((2 * row_types...]
    sub x1, other arithmetic: 2.3 us -> 4.78 us  [advance(): change = diffusion * laplace - transport]
    unnamed x15 -> x45, local copies, waits for them, and re-layouts: 1 us -> 3.1 us
  transfers between devices with their start and end apart: 8 -> 0, of which waited for: 4 -> 0; matrix products, arithmetic and copies ran while one was open for 2% -> 0% of each run, Pallas kernels for 0% -> 0%
where the time goes in v2:
time: 61.3 us; the launch traced here: 60.7 us
  Pallas kernels  32.2 us (53%)
  local copies, waits for them, and re-layouts  15.6 us (25%)
  other arithmetic  12.4 us (20%)
    pallas_call x1, Pallas kernels, rim_exchange(): pl.pallas_call(rim_kernel, out_shape=(jax.ShapeDtypeStruct((2 * row_types...  18.6 us
    pallas_call x1, Pallas kernels, halo_exchange(): pl.pallas_call(halo_kernel, out_shape=tuple(shapes), in_specs=[vmem] * le...  13.6 us
    slice x6, local copies, waits for them, and re-layouts, halo_exchange(): piece = block[:, rows, cols]  5.02 us
    sub x1, other arithmetic, advance(): change = diffusion * laplace - transport  4.78 us
    unnamed x45, local copies, waits for them, and re-layouts  3.1 us
    select_n x8, other arithmetic, halo_exchange(): pieces[step] = jnp.where(exists, got, jnp.zeros_like(got))  2.9 us
    gather x4, local copies, waits for them, and re-layouts, corner(): return jnp.take(flattened, anchor + offset, axis=1)  2.31 us
    concatenate x3, other arithmetic, halo_exchange(): padded.append(jnp.concatenate(bands, axis=1))  1.7 us

profile of v2, /device:TPU:6, one launch (start us, length us, event | category | flops | bytes accessed | tf_op | source)
XLA Modules:
  0.0 60.7 jit_solution(5918211934814799679)
XLA Ops:
  0.0 1.1 %constant_dynamic-update-slice_fusion.1 = f32[2,16,32,128]{3,2,1,0:T(8,128)S(1)} fusion(f32[1,16,32,128]{3,2,1,0:T(8,128)} %param.20), kind=kLoop, calls=%fused_computation.75 | loop fusion | bytes 524288
  1.1 1.0 %constant_dynamic-update-slice_fusion = f32[2,16,32,128]{3,2,1,0:T(8,128)S(1)} fusion(f32[2,16,32,128]{3,2,1,0:T(8,128)S(1)} %constant_dynamic-update-slice_fusion.1, f32[1,16,32,128]{3,2,1,0:T(8,128)} %param.21), kind=kLoop, calls=%fused_computation.74 | loop fusion | bytes 524288 | tf_op jit(solution)/shard_map/concatenate | solution.py:301
  2.0 0.7 %fusion.21 = (f32[2,1,1,128]{3,2,1,0:T(1,128)}, f32[2,1,1,128]{3,2,1,0:T(1,128)}, f32[2,1,1,128]{3,2,1,0:T(1,128)}, f32[2,1,1,128]{3,2,1,0:T(1,128)}) fusion(f32[2,16,32,128]{3,2,1,0:T(8,128)S(1)} %constant_dynamic-update-slice_fusion), kind=kLoop, calls=%fused_computation.105 | loop fusion | bytes 8192 | tf_op jit(solution)/shard_map/slice | solution.py:222
  2.7 1.5 %fusion.18 = (f32[4,3,3,128]{3,2,1,0:T(4,128)}, f32[4,3,3,128]{3,2,1,0:T(4,128)}, f32[4,3,3,128]{3,2,1,0:T(4,128)}, f32[4,3,3,128]{3,2,1,0:T(4,128)}) fusion(f32[4,16,32,128]{3,2,1,0:T(8,128)} %bitcast.82), kind=kLoop, calls=%fused_computation.102 | loop fusion | bytes 147456 | tf_op jit(solution)/shard_map/slice | solution.py:222
  4.3 0.6 %fusion.22 = (f32[2,1,32,128]{3,2,1,0:T(8,128)}, f32[2,1,32,128]{3,2,1,0:T(8,128)}) fusion(f32[2,16,32,128]{3,2,1,0:T(8,128)S(1)} %constant_dynamic-update-slice_fusion), kind=kLoop, calls=%fused_computation.106 | loop fusion | bytes 131072 | tf_op jit(solution)/shard_map/slice | solution.py:222
  4.9 0.6 %fusion.23 = (f32[2,16,1,128]{3,2,1,0:T(1,128)}, f32[2,16,1,128]{3,2,1,0:T(1,128)}) fusion(f32[2,16,32,128]{3,2,1,0:T(8,128)S(1)} %constant_dynamic-update-slice_fusion), kind=kLoop, calls=%fused_computation.107 | loop fusion | bytes 65536 | tf_op jit(solution)/shard_map/slice | solution.py:222
  5.5 0.8 %fusion.19 = (f32[4,3,32,128]{3,2,1,0:T(8,128)}, f32[4,3,32,128]{3,2,1,0:T(8,128)}) fusion(f32[4,16,32,128]{3,2,1,0:T(8,128)S(1)} %bitcast.83), kind=kLoop, calls=%fused_computation.103 | loop fusion | bytes 786432 | tf_op jit(solution)/shard_map/slice | solution.py:222
  6.3 0.7 %fusion.20 = (f32[4,16,3,128]{3,2,1,0:T(4,128)}, f32[4,16,3,128]{3,2,1,0:T(4,128)}) fusion(f32[4,16,32,128]{3,2,1,0:T(8,128)S(1)} %bitcast.84), kind=kLoop, calls=%fused_computation.104 | loop fusion | bytes 393216 | tf_op jit(solution)/shard_map/slice | solution.py:222
  7.1 13.6 %shard_map.73 = (f32[4,3,3,128]{3,2,1,0:T(4,128)}, f32[2,1,1,128]{3,2,1,0:T(1,128)}, f32[4,3,32,128]{3,2,1,0:T(8,128)}, f32[2,1,32,128]{3,2,1,0:T(8,128)}, f32[4...) custom-call(f32[4,3,3,128]{3,2,1,0:T(4,128)} %get-tuple-element.120., ...), custom_call_target="tpu_custom_call" | custom-call | tf_op jit(solution)/shard_map/pallas_call | solution.py:227
  20.7 0.8 %broadcast_select_fusion.11 = (f32[4,3,3,128]{3,2,1,0:T(4,128)S(1)}, f32[4,3,3,128]{3,2,1,0:T(4,128)S(1)}) fusion(f32[4,3,3,128]{3,2,1,0:T(4,128)} %get-tuple-element.86, pred[]{:T(512)S(6)} %and.132, f32[4,3,3,128]{3,2,1,0:T(4,128)} %get-tuple-element.84, pred[]{:T(512)S(6)} %and.128), kind=kLoop, calls=%fused_computation.64 | loop fusion | flops 9216 | bytes 73730 | tf_op jit(solution)/shard_map/jit(_where)/select_n | solution.py:250
  21.5 1.0 %broadcast_select_fusion.3 = (f32[4,16,3,128]{3,2,1,0:T(4,128)S(1)}, f32[4,16,3,128]{3,2,1,0:T(4,128)S(1)}) fusion(f32[4,16,3,128]{3,2,1,0:T(4,128)} %get-tuple-element.88, pred[]{:T(512)S(6)} %and.137, f32[4,16,3,128]{3,2,1,0:T(4,128)} %get-tuple-element.87, pred[]{:T(512)S(6)} %and.135), kind=kLoop, calls=%fused_computation.42 | loop fusion | flops 49152 | bytes 393218 | tf_op jit(solution)/shard_map/jit(_where)/select_n | solution.py:250
  22.5 1.1 %broadcast_select_fusion.1 = (f32[4,3,32,128]{3,2,1,0:T(8,128)S(1)}, f32[4,3,32,128]{3,2,1,0:T(8,128)S(1)}) fusion(f32[4,3,32,128]{3,2,1,0:T(8,128)} %get-tuple-element.90, pred[]{:T(512)S(6)} %and.142, f32[4,3,32,128]{3,2,1,0:T(8,128)} %get-tuple-element.85, pred[]{:T(512)S(6)} %and.130), kind=kLoop, calls=%fused_computation.36 | loop fusion | flops 98304 | bytes 786434 | tf_op jit(solution)/shard_map/jit(_where)/select_n | solution.py:250
  23.7 0.3 maximum_maximum_fusion.1
  24.0 0.3 copy-done.3
  24.3 0.0 copy-done.4
  24.4 1.3 %maximum_maximum_fusion = f32[4,22,38,128]{3,2,1,0:T(8,128)S(1)} fusion(f32[4,3,3,128]{3,2,1,0:T(4,128)S(1)} %get-tuple-element.159, f32[4,3,32,128]{3,2,1,0:T(8,128)} %copy-done.3, f32[4,3,3,128]{3,2,1,0:T(4,128)S(1)} %get-tuple-element.160, f32[4,16,3,128]{3,2,1,0:T(4,128)S(1)} %get-tuple-element.153, f32[4,16,32,128]{3,2,1,0:T(8,128)S(1)} %bitcast.86, ...), kind=kLoop, calls=%fused_computation.8 | loop fusion | flops 3424256 | bytes 3424256 | tf_op jit(solution)/shard_map/concatenate | solution.py:256
  25.7 0.1 slice.378
  25.9 0.1 fusion.4
  26.1 0.5 copy-done.16
  26.5 0.1 copy-done.11
  26.6 0.0 copy-done.12
  26.7 0.0 copy-done.7
  26.8 4.8 %fusion = f32[4,18,34,128]{3,2,1,0:T(8,128)S(1)} fusion(f32[1,18,34,128]{3,2,1,0:T(8,128)S(1)} %fusion.5, f32[2,1,1,128]{3,2,1,0:T(1,128)S(1)} %get-tuple-element.163, f32[2,1,32,128]{3,2,1,0:T(8,128)S(1)} %get-tuple-element.157, f32[2,1,1,128]{3,2,1,0:T(1,128)S(1)} %get-tuple-element.164, f32[2,16,1,128]{3,2,1,0:T(1,128)S(1)} %get-tuple-element.155, ...), kind=kLoop, calls=%fused_computation.12 | loop fusion | flops 15040512 | bytes 14413824 | tf_op jit(solution)/shard_map/sub | solution.py:284
  31.6 0.1 fusion.1
  31.7 0.1 and_and_fusion
  31.8 1.5 %broadcast_select_fusion = (f32[4,18,34,128]{3,2,1,0:T(8,128)S(1)}, f32[4,18,34,128]{3,2,1,0:T(8,128)}) fusion(pred[18,34]{1,0:T(8,128)(4,1)S(1)} %and_and_fusion, f32[4,18,34,128]{3,2,1,0:T(8,128)S(1)} %fusion.1, f32[4,22,38,128]{3,2,1,0:T(8,128)S(1)} %maximum_maximum_fusion), kind=kLoop, calls=%fused_computation.14 | loop fusion | flops 940032 | bytes 5014116 | tf_op jit(solution)/shard_map/jit(_where)/select_n | solution.py:310
  33.3 0.5 copy.15
  33.8 0.1 copy-done.18
  34.0 0.6 gather_fusion.2
  34.6 0.6 gather_fusion.3
  35.2 0.6 gather_fusion
  35.7 0.6 gather_fusion.1
  36.4 0.1 fusion.13
  36.5 0.1 multiply_subtract_fusion
  36.6 0.6 pad_maximum_fusion.7.col_ref
  37.2 0.6 slice.396.row_ref
  37.8 18.6 %shard_map.74 = (f32[8,4,8,128]{3,2,1,0:T(8,128)}, f32[8,4,4,128]{3,2,1,0:T(4,128)}) custom-call(f32[4,8,128]{2,1,0:T(8,128)} %slice.396.row_ref, f32[4,4,128]{2,1,0:T(4,128)} %pad_maximum_fusion.7.col_ref), custom_call_target="tpu_custom_call" | custom-call | tf_op jit(solution)/shard_map/pallas_call | solution.py:127
  56.4 0.9 %copy.20 = f32[4,2,4,4,128]{4,1,3,2,0:T(2,128)S(1)} copy(f32[4,2,4,4,128]{4,3,0,2,1:T(4,128)} %bitcast.99) | data formatting | bytes 131072 | tf_op jit(solution)/shard_map/transpose | solution.py:333
  57.4 0.1 slice.392
  57.5 0.6 %copy.25 = f32[4,16,32,128]{3,1,0,2:T(8,128)S(1)} copy(f32[4,16,32,128]{3,2,1,0:T(8,128)S(1)} %slice.392) | data formatting | bytes 2097152
  58.2 0.1 fusion.25
  58.3 0.2 copy-done.6
  58.4 0.1 copy.23
  58.5 0.1 fusion.9
  58.7 0.1 copy.45
  58.8 0.1 fusion.24
  58.9 0.2 fusion.8
  59.1 1.6 %copy.24 = f32[4,1,16,32,128]{4,3,2,1,0:T(8,128)} copy(f32[4,1,16,32,128]{4,2,0,3,1:T(8,128)S(1)} %fusion.8) | data formatting | bytes 2097152 | tf_op jit(solution)/shard_map/scatter | solution.py:345
  (55 shorter events, 0.4 us)
Async XLA Ops:
  0.0 5.5 %copy-start = (f32[4,1,16,32,128]{4,3,2,1,0:T(8,128)S(1)}, f32[4,1,16,32,128]{4,3,2,1,0:T(8,128)}, u32[]{:S(2)}) copy-start(f32[4,1,16,32,128]{4,3,2,1,0:T(8,128)} %param.19) | copy-start | bytes 3145732
  2.0 24.7 %copy-start.2 = (f32[2,16,32,128]{3,2,1,0:T(8,128)}, f32[2,16,32,128]{3,2,1,0:T(8,128)S(1)}, u32[]{:S(2)}) copy-start(f32[2,16,32,128]{3,2,1,0:T(8,128)S(1)} %constant_dynamic-update-slice_fusion) | copy-start | bytes 1572868
  20.7 3.0 %copy-start.9 = (f32[4,3,3,128]{3,2,1,0:T(4,128)S(1)}, f32[4,3,3,128]{3,2,1,0:T(4,128)}, u32[]{:S(2)}) copy-start(f32[4,3,3,128]{3,2,1,0:T(4,128)} %get-tuple-element.89) | copy-start | bytes 55300
  20.7 3.0 %copy-start.10 = (f32[4,3,3,128]{3,2,1,0:T(4,128)S(1)}, f32[4,3,3,128]{3,2,1,0:T(4,128)}, u32[]{:S(2)}) copy-start(f32[4,3,3,128]{3,2,1,0:T(4,128)} %get-tuple-element.91) | copy-start | bytes 55300
  22.5 1.9 %copy-start.5 = (f32[4,16,3,128]{3,2,1,0:T(4,128)}, f32[4,16,3,128]{3,2,1,0:T(4,128)S(1)}, u32[]{:S(2)}) copy-start(f32[4,16,3,128]{3,2,1,0:T(4,128)S(1)} %get-tuple-element.154) | copy-start | bytes 294916
  23.6 0.7 %copy-start.3 = (f32[4,3,32,128]{3,2,1,0:T(8,128)}, f32[4,3,32,128]{3,2,1,0:T(8,128)S(1)}, u32[]{:S(2)}) copy-start(f32[4,3,32,128]{3,2,1,0:T(8,128)S(1)} %get-tuple-element.151) | copy-start | bytes 589828
  23.6 0.7 %copy-start.4 = (f32[4,3,32,128]{3,2,1,0:T(8,128)}, f32[4,3,32,128]{3,2,1,0:T(8,128)S(1)}, u32[]{:S(2)}) copy-start(f32[4,3,32,128]{3,2,1,0:T(8,128)S(1)} %get-tuple-element.152) | copy-start | bytes 589828
  25.9 0.7 %copy-start.16 = (f32[2,1,1,128]{3,2,1,0:T(1,128)S(1)}, f32[2,1,1,128]{3,2,1,0:T(1,128)}, u32[]{:S(2)}) copy-start(f32[2,1,1,128]{3,2,1,0:T(1,128)} %get-tuple-element.92) | copy-start | bytes 3076
  25.9 0.7 %copy-start.17 = (f32[2,1,1,128]{3,2,1,0:T(1,128)S(1)}, f32[2,1,1,128]{3,2,1,0:T(1,128)}, u32[]{:S(2)}) copy-start(f32[2,1,1,128]{3,2,1,0:T(1,128)} %get-tuple-element.94) | copy-start | bytes 3076
  25.9 0.7 %copy-start.11 = (f32[2,16,1,128]{3,2,1,0:T(1,128)S(1)}, f32[2,16,1,128]{3,2,1,0:T(1,128)}, u32[]{:S(2)}) copy-start(f32[2,16,1,128]{3,2,1,0:T(1,128)} %get-tuple-element.95) | copy-start | bytes 49156
  25.9 0.7 %copy-start.12 = (f32[2,16,1,128]{3,2,1,0:T(1,128)S(1)}, f32[2,16,1,128]{3,2,1,0:T(1,128)}, u32[]{:S(2)}) copy-start(f32[2,16,1,128]{3,2,1,0:T(1,128)} %get-tuple-element.96) | copy-start | bytes 49156
  25.9 0.8 %copy-start.7 = (f32[2,1,32,128]{3,2,1,0:T(8,128)S(1)}, f32[2,1,32,128]{3,2,1,0:T(8,128)}, u32[]{:S(2)}) copy-start(f32[2,1,32,128]{3,2,1,0:T(8,128)} %get-tuple-element.93) | copy-start | bytes 98308
  25.9 0.8 %copy-start.8 = (f32[2,1,32,128]{3,2,1,0:T(8,128)S(1)}, f32[2,1,32,128]{3,2,1,0:T(8,128)}, u32[]{:S(2)}) copy-start(f32[2,1,32,128]{3,2,1,0:T(8,128)} %get-tuple-element.98) | copy-start | bytes 98308
  25.9 0.8 %copy-start.14 = (f32[2,1,1,128]{3,2,1,0:T(1,128)S(1)}, f32[2,1,1,128]{3,2,1,0:T(1,128)}, u32[]{:S(2)}) copy-start(f32[2,1,1,128]{3,2,1,0:T(1,128)} %get-tuple-element.97) | copy-start | bytes 3076
  25.9 0.8 %copy-start.15 = (f32[2,1,1,128]{3,2,1,0:T(1,128)S(1)}, f32[2,1,1,128]{3,2,1,0:T(1,128)}, u32[]{:S(2)}) copy-start(f32[2,1,1,128]{3,2,1,0:T(1,128)} %get-tuple-element.99) | copy-start | bytes 3076
  33.3 0.7 %copy-start.18 = (s32[1,1,1,12]{3,2,1,0:T(1,128)S(1)}, s32[1,1,1,12]{3,2,1,0:T(1,128)}, u32[]{:S(2)}) copy-start(s32[1,1,1,12]{3,2,1,0:T(1,128)} %param.23) | copy-start | bytes 148
  33.3 0.7 %copy-start.19 = (s32[1,1,1,12]{3,2,1,0:T(1,128)S(1)}, s32[1,1,1,12]{3,2,1,0:T(1,128)}, u32[]{:S(2)}) copy-start(s32[1,1,1,12]{3,2,1,0:T(1,128)} %param.22) | copy-start | bytes 148
  33.3 3.0 %copy-start.13 = (f32[1,1,1,2,12]{4,3,2,1,0:T(2,128)S(1)}, f32[1,1,1,2,12]{4,3,2,1,0:T(2,128)}, u32[]{:S(2)}) copy-start(f32[1,1,1,2,12]{4,3,2,1,0:T(2,128)} %param.24) | copy-start | bytes 292
  33.3 3.2 %copy-start.20 = (f32[1,1,1,12]{3,2,1,0:T(1,128)S(1)}, f32[1,1,1,12]{3,2,1,0:T(1,128)}, u32[]{:S(2)}) copy-start(f32[1,1,1,12]{3,2,1,0:T(1,128)} %param.25) | copy-start | bytes 148
  33.3 24.0 %copy-start.1 = (f32[4,18,34,128]{3,2,1,0:T(8,128)S(1)}, f32[4,18,34,128]{3,2,1,0:T(8,128)}, u32[]{:S(2)}) copy-start(f32[4,18,34,128]{3,2,1,0:T(8,128)} %get-tuple-element.111) | copy-start | bytes 3760132
  57.5 0.9 %copy-start.6 = (f32[8,4,8,128]{3,2,1,0:T(8,128)S(1)}, f32[8,4,8,128]{3,2,1,0:T(8,128)}, u32[]{:S(2)}) copy-start(f32[8,4,8,128]{3,2,1,0:T(8,128)} %get-tuple-element.101) | copy-start | bytes 393220

commit v3 on v1

--- a/solution.py
+++ b/solution.py
@@ -1,3 +1,5 @@
+import functools
+
 import jax
 import jax.numpy as jnp
 from jax import lax
@@ -141,6 +143,130 @@
     )(rows, cols)
 
 
+DIRECTIONS = ((-1, -1), (-1, 0), (-1, 1), (0, -1), (0, 1), (1, -1), (1, 0), (1, 1))
+
+
+def window(step, width, length, offset):
+    if step < 0:
+        return offset, width
+    if step > 0:
+        return offset + length - width, width
+    return offset, length
+
+
+def landing(step, width, length, offset):
+    if step < 0:
+        return offset - width, width
+    if step > 0:
+        return offset + length, width
+    return offset, length
+
+
+def halo_kernel(width, margins, fields_in, coefs_in, fields_out, coefs_out, send_sem, recv_sem):
+    del fields_in, coefs_in
+    count = len(DIRECTIONS)
+    panel = lax.axis_index("panel")
+    colat = lax.axis_index("colat")
+    lon = lax.axis_index("lon")
+    colat_count = lax.axis_size("colat")
+    lon_count = lax.axis_size("lon")
+    height = fields_out.shape[1] - 2 * margins[0][0]
+    breadth = fields_out.shape[2] - 2 * margins[0][1]
+    layers = ((fields_out, width, margins[0]), (coefs_out, 1, margins[1]))
+
+    def present(step):
+        row = colat + step[0]
+        col = lon + step[1]
+        inside = jnp.logical_and(row >= 0, row < colat_count)
+        return jnp.logical_and(inside, jnp.logical_and(col >= 0, col < lon_count))
+
+    def region(ref, rows, cols):
+        return ref.at[:, pl.ds(rows[0], rows[1]), pl.ds(cols[0], cols[1]), :]
+
+    def outgoing(index, part):
+        step = DIRECTIONS[index]
+        ref, depth, (row_pad, col_pad) = layers[part]
+        source = region(
+            ref, window(step[0], depth, height, row_pad), window(step[1], depth, breadth, col_pad)
+        )
+        target = region(
+            ref, landing(-step[0], depth, height, row_pad), landing(-step[1], depth, breadth, col_pad)
+        )
+        return pltpu.make_async_remote_copy(
+            source, target, send_sem.at[index, part], recv_sem.at[count - 1 - index, part],
+            device_id=(panel, colat + step[0], lon + step[1]), device_id_type=MESH,
+        )
+
+    def incoming(index, part):
+        step = DIRECTIONS[index]
+        ref, depth, (row_pad, col_pad) = layers[part]
+        target = region(
+            ref, landing(step[0], depth, height, row_pad), landing(step[1], depth, breadth, col_pad)
+        )
+        return pltpu.make_async_remote_copy(
+            target, target, send_sem.at[index, part], recv_sem.at[index, part],
+            device_id=(panel, colat + step[0], lon + step[1]), device_id_type=MESH,
+        )
+
+    barrier = pltpu.get_barrier_semaphore()
+    expected = jnp.int32(0)
+    for index, step in enumerate(DIRECTIONS):
+        exists = present(step)
+        expected = expected + exists.astype(jnp.int32)
+
+        @pl.when(exists)
+        def _():
+            pl.semaphore_signal(
+                barrier, 1, device_id=(panel, colat + step[0], lon + step[1]),
+                device_id_type=MESH,
+            )
+
+    pl.semaphore_wait(barrier, expected)
+    for index, step in enumerate(DIRECTIONS):
+
+        @pl.when(present(step))
+        def _():
+            outgoing(index, 0).start()
+            outgoing(index, 1).start()
+
+    for index, step in enumerate(DIRECTIONS):
+
+        @pl.when(present(step))
+        def _():
+            outgoing(index, 0).wait_send()
+            outgoing(index, 1).wait_send()
+            incoming(index, 0).wait_recv()
+            incoming(index, 1).wait_recv()
+
+
+def halo_exchange(fields, coefs, width):
+    lane_pad = 8
+    margins = ((width, lane_pad), (1, lane_pad))
+    fields_pad = jnp.pad(fields, ((0, 0), (width, width), (lane_pad, lane_pad), (0, 0)))
+    coefs_pad = jnp.pad(coefs, ((0, 0), (1, 1), (lane_pad, lane_pad), (0, 0)))
+    anywhere = pl.BlockSpec(memory_space=pl.ANY)
+    count = len(DIRECTIONS)
+    fields_pad, coefs_pad = pl.pallas_call(
+        functools.partial(halo_kernel, width, margins),
+        out_shape=(
+            jax.ShapeDtypeStruct(fields_pad.shape, fields_pad.dtype),
+            jax.ShapeDtypeStruct(coefs_pad.shape, coefs_pad.dtype),
+        ),
+        in_specs=[anywhere, anywhere],
+        out_specs=(anywhere, anywhere),
+        scratch_shapes=[
+            pltpu.SemaphoreType.DMA((count, 2)),
+            pltpu.SemaphoreType.DMA((count, 2)),
+        ],
+        input_output_aliases={0: 0, 1: 1},
+        compiler_params=pltpu.CompilerParams(collective_id=1, has_side_effects=True),
+    )(fields_pad, coefs_pad)
+    return (
+        fields_pad[:, :, lane_pad - width : lane_pad + fields.shape[2] + width],
+        coefs_pad[:, :, lane_pad - 1 : lane_pad + fields.shape[2] + 1],
+    )
+
+
 def gradient(stencil):
     return (8.0 * (stencil[3] - stencil[1]) - (stencil[4] - stencil[0])) / 12.0
 
@@ -182,9 +308,17 @@
     colat_count = lax.axis_size("colat")
     lon_count = lax.axis_size("lon")
     row_share = 4 * breadth // colat_count
-    padded = with_halo(fields, (("colat", 1), ("lon", 2)), 2)
-    fresh = advance(padded, thermal, viscous)
-    extended = with_halo(fresh, (("colat", 1), ("lon", 2)), 1)
+    coefs = jnp.concatenate([thermal[None], viscous[None]], axis=0)
+    padded, coef_ext = halo_exchange(fields, coefs, 3)
+    fresh_ext = advance(padded, coef_ext[0], coef_ext[1])
+    row_ids = lax.broadcasted_iota(jnp.int32, (height + 2, breadth + 2), 0) + colat_pos * height - 1
+    col_ids = lax.broadcasted_iota(jnp.int32, (height + 2, breadth + 2), 1) + lon_pos * breadth - 1
+    in_panel = (
+        (row_ids >= 0) & (row_ids < colat_count * height)
+        & (col_ids >= 0) & (col_ids < lon_count * breadth)
+    )
+    extended = jnp.where(in_panel[None, :, :, None], fresh_ext, 0.0)
+    fresh = fresh_ext[:, 1 : 1 + height, 1 : 1 + breadth]
     width = breadth + 2
     flattened = extended.reshape(4, (height + 2) * width, radial_len)
     anchor = donor_row.reshape(-1) * width + donor_column.reshape(-1)
@@ -209,18 +343,20 @@
     col_strip = jnp.transpose(col_strip, (2, 0, 1, 3, 4)).reshape(4, 2, height, radial_len)
     west_strip = jnp.transpose(col_strip, (0, 2, 1, 3))
     east_strip = jnp.stack([col_strip[:, 1], col_strip[:, 0]], axis=2)
-    fresh = fresh.at[:, :, 0:2].set(jnp.where(lon_pos == 0, west_strip, fresh[:, :, 0:2]))
-    fresh = fresh.at[:, :, breadth - 2 :].set(
-        jnp.where(lon_pos == lon_count - 1, east_strip, fresh[:, :, breadth - 2 :])
-    )
     row_strip = row_buf.reshape(2, row_buf.shape[0] // 2, 4, row_share, radial_len)
     row_strip = jnp.transpose(row_strip, (2, 0, 1, 3, 4)).reshape(4, 2, breadth, radial_len)
     north_strip = row_strip
     south_strip = jnp.stack([row_strip[:, 1], row_strip[:, 0]], axis=1)
-    fresh = fresh.at[:, 0:2].set(jnp.where(colat_pos == 0, north_strip, fresh[:, 0:2]))
-    fresh = fresh.at[:, height - 2 :].set(
-        jnp.where(colat_pos == colat_count - 1, south_strip, fresh[:, height - 2 :])
-    )
+    gap_cols = jnp.zeros((4, height, breadth - 4, radial_len), fresh.dtype)
+    col_rim = jnp.concatenate([west_strip, gap_cols, east_strip], axis=2)
+    gap_rows = jnp.zeros((4, height - 4, breadth, radial_len), fresh.dtype)
+    row_rim = jnp.concatenate([north_strip, gap_rows, south_strip], axis=1)
+    row_ids = lax.broadcasted_iota(jnp.int32, (height, breadth), 0)
+    col_ids = lax.broadcasted_iota(jnp.int32, (height, breadth), 1)
+    use_col = ((lon_pos == 0) & (col_ids < 2)) | ((lon_pos == lon_count - 1) & (col_ids >= breadth - 2))
+    use_row = ((colat_pos == 0) & (row_ids < 2)) | ((colat_pos == colat_count - 1) & (row_ids >= height - 2))
+    fresh = jnp.where(use_col[None, :, :, None], col_rim, fresh)
+    fresh = jnp.where(use_row[None, :, :, None], row_rim, fresh)
     return fresh[:, None]
 
 

time: 74.6 us -> 54.4 us (0.73)
  starting transfers between devices: 24.1 us -> 0 us
  waiting for transfers between devices: 13.5 us -> 0 us
  Pallas kernels: 21.6 us -> 30.3 us
  other arithmetic: 7.08 us -> 13.3 us
  local copies, waits for them, and re-layouts: 7.41 us -> 10.1 us
    ppermute x8 -> x0, starting transfers between devices: 24.1 us -> none  [the longest x4 16.9 us: with_halo(): before = lax.ppermute(last, axis, up)]
    ppermute x8 -> x0, waiting for transfers between devices: 13.5 us -> none  [the longest x4 11.5 us: with_halo(): after = lax.ppermute(leading, axis, down)]
    pallas_call x0 -> x1, Pallas kernels: none -> 11.8 us  [halo_exchange(): pl.pallas_call(functools.partial(halo_kernel, width, margins), out_shape=...]
    pallas_call x1, Pallas kernels: 21.6 us -> 18.5 us  [rim_exchange(): pl.pallas_call(rim_kernel, out_shape=(jax.ShapeDtypeStruct((2 * row_types...]
    select_n x0 -> x1, other arithmetic: none -> 2.83 us  [local(): extended = jnp.where(in_panel[None, :, :, None], fresh_ext, 0.0)]
    pad x0 -> x1, local copies, waits for them, and re-layouts: none -> 2.81 us  [halo_exchange(): jnp.pad(fields, ((0, 0), (width, width), (lane_pad, lane_pad), (0, 0)))]
    scatter x4 -> x0, other arithmetic: 1.81 us -> none  [the longest x1 0.94 us: local(): fresh.at[:, 0:2].set(jnp.where(colat_pos == 0, north_strip, fresh[:, 0:2]))]
    scatter-add x1, other arithmetic: 0.07 us -> 1.76 us  [advance(): change = change.at[1].add(BUOYANCY * center[0])]
  transfers between devices with their start and end apart: 8 -> 0, of which waited for: 4 -> 0; matrix products, arithmetic and copies ran while one was open for 2% -> 0% of each run, Pallas kernels for 0% -> 0%
where the time goes in v3:
time: 54.4 us; the launch traced here: 54 us
  Pallas kernels  30.3 us (56%)
  other arithmetic  13.3 us (24%)
  local copies, waits for them, and re-layouts  10.1 us (19%)
    pallas_call x1, Pallas kernels, rim_exchange(): pl.pallas_call(rim_kernel, out_shape=(jax.ShapeDtypeStruct((2 * row_types...  18.5 us
    pallas_call x1, Pallas kernels, halo_exchange(): pl.pallas_call(functools.partial(halo_kernel, width, margins), out_shape=...  11.8 us
    sub x1, other arithmetic, advance(): change = diffusion * laplace - transport  3.9 us
    select_n x1, other arithmetic, local(): extended = jnp.where(in_panel[None, :, :, None], fresh_ext, 0.0)  2.83 us
    pad x1, local copies, waits for them, and re-layouts, halo_exchange(): jnp.pad(fields, ((0, 0), (width, width), (lane_pad, lane_pad), (0, 0)))  2.81 us
    gather x4, local copies, waits for them, and re-layouts, corner(): return jnp.take(flattened, anchor + offset, axis=1)  2.31 us
    scatter-add x1, other arithmetic, advance(): change = change.at[1].add(BUOYANCY * center[0])  1.76 us
    unnamed x18, local copies, waits for them, and re-layouts  1.64 us

profile of v3, /device:TPU:6, one launch (start us, length us, event | category | flops | bytes accessed | tf_op | source)
XLA Modules:
  0.0 54.0 jit_solution(14081935953971580469)
XLA Ops:
  0.0 0.0 copy-start.3
  0.0 0.0 copy-start.4
  0.0 2.8 %pad.14.fields_in = f32[4,22,48,128]{3,2,1,0:T(8,128)} pad(f32[4,16,32,128]{3,2,1,0:T(8,128)} %bitcast.89, f32[]{:T(128)} %constant.86.clone.1), padding=0_0x3_3x8_8x0_0 | pad | bytes 3211268 | tf_op jit(solution)/shard_map/jit(_pad)/pad | solution.py:245
  2.8 0.0 copy-done.3
  2.8 0.0 copy-done.4
  2.8 1.0 %select_maximum_fusion.coefs_in = f32[2,18,48,128]{3,2,1,0:T(8,128)} fusion(f32[1,16,32,128]{3,2,1,0:T(8,128)S(1)} %copy-done.3, f32[1,16,32,128]{3,2,1,0:T(8,128)S(1)} %copy-done.4), kind=kLoop, calls=%fused_computation.18 | loop fusion | flops 2654208 | bytes 1409024 | tf_op jit(solution)/shard_map/concatenate | solution.py:311
  3.8 11.8 %shard_map.73 = (f32[4,22,48,128]{3,2,1,0:T(8,128)}, f32[2,18,48,128]{3,2,1,0:T(8,128)}) custom-call(f32[4,22,48,128]{3,2,1,0:T(8,128)} %pad.14.fields_in, f32[2,18,48,128]{3,2,1,0:T(8,128)} %select_maximum_fusion.coefs_in), custom_call_target="tpu_custom_call", output_to_operand_aliasing={{0}: (0, {}), {1}: (1, {})} | custom-call | tf_op jit(solution)/shard_map/pallas_call | solution.py:249
  15.6 0.0 copy-start
  15.6 1.6 %multiply_bitcast_fusion.2 = (f32[18,34,128]{2,1,0:T(8,128)S(1)}, f32[18,34,128]{2,1,0:T(8,128)S(1)}, f32[18,34,128]{2,1,0:T(8,128)S(1)}) fusion(f32[4,22,48,128]{3,2,1,0:T(8,128)} %get-tuple-element.22), kind=kLoop, calls=%fused_computation.27 | loop fusion | flops 235008 | bytes 1880064 | tf_op jit(solution)/shard_map/mul | solution.py:289
  17.2 0.4 copy-done
  17.6 0.0 copy-start.1
  17.6 0.1 slice.147
  17.8 1.0 %copy-done.1 = f32[2,18,48,128]{3,2,1,0:T(8,128)S(1)} copy-done((f32[2,18,48,128]{3,2,1,0:T(8,128)S(1)}, f32[2,18,48,128]{3,2,1,0:T(8,128)}, u32[]{:S(2)}) %copy-start.1) | copy-done | bytes 884760
  18.8 0.1 slice.148
  18.9 3.9 %fusion = f32[4,18,34,128]{3,2,1,0:T(8,128)} fusion(f32[1,18,34,128]{3,2,1,0:T(8,128)S(1)} %slice.149, f32[2,18,34,128]{3,2,1,0:T(8,128)S(1)} %slice.148, f32[4,22,48,128]{3,2,1,0:T(8,128)S(1)} %copy-done, f32[4,18,34,128]{3,2,1,0:T(8,128)S(1)} %slice.147, f32[18,34,128]{2,1,0:T(8,128)S(1)} %get-tuple-element.38, f32[18,34,128]{2,1,0:T(8,128)S(1)} %get-tuple-element.37, ...), kind=kLoop, calls=%fused_computation.9 | loop fusion | flops 12533760 | bytes 14413824 | tf_op jit(solution)/shard_map/sub | solution.py:294
  22.8 1.8 %fusion.6 = f32[4,18,34,128]{3,2,1,0:T(8,128)} fusion(f32[4,18,34,128]{3,2,1,0:T(8,128)} %fusion, f32[4,22,48,128]{3,2,1,0:T(8,128)S(1)} %copy-done), kind=kLoop, calls=%fused_computation.24 | loop fusion | flops 78336 | bytes 1050624 | tf_op jit(solution)/shard_map/scatter-add | solution.py:295
  24.6 0.1 and_and_fusion
  24.6 2.8 %broadcast_select_fusion = (f32[4,18,34,128]{3,2,1,0:T(8,128)S(1)}, f32[4,18,34,128]{3,2,1,0:T(8,128)}) fusion(pred[18,34]{1,0:T(8,128)(4,1)S(1)} %and_and_fusion, f32[4,18,34,128]{3,2,1,0:T(8,128)} %fusion.6, f32[4,22,48,128]{3,2,1,0:T(8,128)S(1)} %copy-done), kind=kLoop, calls=%fused_computation.22 | loop fusion | flops 940032 | bytes 5014116 | tf_op jit(solution)/shard_map/jit(_where)/select_n | solution.py:320
  27.5 0.0 copy-start.6
  27.5 0.0 copy-start.7
  27.5 0.0 copy-start.5
  27.5 0.0 copy-start.8
  27.5 0.5 copy.15
  28.0 0.0 copy-start.2
  28.0 0.1 copy-done.6
  28.1 0.0 copy-done.7
  28.2 0.6 %gather_fusion.2 = f32[12,4,128]{2,1,0:T(4,128)S(1)} fusion(f32[4,612,128]{2,0,1:T(4,128)S(1)} %bitcast.83, s32[1024]{0:T(1024)S(1)} %get-tuple-element.58), kind=kCustom, calls=%fused_computation.2.clone | custom fusion | bytes 49200 | tf_op jit(solution)/shard_map/jit(_take)/gather | solution.py:327
  28.7 0.6 %gather_fusion.3 = f32[12,4,128]{2,1,0:T(4,128)S(1)} fusion(f32[4,612,128]{2,0,1:T(4,128)S(1)} %bitcast.84, s32[1024]{0:T(1024)S(1)} %get-tuple-element.57), kind=kCustom, calls=%fused_computation.3.clone | custom fusion | bytes 49200 | tf_op jit(solution)/shard_map/jit(_take)/gather | solution.py:327
  29.3 0.6 %gather_fusion.1 = f32[12,4,128]{2,1,0:T(4,128)S(1)} fusion(f32[4,612,128]{2,0,1:T(4,128)S(1)} %bitcast.85, s32[1024]{0:T(1024)S(1)} %pad_clamp_fusion.2), kind=kCustom, calls=%fused_computation.1.clone | custom fusion | bytes 49200 | tf_op jit(solution)/shard_map/jit(_take)/gather | solution.py:327
  29.9 0.6 %gather_fusion = f32[12,4,128]{2,1,0:T(4,128)S(1)} fusion(f32[4,612,128]{2,0,1:T(4,128)S(1)} %bitcast.86, s32[1024]{0:T(1024)S(1)} %pad_clamp_fusion.3), kind=kCustom, calls=%fused_computation.clone | custom fusion | bytes 49200 | tf_op jit(solution)/shard_map/jit(_take)/gather | solution.py:327
  30.5 0.0 copy-done.5
  30.6 0.1 fusion.9
  30.7 0.0 copy-done.8
  30.7 0.1 multiply_subtract_fusion
  30.8 0.6 %pad_maximum_fusion.1.col_ref = f32[4,4,128]{2,1,0:T(4,128)} fusion(f32[1,12,128]{2,1,0:T(8,128)S(1)} %get-tuple-element.44, f32[1,12,128]{2,1,0:T(8,128)S(1)} %get-tuple-element.43, f32[2,12,128]{2,1,0:T(8,128)S(1)} %slice.186), kind=kLoop, calls=%fused_computation.44 | loop fusion | flops 4096 | bytes 32768 | tf_op jit(solution)/shard_map/slice | solution.py:340
  31.4 0.6 %slice.189.row_ref = f32[4,8,128]{2,1,0:T(8,128)} slice(f32[4,12,128]{2,1,0:T(8,128)S(1)} %pad_maximum_fusion), slice={[0:4], [0:8], [0:128]} | slice | bytes 32768 | tf_op jit(solution)/shard_map/slice | solution.py:340
  32.0 18.5 %shard_map.74 = (f32[8,4,8,128]{3,2,1,0:T(8,128)}, f32[8,4,4,128]{3,2,1,0:T(4,128)}) custom-call(f32[4,8,128]{2,1,0:T(8,128)} %slice.189.row_ref, f32[4,4,128]{2,1,0:T(4,128)} %pad_maximum_fusion.1.col_ref), custom_call_target="tpu_custom_call" | custom-call | tf_op jit(solution)/shard_map/pallas_call | solution.py:129
  50.6 0.9 %copy.38 = f32[4,2,4,8,128]{4,3,2,1,0:T(8,128)S(1)} copy(f32[4,2,4,8,128]{4,3,0,2,1:T(8,128)} %bitcast.94) | data formatting | bytes 262144 | tf_op jit(solution)/shard_map/transpose | solution.py:347
  51.5 0.9 %copy.21 = f32[4,2,4,4,128]{4,3,2,0,1:T(4,128)S(1)} copy(f32[4,2,4,4,128]{4,3,0,2,1:T(4,128)} %bitcast.95) | data formatting | bytes 131072 | tf_op jit(solution)/shard_map/transpose | solution.py:343
  52.4 0.1 copy.22
  52.5 0.1 pad.18.clone
  52.6 0.1 pad.22.clone
  52.6 0.0 copy-done.2
  52.6 1.3 %fusion.2 = f32[4,1,16,32,128]{4,3,2,1,0:T(8,128)} fusion(f32[4,18,34,128]{3,2,1,0:T(8,128)S(1)} %copy-done.2, f32[4,1,32,128]{3,2,1,0:T(8,128)S(1)} %get-tuple-element.40, f32[4,1,32,128]{3,2,1,0:T(8,128)S(1)} %get-tuple-element.39, f32[4,2,32,128]{3,2,1,0:T(8,128)S(1)} %bitcast.88, f32[4,16,1,128]{3,2,1,0:T(1,128)S(1)} %bitcast.93, ...), kind=kLoop, calls=%fused_computation.17 | loop fusion | flops 2097152 | bytes 2490608 | tf_op jit(solution)/shard_map/broadcast_in_dim | solution.py:360
  (20 shorter events, 0.2 us)
Async XLA Ops:
  0.0 2.8 %copy-start.3 = (f32[1,16,32,128]{3,2,1,0:T(8,128)S(1)}, f32[1,16,32,128]{3,2,1,0:T(8,128)}, u32[]{:S(2)}) copy-start(f32[1,16,32,128]{3,2,1,0:T(8,128)} %param.13) | copy-start | bytes 786436
  0.0 2.8 %copy-start.4 = (f32[1,16,32,128]{3,2,1,0:T(8,128)S(1)}, f32[1,16,32,128]{3,2,1,0:T(8,128)}, u32[]{:S(2)}) copy-start(f32[1,16,32,128]{3,2,1,0:T(8,128)} %param.12) | copy-start | bytes 786436
  15.6 2.0 %copy-start = (f32[4,22,48,128]{3,2,1,0:T(8,128)S(1)}, f32[4,22,48,128]{3,2,1,0:T(8,128)}, u32[]{:S(2)}) copy-start(f32[4,22,48,128]{3,2,1,0:T(8,128)} %get-tuple-element.22) | copy-start | bytes 6488068
  17.6 1.2 %copy-start.1 = (f32[2,18,48,128]{3,2,1,0:T(8,128)S(1)}, f32[2,18,48,128]{3,2,1,0:T(8,128)}, u32[]{:S(2)}) copy-start(f32[2,18,48,128]{3,2,1,0:T(8,128)} %get-tuple-element.23) | copy-start | bytes 2654212
  27.5 0.7 %copy-start.6 = (s32[1,1,1,12]{3,2,1,0:T(1,128)S(1)}, s32[1,1,1,12]{3,2,1,0:T(1,128)}, u32[]{:S(2)}) copy-start(s32[1,1,1,12]{3,2,1,0:T(1,128)} %param.15) | copy-start | bytes 148
  27.5 0.7 %copy-start.7 = (s32[1,1,1,12]{3,2,1,0:T(1,128)S(1)}, s32[1,1,1,12]{3,2,1,0:T(1,128)}, u32[]{:S(2)}) copy-start(s32[1,1,1,12]{3,2,1,0:T(1,128)} %param.14) | copy-start | bytes 148
  27.5 3.1 %copy-start.5 = (f32[1,1,1,2,12]{4,3,2,1,0:T(2,128)S(1)}, f32[1,1,1,2,12]{4,3,2,1,0:T(2,128)}, u32[]{:S(2)}) copy-start(f32[1,1,1,2,12]{4,3,2,1,0:T(2,128)} %param.16) | copy-start | bytes 292
  27.5 3.2 %copy-start.8 = (f32[1,1,1,12]{3,2,1,0:T(1,128)S(1)}, f32[1,1,1,12]{3,2,1,0:T(1,128)}, u32[]{:S(2)}) copy-start(f32[1,1,1,12]{3,2,1,0:T(1,128)} %param.17) | copy-start | bytes 148
  28.0 24.7 %copy-start.2 = (f32[4,18,34,128]{3,2,1,0:T(8,128)S(1)}, f32[4,18,34,128]{3,2,1,0:T(8,128)}, u32[]{:S(2)}) copy-start(f32[4,18,34,128]{3,2,1,0:T(8,128)} %get-tuple-element.35) | copy-start | bytes 3760132

commit v4 on v3

--- a/solution.py
+++ b/solution.py
@@ -261,10 +261,7 @@
         input_output_aliases={0: 0, 1: 1},
         compiler_params=pltpu.CompilerParams(collective_id=1, has_side_effects=True),
     )(fields_pad, coefs_pad)
-    return (
-        fields_pad[:, :, lane_pad - width : lane_pad + fields.shape[2] + width],
-        coefs_pad[:, :, lane_pad - 1 : lane_pad + fields.shape[2] + 1],
-    )
+    return fields_pad, coefs_pad
 
 
 def gradient(stencil):
@@ -273,6 +270,70 @@
 
 def curvature(stencil):
     return (16.0 * (stencil[3] + stencil[1]) - (stencil[4] + stencil[0]) - 30.0 * stencil[2]) / 12.0
+
+
+def shifted(block, step):
+    size = block.shape[-1]
+    lane = lax.broadcasted_iota(jnp.int32, block.shape, block.ndim - 1)
+    moved = pltpu.roll(block, (size - step) % size, block.ndim - 1)
+    keep = jnp.logical_and(lane + step >= 0, lane + step < size)
+    return jnp.where(keep, moved, 0.0)
+
+
+def stencil_kernel(row_pad, col_pad, fields_ref, coefs_ref, out_ref):
+    colat = lax.axis_index("colat")
+    lon = lax.axis_index("lon")
+    colat_count = lax.axis_size("colat")
+    lon_count = lax.axis_size("lon")
+    ext_rows, span, radial_len = out_ref.shape[1], out_ref.shape[2], out_ref.shape[3]
+    height = ext_rows - 2
+    breadth = fields_ref.shape[2] - 2 * col_pad
+    lead = (span - breadth) // 2
+    col_ids = lax.broadcasted_iota(jnp.int32, (span, radial_len), 0) - lead + lon * breadth
+    col_ok = jnp.logical_and(col_ids >= 0, col_ids < lon_count * breadth)
+
+    def body(row, carry):
+        global_row = row - 1 + colat * height
+        ok = jnp.logical_and(col_ok, jnp.logical_and(global_row >= 0, global_row < colat_count * height))
+
+        def load(field, down, across):
+            return fields_ref[field, row + row_pad - 1 + down, pl.ds(col_pad - lead + across, span), :]
+
+        center = [load(field, 0, 0) for field in range(4)]
+        thermal = coefs_ref[0, row, pl.ds(col_pad - lead, span), :]
+        viscous = coefs_ref[1, row, pl.ds(col_pad - lead, span), :]
+        for field in range(4):
+            along_lat = [load(field, offset - 2, 0) for offset in range(5)]
+            along_lon = [load(field, 0, offset - 2) for offset in range(5)]
+            along_rad = [shifted(center[field], offset - 2) for offset in range(5)]
+            laplace = curvature(along_rad) + curvature(along_lat) + curvature(along_lon)
+            transport = (
+                center[1] * gradient(along_rad)
+                + center[2] * gradient(along_lat)
+                + center[3] * gradient(along_lon)
+            )
+            change = (thermal if field == 0 else viscous) * laplace - transport
+            if field == 1:
+                change = change + BUOYANCY * center[0]
+            out_ref[field, row] = jnp.where(ok, center[field] + TIME_STEP * change, 0.0)
+        return carry
+
+    lax.fori_loop(0, ext_rows, body, 0)
+
+
+def stepped(fields_pad, coefs_pad, row_pad, col_pad, lead):
+    height = coefs_pad.shape[1] - 2
+    breadth = fields_pad.shape[2] - 2 * col_pad
+    span = breadth + 2 * lead
+    vmem = pl.BlockSpec(memory_space=pltpu.VMEM)
+    return pl.pallas_call(
+        functools.partial(stencil_kernel, row_pad, col_pad),
+        out_shape=jax.ShapeDtypeStruct(
+            (4, height + 2, span, fields_pad.shape[3]), fields_pad.dtype
+        ),
+        in_specs=[vmem, vmem],
+        out_specs=vmem,
+    )(fields_pad, coefs_pad)
 
 
 def advance(padded, thermal, viscous):
@@ -309,19 +370,13 @@
     lon_count = lax.axis_size("lon")
     row_share = 4 * breadth // colat_count
     coefs = jnp.concatenate([thermal[None], viscous[None]], axis=0)
-    padded, coef_ext = halo_exchange(fields, coefs, 3)
-    fresh_ext = advance(padded, coef_ext[0], coef_ext[1])
-    row_ids = lax.broadcasted_iota(jnp.int32, (height + 2, breadth + 2), 0) + colat_pos * height - 1
-    col_ids = lax.broadcasted_iota(jnp.int32, (height + 2, breadth + 2), 1) + lon_pos * breadth - 1
-    in_panel = (
-        (row_ids >= 0) & (row_ids < colat_count * height)
-        & (col_ids >= 0) & (col_ids < lon_count * breadth)
-    )
-    extended = jnp.where(in_panel[None, :, :, None], fresh_ext, 0.0)
-    fresh = fresh_ext[:, 1 : 1 + height, 1 : 1 + breadth]
-    width = breadth + 2
+    fields_pad, coefs_pad = halo_exchange(fields, coefs, 3)
+    lead = 4
+    extended = stepped(fields_pad, coefs_pad, 3, 8, lead)
+    fresh = extended[:, 1 : 1 + height, lead : lead + breadth]
+    width = extended.shape[2]
     flattened = extended.reshape(4, (height + 2) * width, radial_len)
-    anchor = donor_row.reshape(-1) * width + donor_column.reshape(-1)
+    anchor = donor_row.reshape(-1) * width + donor_column.reshape(-1) + (lead - 1)
 
     def corner(offset):
         return jnp.take(flattened, anchor + offset, axis=1)

time: 54.4 us -> 50.2 us (0.923)
  other arithmetic: 13.3 us -> 3.14 us
  Pallas kernels: 30.3 us -> 36.7 us
    pallas_call x0 -> x1, Pallas kernels: none -> 6.4 us  [stepped(): pl.pallas_call(functools.partial(stencil_kernel, row_pad, col_pad), out_s...]
    sub x1 -> x0, other arithmetic: 3.9 us -> none  [advance(): change = diffusion * laplace - transport]
    select_n x2 -> x0, other arithmetic: 2.84 us -> none  [the longest x1 2.83 us: local(): extended = jnp.where(in_panel[None, :, :, None], fresh_ext, 0.0)]
    reshape x0 -> x1, local copies, waits for them, and re-layouts: none -> 1.99 us  [local(): flattened = extended.reshape(4, (height + 2) * width, radial_len)]
    scatter-add x1 -> x0, other arithmetic: 1.76 us -> none  [advance(): change = change.at[1].add(BUOYANCY * center[0])]
    unnamed x18 -> x14, local copies, waits for them, and re-layouts: 1.64 us -> 0.03 us
    mul x1 -> x0, other arithmetic: 1.57 us -> none  [advance(): center[1:2] * gradient(along_rad) + center[2:3] * gradient(along_lat)]
where the time goes in v4:
time: 50.2 us; the launch traced here: 49.8 us
  Pallas kernels  36.7 us (73%)
  local copies, waits for them, and re-layouts  9.79 us (20%)
  other arithmetic  3.14 us (6%)
    pallas_call x1, Pallas kernels, rim_exchange(): pl.pallas_call(rim_kernel, out_shape=(jax.ShapeDtypeStruct((2 * row_types...  18.5 us
    pallas_call x1, Pallas kernels, halo_exchange(): pl.pallas_call(functools.partial(halo_kernel, width, margins), out_shape=...  11.8 us
    pallas_call x1, Pallas kernels, stepped(): pl.pallas_call(functools.partial(stencil_kernel, row_pad, col_pad), out_s...  6.4 us
    pad x1, local copies, waits for them, and re-layouts, halo_exchange(): jnp.pad(fields, ((0, 0), (width, width), (lane_pad, lane_pad), (0, 0)))  2.82 us
    gather x4, local copies, waits for them, and re-layouts, corner(): return jnp.take(flattened, anchor + offset, axis=1)  2.31 us
    reshape x1, local copies, waits for them, and re-layouts, local(): flattened = extended.reshape(4, (height + 2) * width, radial_len)  1.99 us
    broadcast_in_dim x1, other arithmetic, local(): return fresh[:, None]  1.32 us

profile of v4, /device:TPU:6, one launch (start us, length us, event | category | flops | bytes accessed | tf_op | source)
XLA Modules:
  0.0 49.8 jit_solution(17979721572717629890)
XLA Ops:
  0.0 0.0 copy-start.1
  0.0 0.0 copy-start.2
  0.0 2.8 %pad.8.fields_in = f32[4,22,48,128]{3,2,1,0:T(8,128)} pad(f32[4,16,32,128]{3,2,1,0:T(8,128)} %bitcast.73, f32[]{:T(128)} %constant.18.clone.1), padding=0_0x3_3x8_8x0_0 | pad | bytes 3211268 | tf_op jit(solution)/shard_map/jit(_pad)/pad | solution.py:245
  2.8 0.0 copy-done.1
  2.8 0.0 copy-done.2
  2.8 1.0 %select_maximum_fusion.coefs_in = f32[2,18,48,128]{3,2,1,0:T(8,128)} fusion(f32[1,16,32,128]{3,2,1,0:T(8,128)S(1)} %copy-done.1, f32[1,16,32,128]{3,2,1,0:T(8,128)S(1)} %copy-done.2), kind=kLoop, calls=%fused_computation.11 | loop fusion | flops 2654208 | bytes 1409024 | tf_op jit(solution)/shard_map/concatenate | solution.py:372
  3.8 11.8 %shard_map.73 = (f32[4,22,48,128]{3,2,1,0:T(8,128)}, f32[2,18,48,128]{3,2,1,0:T(8,128)}) custom-call(f32[4,22,48,128]{3,2,1,0:T(8,128)} %pad.8.fields_in, f32[2,18,48,128]{3,2,1,0:T(8,128)} %select_maximum_fusion.coefs_in), custom_call_target="tpu_custom_call", output_to_operand_aliasing={{0}: (0, {}), {1}: (1, {})} | custom-call | tf_op jit(solution)/shard_map/pallas_call | solution.py:249
  15.6 6.4 %shard_map.74 = f32[4,18,40,128]{3,2,1,0:T(8,128)} custom-call(f32[4,22,48,128]{3,2,1,0:T(8,128)} %get-tuple-element.10.fields_ref, f32[2,18,48,128]{3,2,1,0:T(8,128)} %get-tuple-element.11.coefs_ref), custom_call_target="tpu_custom_call" | custom-call | tf_op jit(solution)/shard_map/pallas_call | solution.py:329
  22.0 0.0 copy-start.4
  22.0 0.0 copy-start.5
  22.0 0.0 copy-start.3
  22.0 0.0 copy-start.6
  22.0 2.0 %copy.15 = f32[4,720,128]{2,0,1:T(4,128)S(1)} copy(f32[4,720,128]{2,1,0:T(8,128)} %bitcast.70) | data formatting | bytes 2949120 | tf_op jit(solution)/shard_map/reshape | solution.py:378
  24.0 0.0 copy-done.4
  24.0 0.0 copy-done.5
  24.0 0.0 copy-start
  24.1 0.6 %gather_fusion.3 = f32[12,4,128]{2,1,0:T(4,128)S(1)} fusion(f32[4,720,128]{2,0,1:T(4,128)S(1)} %copy.15, s32[1024]{0:T(1024)S(1)} %get-tuple-element.39), kind=kCustom, calls=%fused_computation.3.clone | custom fusion | bytes 49200 | tf_op jit(solution)/shard_map/jit(_take)/gather | solution.py:382
  24.7 0.6 %gather_fusion.2 = f32[12,4,128]{2,1,0:T(4,128)S(1)} fusion(f32[4,720,128]{2,0,1:T(4,128)S(1)} %copy.15, s32[1024]{0:T(1024)S(1)} %get-tuple-element.40), kind=kCustom, calls=%fused_computation.2.clone | custom fusion | bytes 49200 | tf_op jit(solution)/shard_map/jit(_take)/gather | solution.py:382
  25.3 0.6 %gather_fusion.1 = f32[12,4,128]{2,1,0:T(4,128)S(1)} fusion(f32[4,720,128]{2,0,1:T(4,128)S(1)} %copy.15, s32[1024]{0:T(1024)S(1)} %pad_clamp_fusion.2), kind=kCustom, calls=%fused_computation.1.clone | custom fusion | bytes 49200 | tf_op jit(solution)/shard_map/jit(_take)/gather | solution.py:382
  25.9 0.6 %gather_fusion = f32[12,4,128]{2,1,0:T(4,128)S(1)} fusion(f32[4,720,128]{2,0,1:T(4,128)S(1)} %copy.15, s32[1024]{0:T(1024)S(1)} %pad_clamp_fusion.3), kind=kCustom, calls=%fused_computation.clone | custom fusion | bytes 49200 | tf_op jit(solution)/shard_map/jit(_take)/gather | solution.py:382
  26.4 0.0 copy-done.3
  26.5 0.1 fusion.7
  26.6 0.0 copy-done.6
  26.6 0.1 multiply_subtract_fusion
  26.7 0.6 %slice.63.row_ref = f32[4,8,128]{2,1,0:T(8,128)} slice(f32[4,12,128]{2,1,0:T(8,128)S(1)} %pad_maximum_fusion), slice={[0:4], [0:8], [0:128]} | slice | bytes 32768 | tf_op jit(solution)/shard_map/slice | solution.py:395
  27.3 0.6 %pad_maximum_fusion.1.col_ref = f32[4,4,128]{2,1,0:T(4,128)} fusion(f32[1,12,128]{2,1,0:T(8,128)S(1)} %get-tuple-element.28, f32[1,12,128]{2,1,0:T(8,128)S(1)} %get-tuple-element.27, f32[2,12,128]{2,1,0:T(8,128)S(1)} %slice.60), kind=kLoop, calls=%fused_computation.30 | loop fusion | flops 4096 | bytes 32768 | tf_op jit(solution)/shard_map/slice | solution.py:395
  27.9 18.5 %shard_map.75 = (f32[8,4,8,128]{3,2,1,0:T(8,128)}, f32[8,4,4,128]{3,2,1,0:T(4,128)}) custom-call(f32[4,8,128]{2,1,0:T(8,128)} %slice.63.row_ref, f32[4,4,128]{2,1,0:T(4,128)} %pad_maximum_fusion.1.col_ref), custom_call_target="tpu_custom_call" | custom-call | tf_op jit(solution)/shard_map/pallas_call | solution.py:129
  46.5 0.9 %copy.41 = f32[4,2,4,8,128]{4,3,2,1,0:T(8,128)S(1)} copy(f32[4,2,4,8,128]{4,3,0,2,1:T(8,128)} %bitcast.78) | data formatting | bytes 262144 | tf_op jit(solution)/shard_map/transpose | solution.py:402
  47.4 0.9 %copy.24 = f32[4,2,4,4,128]{4,3,2,0,1:T(4,128)S(1)} copy(f32[4,2,4,4,128]{4,3,0,2,1:T(4,128)} %bitcast.79) | data formatting | bytes 131072 | tf_op jit(solution)/shard_map/transpose | solution.py:398
  48.3 0.1 copy.25
  48.3 0.1 pad.11.clone
  48.4 0.1 pad.15.clone
  48.5 0.0 copy-done
  48.5 1.3 %fusion.1 = f32[4,1,16,32,128]{4,3,2,1,0:T(8,128)} fusion(f32[4,18,40,128]{3,2,1,0:T(8,128)S(1)} %copy-done, f32[4,1,32,128]{3,2,1,0:T(8,128)S(1)} %get-tuple-element.24, f32[4,1,32,128]{3,2,1,0:T(8,128)S(1)} %get-tuple-element.23, f32[4,2,32,128]{3,2,1,0:T(8,128)S(1)} %bitcast.72, f32[4,16,1,128]{3,2,1,0:T(1,128)S(1)} %bitcast.77, ...), kind=kLoop, calls=%fused_computation.10 | loop fusion | flops 2097152 | bytes 2490608 | tf_op jit(solution)/shard_map/broadcast_in_dim | solution.py:415
  (16 shorter events, 0.1 us)
Async XLA Ops:
  0.0 2.8 %copy-start.1 = (f32[1,16,32,128]{3,2,1,0:T(8,128)S(1)}, f32[1,16,32,128]{3,2,1,0:T(8,128)}, u32[]{:S(2)}) copy-start(f32[1,16,32,128]{3,2,1,0:T(8,128)} %param.11) | copy-start | bytes 786436
  0.0 2.8 %copy-start.2 = (f32[1,16,32,128]{3,2,1,0:T(8,128)S(1)}, f32[1,16,32,128]{3,2,1,0:T(8,128)}, u32[]{:S(2)}) copy-start(f32[1,16,32,128]{3,2,1,0:T(8,128)} %param.10) | copy-start | bytes 786436
  22.0 2.0 %copy-start.4 = (s32[1,1,1,12]{3,2,1,0:T(1,128)S(1)}, s32[1,1,1,12]{3,2,1,0:T(1,128)}, u32[]{:S(2)}) copy-start(s32[1,1,1,12]{3,2,1,0:T(1,128)} %param.13) | copy-start | bytes 148
  22.0 2.0 %copy-start.5 = (s32[1,1,1,12]{3,2,1,0:T(1,128)S(1)}, s32[1,1,1,12]{3,2,1,0:T(1,128)}, u32[]{:S(2)}) copy-start(s32[1,1,1,12]{3,2,1,0:T(1,128)} %param.12) | copy-start | bytes 148
  22.0 4.4 %copy-start.3 = (f32[1,1,1,2,12]{4,3,2,1,0:T(2,128)S(1)}, f32[1,1,1,2,12]{4,3,2,1,0:T(2,128)}, u32[]{:S(2)}) copy-start(f32[1,1,1,2,12]{4,3,2,1,0:T(2,128)} %param.14) | copy-start | bytes 292
  22.0 4.6 %copy-start.6 = (f32[1,1,1,12]{3,2,1,0:T(1,128)S(1)}, f32[1,1,1,12]{3,2,1,0:T(1,128)}, u32[]{:S(2)}) copy-start(f32[1,1,1,12]{3,2,1,0:T(1,128)} %param.15) | copy-start | bytes 148
  24.0 24.5 %copy-start = (f32[4,18,40,128]{3,2,1,0:T(8,128)S(1)}, f32[4,18,40,128]{3,2,1,0:T(8,128)}, u32[]{:S(2)}) copy-start(f32[4,18,40,128]{3,2,1,0:T(8,128)} %shard_map.74) | copy-start | bytes 4423684

commit v5 on v4

--- a/solution.py
+++ b/solution.py
@@ -280,11 +280,57 @@
     return jnp.where(keep, moved, 0.0)
 
 
-def stencil_kernel(row_pad, col_pad, fields_ref, coefs_ref, out_ref):
+def step_kernel(
+    row_pad, col_pad, fields_ref, coefs_ref, rows_ref, cols_ref, frac_ref, trig_ref,
+    out_ref, row_out, col_out, row_send, col_send, send_sem, row_sem, col_sem,
+):
+    panel = lax.axis_index("panel")
     colat = lax.axis_index("colat")
     lon = lax.axis_index("lon")
     colat_count = lax.axis_size("colat")
     lon_count = lax.axis_size("lon")
+    row_types = row_out.shape[0] // 2
+    col_types = col_out.shape[0] // 2
+    row_share = row_send.shape[1]
+    other = 1 - panel
+
+    def route(share, per_type, count):
+        kind = share // per_type
+        edge = (kind % 2) * (count - 1)
+        slot = (kind // 2) * per_type + share % per_type
+        return edge, slot
+
+    row_edge, row_slot = route(colat, row_types, colat_count)
+    col_edge, col_slot = route(lon, col_types, lon_count)
+    row_dest = (other, row_edge, lon)
+    col_dest = (other, colat, col_edge)
+    at_row_edge = jnp.logical_or(colat == 0, colat == colat_count - 1)
+    at_col_edge = jnp.logical_or(lon == 0, lon == lon_count - 1)
+    parity_row = (colat // (colat_count - 1)).astype(jnp.int32)
+    parity_col = (lon // (lon_count - 1)).astype(jnp.int32)
+
+    def row_sender(slot):
+        kind = 2 * (slot // row_types) + parity_row
+        return (other, kind * row_types + slot % row_types, lon)
+
+    def col_sender(slot):
+        kind = 2 * (slot // col_types) + parity_col
+        return (other, colat, kind * col_types + slot % col_types)
+
+    barrier = pltpu.get_barrier_semaphore()
+    pl.semaphore_signal(barrier, 1, device_id=row_dest, device_id_type=MESH)
+    pl.semaphore_signal(barrier, 1, device_id=col_dest, device_id_type=MESH)
+
+    @pl.when(at_row_edge)
+    def _():
+        for slot in range(2 * row_types):
+            pl.semaphore_signal(barrier, 1, device_id=row_sender(slot), device_id_type=MESH)
+
+    @pl.when(at_col_edge)
+    def _():
+        for slot in range(2 * col_types):
+            pl.semaphore_signal(barrier, 1, device_id=col_sender(slot), device_id_type=MESH)
+
     ext_rows, span, radial_len = out_ref.shape[1], out_ref.shape[2], out_ref.shape[3]
     height = ext_rows - 2
     breadth = fields_ref.shape[2] - 2 * col_pad
@@ -320,20 +366,101 @@
 
     lax.fori_loop(0, ext_rows, body, 0)
 
-
-def stepped(fields_pad, coefs_pad, row_pad, col_pad, lead):
+    slots = rows_ref.shape[0]
+    column = lax.broadcasted_iota(jnp.int32, (span, radial_len), 0)
+    for slot in range(slots):
+        first = rows_ref[slot]
+        across = cols_ref[slot] + (lead - 1)
+        frac_row = frac_ref[0, slot]
+        frac_lon = frac_ref[1, slot]
+        weight = jnp.where(
+            column == across, 1.0 - frac_lon, jnp.where(column == across + 1, frac_lon, 0.0)
+        )
+        mixed = []
+        for field in range(4):
+            upper = jnp.sum(weight * out_ref[field, first], axis=0, keepdims=True)
+            lower = jnp.sum(weight * out_ref[field, first + 1], axis=0, keepdims=True)
+            mixed.append((1.0 - frac_row) * upper + frac_row * lower)
+        cosine = trig_ref[0, slot]
+        sine_part = trig_ref[1, slot]
+        turned = [
+            mixed[0],
+            mixed[1],
+            cosine * mixed[2] - sine_part * mixed[3],
+            sine_part * mixed[2] + cosine * mixed[3],
+        ]
+        for field in range(4):
+            if slot < row_share:
+                row_send[field, pl.ds(slot, 1), :] = turned[field]
+            else:
+                col_send[field, pl.ds(slot - row_share, 1), :] = turned[field]
+
+    expected = (
+        2
+        + at_row_edge.astype(jnp.int32) * (2 * row_types)
+        + at_col_edge.astype(jnp.int32) * (2 * col_types)
+    )
+    pl.semaphore_wait(barrier, expected)
+
+    row_copy = pltpu.make_async_remote_copy(
+        row_send, row_out.at[row_slot], send_sem.at[0], row_sem.at[row_slot],
+        device_id=row_dest, device_id_type=MESH,
+    )
+    col_copy = pltpu.make_async_remote_copy(
+        col_send, col_out.at[col_slot], send_sem.at[1], col_sem.at[col_slot],
+        device_id=col_dest, device_id_type=MESH,
+    )
+    row_copy.start()
+    col_copy.start()
+    row_copy.wait_send()
+    col_copy.wait_send()
+
+    @pl.when(at_row_edge)
+    def _():
+        for slot in range(2 * row_types):
+            pltpu.make_async_remote_copy(
+                row_send, row_out.at[slot], send_sem.at[0], row_sem.at[slot],
+                device_id=row_sender(slot), device_id_type=MESH,
+            ).wait_recv()
+
+    @pl.when(at_col_edge)
+    def _():
+        for slot in range(2 * col_types):
+            pltpu.make_async_remote_copy(
+                col_send, col_out.at[slot], send_sem.at[1], col_sem.at[slot],
+                device_id=col_sender(slot), device_id_type=MESH,
+            ).wait_recv()
+
+
+def stepped(fields_pad, coefs_pad, row_pad, col_pad, lead, rows, cols, frac, trig, row_share):
     height = coefs_pad.shape[1] - 2
     breadth = fields_pad.shape[2] - 2 * col_pad
     span = breadth + 2 * lead
+    radial_len = fields_pad.shape[3]
+    slots = rows.shape[0]
+    row_types = lax.axis_size("colat") // 4
+    col_types = lax.axis_size("lon") // 4
+    dtype = fields_pad.dtype
     vmem = pl.BlockSpec(memory_space=pltpu.VMEM)
+    smem = pl.BlockSpec(memory_space=pltpu.SMEM)
     return pl.pallas_call(
-        functools.partial(stencil_kernel, row_pad, col_pad),
-        out_shape=jax.ShapeDtypeStruct(
-            (4, height + 2, span, fields_pad.shape[3]), fields_pad.dtype
+        functools.partial(step_kernel, row_pad, col_pad),
+        out_shape=(
+            jax.ShapeDtypeStruct((4, height + 2, span, radial_len), dtype),
+            jax.ShapeDtypeStruct((2 * row_types, 4, row_share, radial_len), dtype),
+            jax.ShapeDtypeStruct((2 * col_types, 4, slots - row_share, radial_len), dtype),
         ),
-        in_specs=[vmem, vmem],
-        out_specs=vmem,
-    )(fields_pad, coefs_pad)
+        in_specs=[vmem, vmem, smem, smem, smem, smem],
+        out_specs=(vmem, vmem, vmem),
+        scratch_shapes=[
+            pltpu.VMEM((4, row_share, radial_len), dtype),
+            pltpu.VMEM((4, slots - row_share, radial_len), dtype),
+            pltpu.SemaphoreType.DMA((2,)),
+            pltpu.SemaphoreType.DMA((2 * row_types,)),
+            pltpu.SemaphoreType.DMA((2 * col_types,)),
+        ],
+        compiler_params=pltpu.CompilerParams(collective_id=0, has_side_effects=True),
+    )(fields_pad, coefs_pad, rows, cols, frac, trig)
 
 
 def advance(padded, thermal, viscous):
@@ -372,28 +499,16 @@
     coefs = jnp.concatenate([thermal[None], viscous[None]], axis=0)
     fields_pad, coefs_pad = halo_exchange(fields, coefs, 3)
     lead = 4
-    extended = stepped(fields_pad, coefs_pad, 3, 8, lead)
+    angles = rim_angle.reshape(-1)
+    trig = jnp.stack([jnp.cos(angles), jnp.sin(angles)])
+    frac = donor_offset.reshape(2, -1)
+    extended, row_buf, col_buf = stepped(
+        fields_pad, coefs_pad, 3, 8, lead, donor_row.reshape(-1), donor_column.reshape(-1),
+        frac, trig, row_share,
+    )
     fresh = extended[:, 1 : 1 + height, lead : lead + breadth]
-    width = extended.shape[2]
-    flattened = extended.reshape(4, (height + 2) * width, radial_len)
-    anchor = donor_row.reshape(-1) * width + donor_column.reshape(-1) + (lead - 1)
-
-    def corner(offset):
-        return jnp.take(flattened, anchor + offset, axis=1)
-
-    frac_row = donor_offset[0, 0, 0, 0][None, :, None]
-    frac_lon = donor_offset[0, 0, 0, 1][None, :, None]
-    blended = (1.0 - frac_row) * (
-        (1.0 - frac_lon) * corner(0) + frac_lon * corner(1)
-    ) + frac_row * ((1.0 - frac_lon) * corner(width) + frac_lon * corner(width + 1))
-    angles = rim_angle.reshape(-1)
-    cosine = jnp.cos(angles)[:, None]
-    sine_part = jnp.sin(angles)[:, None]
-    turned_lat = cosine * blended[2] - sine_part * blended[3]
-    turned_lon = sine_part * blended[2] + cosine * blended[3]
-    blended = jnp.stack([blended[0], blended[1], turned_lat, turned_lon])
-    row_buf, col_buf = rim_exchange(blended[:, 0:row_share], blended[:, row_share:])
-    col_share = blended.shape[1] - row_share
+    slot_count = donor_row.shape[-1]
+    col_share = slot_count - row_share
     col_strip = col_buf.reshape(2, col_buf.shape[0] // 2, 4, col_share, radial_len)
     col_strip = jnp.transpose(col_strip, (2, 0, 1, 3, 4)).reshape(4, 2, height, radial_len)
     west_strip = jnp.transpose(col_strip, (0, 2, 1, 3))

time: 50.2 us -> 45.2 us (0.900)
  local copies, waits for them, and re-layouts: 9.79 us -> 4.86 us
  other arithmetic: 3.14 us -> 4.19 us
  Pallas kernels: 36.7 us -> 35.8 us
    gather x4 -> x0, local copies, waits for them, and re-layouts: 2.31 us -> none  [corner(): return jnp.take(flattened, anchor + offset, axis=1)]
    reshape x1 -> x0, local copies, waits for them, and re-layouts: 1.99 us -> none  [local(): flattened = extended.reshape(4, (height + 2) * width, radial_len)]
    broadcast_in_dim x1, other arithmetic: 1.32 us -> 2.64 us  [local(): return fresh[:, None]]
    pallas_call x2 -> x1, Pallas kernels: 24.9 us -> 24 us  [stepped(): pl.pallas_call(functools.partial(step_kernel, row_pad, col_pad), out_shap...]
    slice x2 -> x0, local copies, waits for them, and re-layouts: 0.61 us -> none  [the longest x1 0.61 us: local(): blended[:, 0:row_share]]
    slice x1 -> x0, other arithmetic: 0.6 us -> none  [local(): blended[:, row_share:]]
    another operation x1, other arithmetic: 0.01 us -> 0.58 us  [local(): trig = jnp.stack([jnp.cos(angles), jnp.sin(angles)])]
where the time goes in v5:
time: 45.2 us; the launch traced here: 44.9 us
  Pallas kernels  35.8 us (79%)
  local copies, waits for them, and re-layouts  4.86 us (11%)
  other arithmetic  4.19 us (9%)
    pallas_call x1, Pallas kernels, stepped(): pl.pallas_call(functools.partial(step_kernel, row_pad, col_pad), out_shap...  24 us
    pallas_call x1, Pallas kernels, halo_exchange(): pl.pallas_call(functools.partial(halo_kernel, width, margins), out_shape=...  11.8 us
    pad x1, local copies, waits for them, and re-layouts, halo_exchange(): jnp.pad(fields, ((0, 0), (width, width), (lane_pad, lane_pad), (0, 0)))  2.82 us
    broadcast_in_dim x1, other arithmetic, local(): return fresh[:, None]  2.64 us
    concatenate x1, other arithmetic, local(): coefs = jnp.concatenate([thermal[None], viscous[None]], axis=0)  0.96 us
    transpose x1, local copies, waits for them, and re-layouts, local(): jnp.transpose(row_strip, (2, 0, 1, 3, 4)).reshape(4, 2, breadth, radial_len)  0.91 us

profile of v5, /device:TPU:6, one launch (start us, length us, event | category | flops | bytes accessed | tf_op | source)
XLA Modules:
  0.0 44.9 jit_solution(1529234414289853486)
XLA Ops:
  0.0 0.0 copy-start
  0.0 0.0 copy-start.1
  0.0 2.8 %pad.8.fields_in = f32[4,22,48,128]{3,2,1,0:T(8,128)} pad(f32[4,16,32,128]{3,2,1,0:T(8,128)} %bitcast.30, f32[]{:T(128)} %constant.19.clone.1), padding=0_0x3_3x8_8x0_0 | pad | bytes 3211268 | tf_op jit(solution)/shard_map/jit(_pad)/pad | solution.py:245
  2.8 0.0 copy-done
  2.8 0.0 copy-done.1
  2.8 0.0 copy-start.2
  2.8 1.0 %select_maximum_fusion.coefs_in = f32[2,18,48,128]{3,2,1,0:T(8,128)} fusion(f32[1,16,32,128]{3,2,1,0:T(8,128)S(1)} %copy-done, f32[1,16,32,128]{3,2,1,0:T(8,128)S(1)} %copy-done.1), kind=kLoop, calls=%fused_computation.7 | loop fusion | flops 2654208 | bytes 1409024 | tf_op jit(solution)/shard_map/concatenate | solution.py:499
  3.8 11.8 %shard_map.73 = (f32[4,22,48,128]{3,2,1,0:T(8,128)}, f32[2,18,48,128]{3,2,1,0:T(8,128)}) custom-call(f32[4,22,48,128]{3,2,1,0:T(8,128)} %pad.8.fields_in, f32[2,18,48,128]{3,2,1,0:T(8,128)} %select_maximum_fusion.coefs_in), custom_call_target="tpu_custom_call", output_to_operand_aliasing={{0}: (0, {}), {1}: (1, {})} | custom-call | tf_op jit(solution)/shard_map/pallas_call | solution.py:249
  15.6 0.0 copy-done.2
  15.6 0.6 %pad_maximum_fusion.trig_ref = f32[2,12]{1,0:T(2,128)} fusion(f32[1,12]{1,0:T(1,128)S(1)} %get-tuple-element.20, f32[1,12]{1,0:T(1,128)S(1)} %get-tuple-element.19), kind=kLoop, calls=%fused_computation.14 | loop fusion | flops 24 | bytes 192 | tf_op jit(solution)/shard_map/stack | solution.py:503
  16.2 24.0 %shard_map.74 = (f32[4,18,40,128]{3,2,1,0:T(8,128)}, f32[8,4,8,128]{3,2,1,0:T(8,128)}, f32[8,4,4,128]{3,2,1,0:T(4,128)}) custom-call(f32[4,22,48,128]{3,2,1,0:T(8,128)} %get-tuple-element.10.fields_ref, f32[2,18,48,128]{3,2,1,0:T(8,128)} %get-tuple-element.11.coefs_ref, s32[12]{0:T(128)} %bitcast.38, s32[12]{0:T(128)} %bitcast.39, f32[2,12]{1,0:T(2,128)} %bitcast.37, ...), custom_call_target="tpu_custom_call" | custom-call | tf_op jit(solution)/shard_map/pallas_call | solution.py:446
  40.2 0.9 %copy.16 = f32[4,2,4,8,128]{4,3,2,1,0:T(8,128)S(1)} copy(f32[4,2,4,8,128]{4,3,0,2,1:T(8,128)} %bitcast.35) | data formatting | bytes 262144 | tf_op jit(solution)/shard_map/transpose | solution.py:517
  41.2 0.9 %copy.11 = f32[4,2,4,4,128]{4,3,2,0,1:T(4,128)S(1)} copy(f32[4,2,4,4,128]{4,3,0,2,1:T(4,128)} %bitcast.36) | data formatting | bytes 131072 | tf_op jit(solution)/shard_map/transpose | solution.py:513
  42.0 0.1 copy.12
  42.1 0.1 pad.11.clone
  42.2 0.1 pad.15.clone
  42.3 2.6 %fusion = f32[4,1,16,32,128]{4,3,2,1,0:T(8,128)} fusion(f32[4,1,32,128]{3,2,1,0:T(8,128)S(1)} %get-tuple-element.16, f32[4,1,32,128]{3,2,1,0:T(8,128)S(1)} %get-tuple-element.15, f32[4,2,32,128]{3,2,1,0:T(8,128)S(1)} %bitcast.29, f32[4,16,1,128]{3,2,1,0:T(1,128)S(1)} %bitcast.34, f32[4,16,1,128]{3,2,1,0:T(1,128)S(1)} %bitcast.33, ...), kind=kLoop, calls=%fused_computation.5 | loop fusion | flops 2097152 | bytes 2490608 | tf_op jit(solution)/shard_map/broadcast_in_dim | solution.py:530
  (7 shorter events, 0.1 us)
Async XLA Ops:
  0.0 2.8 %copy-start = (f32[1,16,32,128]{3,2,1,0:T(8,128)S(1)}, f32[1,16,32,128]{3,2,1,0:T(8,128)}, u32[]{:S(2)}) copy-start(f32[1,16,32,128]{3,2,1,0:T(8,128)} %param.9) | copy-start | bytes 786436
  0.0 2.8 %copy-start.1 = (f32[1,16,32,128]{3,2,1,0:T(8,128)S(1)}, f32[1,16,32,128]{3,2,1,0:T(8,128)}, u32[]{:S(2)}) copy-start(f32[1,16,32,128]{3,2,1,0:T(8,128)} %param.8) | copy-start | bytes 786436
  2.8 12.8 %copy-start.2 = (f32[1,1,1,12]{3,2,1,0:T(1,128)S(1)}, f32[1,1,1,12]{3,2,1,0:T(1,128)}, u32[]{:S(2)}) copy-start(f32[1,1,1,12]{3,2,1,0:T(1,128)} %param.13) | copy-start | bytes 148

commit v6 on v5

--- a/solution.py
+++ b/solution.py
@@ -34,113 +34,6 @@
         if high != low and high < count:
             route += [(low, high), (high, low)]
     return lax.ppermute(block, axis, route)
-
-
-def rim_kernel(row_ref, col_ref, row_out, col_out, send_sem, row_sem, col_sem):
-    panel = lax.axis_index("panel")
-    colat = lax.axis_index("colat")
-    lon = lax.axis_index("lon")
-    colat_count = lax.axis_size("colat")
-    lon_count = lax.axis_size("lon")
-    row_types = row_out.shape[0] // 2
-    col_types = col_out.shape[0] // 2
-    other = 1 - panel
-
-    def route(share, per_type, count):
-        kind = share // per_type
-        edge = (kind % 2) * (count - 1)
-        slot = (kind // 2) * per_type + share % per_type
-        return edge, slot
-
-    row_edge, row_slot = route(colat, row_types, colat_count)
-    col_edge, col_slot = route(lon, col_types, lon_count)
-    row_dest = (other, row_edge, lon)
-    col_dest = (other, colat, col_edge)
-    at_row_edge = jnp.logical_or(colat == 0, colat == colat_count - 1)
-    at_col_edge = jnp.logical_or(lon == 0, lon == lon_count - 1)
-    parity_row = (colat // (colat_count - 1)).astype(jnp.int32)
-    parity_col = (lon // (lon_count - 1)).astype(jnp.int32)
-
-    def row_sender(slot):
-        kind = 2 * (slot // row_types) + parity_row
-        return (other, kind * row_types + slot % row_types, lon)
-
-    def col_sender(slot):
-        kind = 2 * (slot // col_types) + parity_col
-        return (other, colat, kind * col_types + slot % col_types)
-
-    barrier = pltpu.get_barrier_semaphore()
-    pl.semaphore_signal(barrier, 1, device_id=row_dest, device_id_type=MESH)
-    pl.semaphore_signal(barrier, 1, device_id=col_dest, device_id_type=MESH)
-
-    @pl.when(at_row_edge)
-    def _():
-        for slot in range(2 * row_types):
-            pl.semaphore_signal(barrier, 1, device_id=row_sender(slot), device_id_type=MESH)
-
-    @pl.when(at_col_edge)
-    def _():
-        for slot in range(2 * col_types):
-            pl.semaphore_signal(barrier, 1, device_id=col_sender(slot), device_id_type=MESH)
-
-    expected = (
-        2
-        + at_row_edge.astype(jnp.int32) * (2 * row_types)
-        + at_col_edge.astype(jnp.int32) * (2 * col_types)
-    )
-    pl.semaphore_wait(barrier, expected)
-
-    row_copy = pltpu.make_async_remote_copy(
-        row_ref, row_out.at[row_slot], send_sem.at[0], row_sem.at[row_slot],
-        device_id=row_dest, device_id_type=MESH,
-    )
-    col_copy = pltpu.make_async_remote_copy(
-        col_ref, col_out.at[col_slot], send_sem.at[1], col_sem.at[col_slot],
-        device_id=col_dest, device_id_type=MESH,
-    )
-    row_copy.start()
-    col_copy.start()
-    row_copy.wait_send()
-    col_copy.wait_send()
-
-    @pl.when(at_row_edge)
-    def _():
-        for slot in range(2 * row_types):
-            pltpu.make_async_remote_copy(
-                row_ref, row_out.at[slot], send_sem.at[0], row_sem.at[slot],
-                device_id=row_sender(slot), device_id_type=MESH,
-            ).wait_recv()
-
-    @pl.when(at_col_edge)
-    def _():
-        for slot in range(2 * col_types):
-            pltpu.make_async_remote_copy(
-                col_ref, col_out.at[slot], send_sem.at[1], col_sem.at[slot],
-                device_id=col_sender(slot), device_id_type=MESH,
-            ).wait_recv()
-
-
-def rim_exchange(rows, cols):
-    colat_count = lax.axis_size("colat")
-    lon_count = lax.axis_size("lon")
-    row_types = colat_count // 4
-    col_types = lon_count // 4
-    vmem = pl.BlockSpec(memory_space=pltpu.VMEM)
-    return pl.pallas_call(
-        rim_kernel,
-        out_shape=(
-            jax.ShapeDtypeStruct((2 * row_types,) + rows.shape, rows.dtype),
-            jax.ShapeDtypeStruct((2 * col_types,) + cols.shape, cols.dtype),
-        ),
-        in_specs=[vmem, vmem],
-        out_specs=(vmem, vmem),
-        scratch_shapes=[
-            pltpu.SemaphoreType.DMA((2,)),
-            pltpu.SemaphoreType.DMA((2 * row_types,)),
-            pltpu.SemaphoreType.DMA((2 * col_types,)),
-        ],
-        compiler_params=pltpu.CompilerParams(collective_id=0, has_side_effects=True),
-    )(rows, cols)
 
 
 DIRECTIONS = ((-1, -1), (-1, 0), (-1, 1), (0, -1), (0, 1), (1, -1), (1, 0), (1, 1))
@@ -282,7 +175,7 @@
 
 def step_kernel(
     row_pad, col_pad, fields_ref, coefs_ref, rows_ref, cols_ref, frac_ref, trig_ref,
-    out_ref, row_out, col_out, row_send, col_send, send_sem, row_sem, col_sem,
+    out_ref, final_ref, row_out, col_out, row_send, col_send, send_sem, row_sem, col_sem,
 ):
     panel = lax.axis_index("panel")
     colat = lax.axis_index("colat")
@@ -365,6 +258,8 @@
         return carry
 
     lax.fori_loop(0, ext_rows, body, 0)
+    for field in range(4):
+        final_ref[field] = out_ref[field, pl.ds(1, height), pl.ds(lead, breadth), :]
 
     slots = rows_ref.shape[0]
     column = lax.broadcasted_iota(jnp.int32, (span, radial_len), 0)
@@ -431,6 +326,41 @@
                 device_id=col_sender(slot), device_id_type=MESH,
             ).wait_recv()
 
+    col_share = col_out.shape[2]
+
+    def put_columns(first, second):
+        for slot in range(2 * col_types):
+            column = first if slot < col_types else second
+            base = (slot % col_types) * col_share
+            for field in range(4):
+                for offset in range(col_share):
+                    final_ref[field, base + offset, pl.ds(column, 1), :] = (
+                        col_out[slot, field, pl.ds(offset, 1), :]
+                    )
+
+    def put_rows(first, second):
+        for slot in range(2 * row_types):
+            line = first if slot < row_types else second
+            base = (slot % row_types) * row_share
+            for field in range(4):
+                final_ref[field, line, pl.ds(base, row_share), :] = row_out[slot, field]
+
+    @pl.when(lon == 0)
+    def _():
+        put_columns(0, 1)
+
+    @pl.when(lon == lon_count - 1)
+    def _():
+        put_columns(breadth - 1, breadth - 2)
+
+    @pl.when(colat == 0)
+    def _():
+        put_rows(0, 1)
+
+    @pl.when(colat == colat_count - 1)
+    def _():
+        put_rows(height - 1, height - 2)
+
 
 def stepped(fields_pad, coefs_pad, row_pad, col_pad, lead, rows, cols, frac, trig, row_share):
     height = coefs_pad.shape[1] - 2
@@ -447,11 +377,12 @@
         functools.partial(step_kernel, row_pad, col_pad),
         out_shape=(
             jax.ShapeDtypeStruct((4, height + 2, span, radial_len), dtype),
+            jax.ShapeDtypeStruct((4, height, breadth, radial_len), dtype),
             jax.ShapeDtypeStruct((2 * row_types, 4, row_share, radial_len), dtype),
             jax.ShapeDtypeStruct((2 * col_types, 4, slots - row_share, radial_len), dtype),
         ),
         in_specs=[vmem, vmem, smem, smem, smem, smem],
-        out_specs=(vmem, vmem, vmem),
+        out_specs=(vmem, vmem, vmem, vmem),
         scratch_shapes=[
             pltpu.VMEM((4, row_share, radial_len), dtype),
             pltpu.VMEM((4, slots - row_share, radial_len), dtype),
@@ -502,31 +433,10 @@
     angles = rim_angle.reshape(-1)
     trig = jnp.stack([jnp.cos(angles), jnp.sin(angles)])
     frac = donor_offset.reshape(2, -1)
-    extended, row_buf, col_buf = stepped(
+    extended, fresh, row_buf, col_buf = stepped(
         fields_pad, coefs_pad, 3, 8, lead, donor_row.reshape(-1), donor_column.reshape(-1),
         frac, trig, row_share,
     )
-    fresh = extended[:, 1 : 1 + height, lead : lead + breadth]
-    slot_count = donor_row.shape[-1]
-    col_share = slot_count - row_share
-    col_strip = col_buf.reshape(2, col_buf.shape[0] // 2, 4, col_share, radial_len)
-    col_strip = jnp.transpose(col_strip, (2, 0, 1, 3, 4)).reshape(4, 2, height, radial_len)
-    west_strip = jnp.transpose(col_strip, (0, 2, 1, 3))
-    east_strip = jnp.stack([col_strip[:, 1], col_strip[:, 0]], axis=2)
-    row_strip = row_buf.reshape(2, row_buf.shape[0] // 2, 4, row_share, radial_len)
-    row_strip = jnp.transpose(row_strip, (2, 0, 1, 3, 4)).reshape(4, 2, breadth, radial_len)
-    north_strip = row_strip
-    south_strip = jnp.stack([row_strip[:, 1], row_strip[:, 0]], axis=1)
-    gap_cols = jnp.zeros((4, height, breadth - 4, radial_len), fresh.dtype)
-    col_rim = jnp.concatenate([west_strip, gap_cols, east_strip], axis=2)
-    gap_rows = jnp.zeros((4, height - 4, breadth, radial_len), fresh.dtype)
-    row_rim = jnp.concatenate([north_strip, gap_rows, south_strip], axis=1)
-    row_ids = lax.broadcasted_iota(jnp.int32, (height, breadth), 0)
-    col_ids = lax.broadcasted_iota(jnp.int32, (height, breadth), 1)
-    use_col = ((lon_pos == 0) & (col_ids < 2)) | ((lon_pos == lon_count - 1) & (col_ids >= breadth - 2))
-    use_row = ((colat_pos == 0) & (row_ids < 2)) | ((colat_pos == colat_count - 1) & (row_ids >= height - 2))
-    fresh = jnp.where(use_col[None, :, :, None], col_rim, fresh)
-    fresh = jnp.where(use_row[None, :, :, None], row_rim, fresh)
     return fresh[:, None]
 
 

time: 45.2 us -> 43.3 us (0.958)
  other arithmetic: 4.19 us -> 1.58 us
  Pallas kernels: 35.8 us -> 36.3 us
    broadcast_in_dim x1 -> x0, other arithmetic: 2.64 us -> none  [local(): return fresh[:, None]]
    unnamed x6 -> x7, local copies, waits for them, and re-layouts: 0.01 us -> 2.27 us
    transpose x3 -> x0, local copies, waits for them, and re-layouts: 1.82 us -> none  [the longest x1 0.91 us: local(): jnp.transpose(row_strip, (2, 0, 1, 3, 4)).reshape(4, 2, breadth, radial_len)]
    pallas_call x1, Pallas kernels: 24 us -> 24.5 us  [stepped(): pl.pallas_call(functools.partial(step_kernel, row_pad, col_pad), out_shap...]
where the time goes in v6:
time: 43.3 us; the launch traced here: 43 us
  Pallas kernels  36.3 us (84%)
  local copies, waits for them, and re-layouts  5.14 us (12%)
  other arithmetic  1.58 us (4%)
    pallas_call x1, Pallas kernels, stepped(): pl.pallas_call(functools.partial(step_kernel, row_pad, col_pad), out_shap...  24.5 us
    pallas_call x1, Pallas kernels, halo_exchange(): pl.pallas_call(functools.partial(halo_kernel, width, margins), out_shape=...  11.8 us
    pad x1, local copies, waits for them, and re-layouts, halo_exchange(): jnp.pad(fields, ((0, 0), (width, width), (lane_pad, lane_pad), (0, 0)))  2.83 us
    unnamed x7, local copies, waits for them, and re-layouts  2.27 us
    concatenate x1, other arithmetic, local(): coefs = jnp.concatenate([thermal[None], viscous[None]], axis=0)  1.01 us

profile of v6, /device:TPU:6, one launch (start us, length us, event | category | flops | bytes accessed | tf_op | source)
XLA Modules:
  0.0 43.0 jit_solution(1064164424695999314)
XLA Ops:
  0.0 0.0 copy-start
  0.0 0.0 copy-start.1
  0.0 2.8 %pad.8.fields_in = f32[4,22,48,128]{3,2,1,0:T(8,128)} pad(f32[4,16,32,128]{3,2,1,0:T(8,128)} %bitcast.11, f32[]{:T(128)} %constant.2.clone.1), padding=0_0x3_3x8_8x0_0 | pad | bytes 3211268 | tf_op jit(solution)/shard_map/jit(_pad)/pad | solution.py:138
  2.8 0.0 copy-done
  2.8 0.0 copy-done.1
  2.8 0.0 copy-start.2
  2.8 1.0 %select_maximum_fusion.coefs_in = f32[2,18,48,128]{3,2,1,0:T(8,128)} fusion(f32[1,16,32,128]{3,2,1,0:T(8,128)S(1)} %copy-done, f32[1,16,32,128]{3,2,1,0:T(8,128)S(1)} %copy-done.1), kind=kLoop, calls=%fused_computation.4 | loop fusion | flops 2654208 | bytes 1409024 | tf_op jit(solution)/shard_map/concatenate | solution.py:430
  3.8 11.8 %shard_map.73 = (f32[4,22,48,128]{3,2,1,0:T(8,128)}, f32[2,18,48,128]{3,2,1,0:T(8,128)}) custom-call(f32[4,22,48,128]{3,2,1,0:T(8,128)} %pad.8.fields_in, f32[2,18,48,128]{3,2,1,0:T(8,128)} %select_maximum_fusion.coefs_in), custom_call_target="tpu_custom_call", output_to_operand_aliasing={{0}: (0, {}), {1}: (1, {})} | custom-call | tf_op jit(solution)/shard_map/pallas_call | solution.py:142
  15.7 0.0 copy-done.2
  15.7 0.6 %pad_maximum_fusion.trig_ref = f32[2,12]{1,0:T(2,128)} fusion(f32[1,12]{1,0:T(1,128)S(1)} %get-tuple-element.12, f32[1,12]{1,0:T(1,128)S(1)} %get-tuple-element.11), kind=kLoop, calls=%fused_computation.8 | loop fusion | flops 24 | bytes 192 | tf_op jit(solution)/shard_map/stack | solution.py:434
  16.3 24.5 %shard_map.74 = (f32[4,18,40,128]{3,2,1,0:T(8,128)}, f32[4,16,32,128]{3,2,1,0:T(8,128)}, f32[8,4,8,128]{3,2,1,0:T(8,128)}, f32[8,4,4,128]{3,2,1,0:T(4,128)}) custom-call(f32[4,22,48,128]{3,2,1,0:T(8,128)} %get-tuple-element.8.fields_ref, f32[2,18,48,128]{3,2,1,0:T(8,128)} %get-tuple-element.9.coefs_ref, s32[12]{0:T(128)} %bitcast.14, s32[12]{0:T(128)} %bitcast.15, ...), custom_call_target="tpu_custom_call" | custom-call | tf_op jit(solution)/shard_map/pallas_call | solution.py:376
  40.8 2.3 %copy.14 = f32[4,1,16,32,128]{4,3,2,1,0:T(8,128)} copy(f32[4,1,16,32,128]{4,3,2,1,0:T(8,128)} %bitcast.12) | data formatting | bytes 2097152
  (1 shorter events, 0.0 us)
Async XLA Ops:
  0.0 2.8 %copy-start = (f32[1,16,32,128]{3,2,1,0:T(8,128)S(1)}, f32[1,16,32,128]{3,2,1,0:T(8,128)}, u32[]{:S(2)}) copy-start(f32[1,16,32,128]{3,2,1,0:T(8,128)} %param.9) | copy-start | bytes 786436
  0.0 2.8 %copy-start.1 = (f32[1,16,32,128]{3,2,1,0:T(8,128)S(1)}, f32[1,16,32,128]{3,2,1,0:T(8,128)}, u32[]{:S(2)}) copy-start(f32[1,16,32,128]{3,2,1,0:T(8,128)} %param.8) | copy-start | bytes 786436
  2.8 12.8 %copy-start.2 = (f32[1,1,1,12]{3,2,1,0:T(1,128)S(1)}, f32[1,1,1,12]{3,2,1,0:T(1,128)}, u32[]{:S(2)}) copy-start(f32[1,1,1,12]{3,2,1,0:T(1,128)} %param.13) | copy-start | bytes 148

commit v7 on v6

--- a/solution.py
+++ b/solution.py
@@ -165,6 +165,14 @@
     return (16.0 * (stencil[3] + stencil[1]) - (stencil[4] + stencil[0]) - 30.0 * stencil[2]) / 12.0
 
 
+def slope(stencil):
+    return 8.0 * (stencil[3] - stencil[1]) - (stencil[4] - stencil[0])
+
+
+def spread(stencil):
+    return 16.0 * (stencil[3] + stencil[1]) - (stencil[4] + stencil[0]) - 30.0 * stencil[2]
+
+
 def shifted(block, step):
     size = block.shape[-1]
     lane = lax.broadcasted_iota(jnp.int32, block.shape, block.ndim - 1)
@@ -245,16 +253,17 @@
             along_lat = [load(field, offset - 2, 0) for offset in range(5)]
             along_lon = [load(field, 0, offset - 2) for offset in range(5)]
             along_rad = [shifted(center[field], offset - 2) for offset in range(5)]
-            laplace = curvature(along_rad) + curvature(along_lat) + curvature(along_lon)
+            laplace = spread(along_rad) + spread(along_lat) + spread(along_lon)
             transport = (
-                center[1] * gradient(along_rad)
-                + center[2] * gradient(along_lat)
-                + center[3] * gradient(along_lon)
+                center[1] * slope(along_rad)
+                + center[2] * slope(along_lat)
+                + center[3] * slope(along_lon)
             )
             change = (thermal if field == 0 else viscous) * laplace - transport
+            stepped_value = center[field] + (TIME_STEP / 12.0) * change
             if field == 1:
-                change = change + BUOYANCY * center[0]
-            out_ref[field, row] = jnp.where(ok, center[field] + TIME_STEP * change, 0.0)
+                stepped_value = stepped_value + (TIME_STEP * BUOYANCY) * center[0]
+            out_ref[field, row] = jnp.where(ok, stepped_value, 0.0)
         return carry
 
     lax.fori_loop(0, ext_rows, body, 0)

time: 43.3 us -> 43 us (level)
  no operation moved by 1% of the time
where the time goes in v7:
time: 43 us; the launch traced here: 42.7 us
  Pallas kernels  36 us (84%)
  local copies, waits for them, and re-layouts  5.14 us (12%)
  other arithmetic  1.58 us (4%)
    pallas_call x1, Pallas kernels, stepped(): pl.pallas_call(functools.partial(step_kernel, row_pad, col_pad), out_shap...  24.2 us
    pallas_call x1, Pallas kernels, halo_exchange(): pl.pallas_call(functools.partial(halo_kernel, width, margins), out_shape=...  11.8 us
    pad x1, local copies, waits for them, and re-layouts, halo_exchange(): jnp.pad(fields, ((0, 0), (width, width), (lane_pad, lane_pad), (0, 0)))  2.83 us
    unnamed x7, local copies, waits for them, and re-layouts  2.27 us
    concatenate x1, other arithmetic, local(): coefs = jnp.concatenate([thermal[None], viscous[None]], axis=0)  1.01 us

profile of v7, /device:TPU:6, one launch (start us, length us, event | category | flops | bytes accessed | tf_op | source)
XLA Modules:
  0.0 42.7 jit_solution(13905142917703272474)
XLA Ops:
  0.0 0.0 copy-start
  0.0 0.0 copy-start.1
  0.0 2.8 %pad.8.fields_in = f32[4,22,48,128]{3,2,1,0:T(8,128)} pad(f32[4,16,32,128]{3,2,1,0:T(8,128)} %bitcast.11, f32[]{:T(128)} %constant.2.clone.1), padding=0_0x3_3x8_8x0_0 | pad | bytes 3211268 | tf_op jit(solution)/shard_map/jit(_pad)/pad | solution.py:138
  2.8 0.0 copy-done
  2.8 0.0 copy-done.1
  2.8 0.0 copy-start.2
  2.8 1.0 %select_maximum_fusion.coefs_in = f32[2,18,48,128]{3,2,1,0:T(8,128)} fusion(f32[1,16,32,128]{3,2,1,0:T(8,128)S(1)} %copy-done, f32[1,16,32,128]{3,2,1,0:T(8,128)S(1)} %copy-done.1), kind=kLoop, calls=%fused_computation.4 | loop fusion | flops 2654208 | bytes 1409024 | tf_op jit(solution)/shard_map/concatenate | solution.py:439
  3.8 11.8 %shard_map.73 = (f32[4,22,48,128]{3,2,1,0:T(8,128)}, f32[2,18,48,128]{3,2,1,0:T(8,128)}) custom-call(f32[4,22,48,128]{3,2,1,0:T(8,128)} %pad.8.fields_in, f32[2,18,48,128]{3,2,1,0:T(8,128)} %select_maximum_fusion.coefs_in), custom_call_target="tpu_custom_call", output_to_operand_aliasing={{0}: (0, {}), {1}: (1, {})} | custom-call | tf_op jit(solution)/shard_map/pallas_call | solution.py:142
  15.7 0.0 copy-done.2
  15.7 0.6 %pad_maximum_fusion.trig_ref = f32[2,12]{1,0:T(2,128)} fusion(f32[1,12]{1,0:T(1,128)S(1)} %get-tuple-element.12, f32[1,12]{1,0:T(1,128)S(1)} %get-tuple-element.11), kind=kLoop, calls=%fused_computation.8 | loop fusion | flops 24 | bytes 192 | tf_op jit(solution)/shard_map/stack | solution.py:443
  16.3 24.2 %shard_map.74 = (f32[4,18,40,128]{3,2,1,0:T(8,128)}, f32[4,16,32,128]{3,2,1,0:T(8,128)}, f32[8,4,8,128]{3,2,1,0:T(8,128)}, f32[8,4,4,128]{3,2,1,0:T(4,128)}) custom-call(f32[4,22,48,128]{3,2,1,0:T(8,128)} %get-tuple-element.8.fields_ref, f32[2,18,48,128]{3,2,1,0:T(8,128)} %get-tuple-element.9.coefs_ref, s32[12]{0:T(128)} %bitcast.14, s32[12]{0:T(128)} %bitcast.15, ...), custom_call_target="tpu_custom_call" | custom-call | tf_op jit(solution)/shard_map/pallas_call | solution.py:385
  40.5 2.3 %copy.14 = f32[4,1,16,32,128]{4,3,2,1,0:T(8,128)} copy(f32[4,1,16,32,128]{4,3,2,1,0:T(8,128)} %bitcast.12) | data formatting | bytes 2097152
  (1 shorter events, 0.0 us)
Async XLA Ops:
  0.0 2.8 %copy-start = (f32[1,16,32,128]{3,2,1,0:T(8,128)S(1)}, f32[1,16,32,128]{3,2,1,0:T(8,128)}, u32[]{:S(2)}) copy-start(f32[1,16,32,128]{3,2,1,0:T(8,128)} %param.9) | copy-start | bytes 786436
  0.0 2.8 %copy-start.1 = (f32[1,16,32,128]{3,2,1,0:T(8,128)S(1)}, f32[1,16,32,128]{3,2,1,0:T(8,128)}, u32[]{:S(2)}) copy-start(f32[1,16,32,128]{3,2,1,0:T(8,128)} %param.8) | copy-start | bytes 786436
  2.8 12.8 %copy-start.2 = (f32[1,1,1,12]{3,2,1,0:T(1,128)S(1)}, f32[1,1,1,12]{3,2,1,0:T(1,128)}, u32[]{:S(2)}) copy-start(f32[1,1,1,12]{3,2,1,0:T(1,128)} %param.13) | copy-start | bytes 148

commit v8 on v7

--- a/solution.py
+++ b/solution.py
@@ -55,17 +55,28 @@
     return offset, length
 
 
-def halo_kernel(width, margins, fields_in, coefs_in, fields_out, coefs_out, send_sem, recv_sem):
-    del fields_in, coefs_in
+def halo_kernel(width, margins, fields_in, thermal_in, viscous_in, fields_out, coefs_out, send_sem, recv_sem):
     count = len(DIRECTIONS)
     panel = lax.axis_index("panel")
     colat = lax.axis_index("colat")
     lon = lax.axis_index("lon")
     colat_count = lax.axis_size("colat")
     lon_count = lax.axis_size("lon")
-    height = fields_out.shape[1] - 2 * margins[0][0]
-    breadth = fields_out.shape[2] - 2 * margins[0][1]
-    layers = ((fields_out, width, margins[0]), (coefs_out, 1, margins[1]))
+    height, breadth = fields_in.shape[1], fields_in.shape[2]
+
+    for out, (row_pad, col_pad) in ((fields_out, margins[0]), (coefs_out, margins[1])):
+        lead = out.shape[:1]
+        total_rows, total_cols = out.shape[1], out.shape[2]
+        out[:, pl.ds(0, row_pad)] = jnp.zeros(lead + (row_pad, total_cols, out.shape[3]), out.dtype)
+        out[:, pl.ds(row_pad + height, row_pad)] = jnp.zeros(
+            lead + (row_pad, total_cols, out.shape[3]), out.dtype
+        )
+        side = jnp.zeros(lead + (height, col_pad, out.shape[3]), out.dtype)
+        out[:, pl.ds(row_pad, height), pl.ds(0, col_pad)] = side
+        out[:, pl.ds(row_pad, height), pl.ds(col_pad + breadth, total_cols - col_pad - breadth)] = side
+    fields_out[:, pl.ds(margins[0][0], height), pl.ds(margins[0][1], breadth)] = fields_in[...]
+    coefs_out[0, pl.ds(margins[1][0], height), pl.ds(margins[1][1], breadth)] = thermal_in[...]
+    coefs_out[1, pl.ds(margins[1][0], height), pl.ds(margins[1][1], breadth)] = viscous_in[...]
 
     def present(step):
         row = colat + step[0]
@@ -73,31 +84,38 @@
         inside = jnp.logical_and(row >= 0, row < colat_count)
         return jnp.logical_and(inside, jnp.logical_and(col >= 0, col < lon_count))
 
-    def region(ref, rows, cols):
-        return ref.at[:, pl.ds(rows[0], rows[1]), pl.ds(cols[0], cols[1]), :]
+    def source(part, step):
+        depth = width if part == 0 else 1
+        rows = window(step[0], depth, height, 0)
+        cols = window(step[1], depth, breadth, 0)
+        ref = (fields_in, thermal_in, viscous_in)[part]
+        if part == 0:
+            return ref.at[:, pl.ds(rows[0], rows[1]), pl.ds(cols[0], cols[1]), :]
+        return ref.at[pl.ds(rows[0], rows[1]), pl.ds(cols[0], cols[1]), :]
+
+    def target(part, step):
+        depth = width if part == 0 else 1
+        row_pad, col_pad = margins[0] if part == 0 else margins[1]
+        rows = landing(step[0], depth, height, row_pad)
+        cols = landing(step[1], depth, breadth, col_pad)
+        if part == 0:
+            return fields_out.at[:, pl.ds(rows[0], rows[1]), pl.ds(cols[0], cols[1]), :]
+        return coefs_out.at[part - 1, pl.ds(rows[0], rows[1]), pl.ds(cols[0], cols[1]), :]
 
     def outgoing(index, part):
         step = DIRECTIONS[index]
-        ref, depth, (row_pad, col_pad) = layers[part]
-        source = region(
-            ref, window(step[0], depth, height, row_pad), window(step[1], depth, breadth, col_pad)
-        )
-        target = region(
-            ref, landing(-step[0], depth, height, row_pad), landing(-step[1], depth, breadth, col_pad)
-        )
+        back = tuple(-s for s in step)
         return pltpu.make_async_remote_copy(
-            source, target, send_sem.at[index, part], recv_sem.at[count - 1 - index, part],
+            source(part, step), target(part, back),
+            send_sem.at[index, part], recv_sem.at[count - 1 - index, part],
             device_id=(panel, colat + step[0], lon + step[1]), device_id_type=MESH,
         )
 
     def incoming(index, part):
         step = DIRECTIONS[index]
-        ref, depth, (row_pad, col_pad) = layers[part]
-        target = region(
-            ref, landing(step[0], depth, height, row_pad), landing(step[1], depth, breadth, col_pad)
-        )
+        spot = target(part, step)
         return pltpu.make_async_remote_copy(
-            target, target, send_sem.at[index, part], recv_sem.at[index, part],
+            spot, spot, send_sem.at[index, part], recv_sem.at[index, part],
             device_id=(panel, colat + step[0], lon + step[1]), device_id_type=MESH,
         )
 
@@ -119,42 +137,41 @@
 
         @pl.when(present(step))
         def _():
-            outgoing(index, 0).start()
-            outgoing(index, 1).start()
+            for part in range(3):
+                outgoing(index, part).start()
 
     for index, step in enumerate(DIRECTIONS):
 
         @pl.when(present(step))
         def _():
-            outgoing(index, 0).wait_send()
-            outgoing(index, 1).wait_send()
-            incoming(index, 0).wait_recv()
-            incoming(index, 1).wait_recv()
-
-
-def halo_exchange(fields, coefs, width):
+            for part in range(3):
+                outgoing(index, part).wait_send()
+            for part in range(3):
+                incoming(index, part).wait_recv()
+
+
+def halo_exchange(fields, thermal, viscous, width):
     lane_pad = 8
+    height, breadth, radial_len = fields.shape[1], fields.shape[2], fields.shape[3]
     margins = ((width, lane_pad), (1, lane_pad))
-    fields_pad = jnp.pad(fields, ((0, 0), (width, width), (lane_pad, lane_pad), (0, 0)))
-    coefs_pad = jnp.pad(coefs, ((0, 0), (1, 1), (lane_pad, lane_pad), (0, 0)))
-    anywhere = pl.BlockSpec(memory_space=pl.ANY)
+    vmem = pl.BlockSpec(memory_space=pltpu.VMEM)
     count = len(DIRECTIONS)
-    fields_pad, coefs_pad = pl.pallas_call(
+    return pl.pallas_call(
         functools.partial(halo_kernel, width, margins),
         out_shape=(
-            jax.ShapeDtypeStruct(fields_pad.shape, fields_pad.dtype),
-            jax.ShapeDtypeStruct(coefs_pad.shape, coefs_pad.dtype),
+            jax.ShapeDtypeStruct(
+                (4, height + 2 * width, breadth + 2 * lane_pad, radial_len), fields.dtype
+            ),
+            jax.ShapeDtypeStruct((2, height + 2, breadth + 2 * lane_pad, radial_len), fields.dtype),
         ),
-        in_specs=[anywhere, anywhere],
-        out_specs=(anywhere, anywhere),
+        in_specs=[vmem, vmem, vmem],
+        out_specs=(vmem, vmem),
         scratch_shapes=[
-            pltpu.SemaphoreType.DMA((count, 2)),
-            pltpu.SemaphoreType.DMA((count, 2)),
+            pltpu.SemaphoreType.DMA((count, 3)),
+            pltpu.SemaphoreType.DMA((count, 3)),
         ],
-        input_output_aliases={0: 0, 1: 1},
         compiler_params=pltpu.CompilerParams(collective_id=1, has_side_effects=True),
-    )(fields_pad, coefs_pad)
-    return fields_pad, coefs_pad
+    )(fields, thermal, viscous)
 
 
 def gradient(stencil):
@@ -436,8 +453,7 @@
     colat_count = lax.axis_size("colat")
     lon_count = lax.axis_size("lon")
     row_share = 4 * breadth // colat_count
-    coefs = jnp.concatenate([thermal[None], viscous[None]], axis=0)
-    fields_pad, coefs_pad = halo_exchange(fields, coefs, 3)
+    fields_pad, coefs_pad = halo_exchange(fields, thermal, viscous, 3)
     lead = 4
     angles = rim_angle.reshape(-1)
     trig = jnp.stack([jnp.cos(angles), jnp.sin(angles)])

time: 43 us -> 42.7 us (level)
  Pallas kernels: 36 us -> 38.9 us
  local copies, waits for them, and re-layouts: 5.14 us -> 2.96 us
  other arithmetic: 1.58 us -> 0.58 us
    pallas_call x1, Pallas kernels: 11.8 us -> 14.8 us  [halo_exchange(): pl.pallas_call(functools.partial(halo_kernel, width, margins), out_shape=...]
    pad x1 -> x0, local copies, waits for them, and re-layouts: 2.83 us -> none  [halo_exchange(): jnp.pad(fields, ((0, 0), (width, width), (lane_pad, lane_pad), (0, 0)))]
    concatenate x1 -> x0, other arithmetic: 1.01 us -> none  [local(): coefs = jnp.concatenate([thermal[None], viscous[None]], axis=0)]
    cos x1, local copies, waits for them, and re-layouts: 0.04 us -> 0.69 us  [local(): trig = jnp.stack([jnp.cos(angles), jnp.sin(angles)])]
    unnamed x7 -> x1, local copies, waits for them, and re-layouts: 2.27 us -> 2.26 us
where the time goes in v8:
time: 42.7 us; the launch traced here: 42.5 us
  Pallas kernels  38.9 us (91%)
  local copies, waits for them, and re-layouts  2.96 us (7%)
  other arithmetic  0.58 us (1%)
    pallas_call x1, Pallas kernels, stepped(): pl.pallas_call(functools.partial(step_kernel, row_pad, col_pad), out_shap...  24.1 us
    pallas_call x1, Pallas kernels, halo_exchange(): pl.pallas_call(functools.partial(halo_kernel, width, margins), out_shape=...  14.8 us
    unnamed x1, local copies, waits for them, and re-layouts  2.26 us

profile of v8, /device:TPU:6, one launch (start us, length us, event | category | flops | bytes accessed | tf_op | source)
XLA Modules:
  0.0 42.5 jit_solution(13449757821678787346)
XLA Ops:
  0.0 0.7 %cosine_bitcast_fusion = (f32[1,12]{1,0:T(1,128)S(1)}, f32[1,12]{1,0:T(1,128)S(1)}) fusion(f32[1,1,1,12]{3,2,1,0:T(1,128)} %param.13), kind=kLoop, calls=%fused_computation.2 | loop fusion | bytes 144 | tf_op jit(solution)/shard_map/cos | solution.py:459
  0.7 0.6 %pad_maximum_fusion.trig_ref = f32[2,12]{1,0:T(2,128)} fusion(f32[1,12]{1,0:T(1,128)S(1)} %get-tuple-element.12, f32[1,12]{1,0:T(1,128)S(1)} %get-tuple-element.11), kind=kLoop, calls=%fused_computation | loop fusion | flops 24 | bytes 192 | tf_op jit(solution)/shard_map/stack | solution.py:459
  1.3 14.8 %shard_map.73 = (f32[4,22,48,128]{3,2,1,0:T(8,128)}, f32[2,18,48,128]{3,2,1,0:T(8,128)}) custom-call(f32[4,16,32,128]{3,2,1,0:T(8,128)} %bitcast.13, f32[16,32,128]{2,1,0:T(8,128)} %bitcast.15, f32[16,32,128]{2,1,0:T(8,128)} %bitcast.16), custom_call_target="tpu_custom_call" | custom-call | tf_op jit(solution)/shard_map/pallas_call | solution.py:159
  16.1 24.1 %shard_map.74 = (f32[4,18,40,128]{3,2,1,0:T(8,128)}, f32[4,16,32,128]{3,2,1,0:T(8,128)}, f32[8,4,8,128]{3,2,1,0:T(8,128)}, f32[8,4,4,128]{3,2,1,0:T(4,128)}) custom-call(f32[4,22,48,128]{3,2,1,0:T(8,128)} %get-tuple-element.8.fields_ref, f32[2,18,48,128]{3,2,1,0:T(8,128)} %get-tuple-element.9.coefs_ref, s32[12]{0:T(128)} %bitcast.18, s32[12]{0:T(128)} %bitcast.19, ...), custom_call_target="tpu_custom_call" | custom-call | tf_op jit(solution)/shard_map/pallas_call | solution.py:402
  40.2 2.3 %copy.10 = f32[4,1,16,32,128]{4,3,2,1,0:T(8,128)} copy(f32[4,1,16,32,128]{4,3,2,1,0:T(8,128)} %bitcast.14) | data formatting | bytes 2097152

commit v9 on v8

--- a/solution.py
+++ b/solution.py
@@ -87,7 +87,7 @@
     def source(part, step):
         depth = width if part == 0 else 1
         rows = window(step[0], depth, height, 0)
-        cols = window(step[1], depth, breadth, 0)
+        cols = window(step[1], margins[0][1], breadth, 0)
         ref = (fields_in, thermal_in, viscous_in)[part]
         if part == 0:
             return ref.at[:, pl.ds(rows[0], rows[1]), pl.ds(cols[0], cols[1]), :]
@@ -97,7 +97,7 @@
         depth = width if part == 0 else 1
         row_pad, col_pad = margins[0] if part == 0 else margins[1]
         rows = landing(step[0], depth, height, row_pad)
-        cols = landing(step[1], depth, breadth, col_pad)
+        cols = landing(step[1], col_pad, breadth, col_pad)
         if part == 0:
             return fields_out.at[:, pl.ds(rows[0], rows[1]), pl.ds(cols[0], cols[1]), :]
         return coefs_out.at[part - 1, pl.ds(rows[0], rows[1]), pl.ds(cols[0], cols[1]), :]

time: 42.7 us -> 43.9 us (1.028)
  Pallas kernels: 38.9 us -> 40.1 us
    pallas_call x1, Pallas kernels: 24.1 us -> 24.9 us  [stepped(): pl.pallas_call(functools.partial(step_kernel, row_pad, col_pad), out_shap...]
where the time goes in v9:
time: 43.9 us; the launch traced here: 43.7 us
  Pallas kernels  40.1 us (91%)
  local copies, waits for them, and re-layouts  2.96 us (7%)
  other arithmetic  0.58 us (1%)
    pallas_call x1, Pallas kernels, stepped(): pl.pallas_call(functools.partial(step_kernel, row_pad, col_pad), out_shap...  24.9 us
    pallas_call x1, Pallas kernels, halo_exchange(): pl.pallas_call(functools.partial(halo_kernel, width, margins), out_shape=...  15.2 us
    unnamed x1, local copies, waits for them, and re-layouts  2.26 us

profile of v9, /device:TPU:6, one launch (start us, length us, event | category | flops | bytes accessed | tf_op | source)
XLA Modules:
  0.0 43.7 jit_solution(13151465356049439619)
XLA Ops:
  0.0 0.7 %cosine_bitcast_fusion = (f32[1,12]{1,0:T(1,128)S(1)}, f32[1,12]{1,0:T(1,128)S(1)}) fusion(f32[1,1,1,12]{3,2,1,0:T(1,128)} %param.13), kind=kLoop, calls=%fused_computation.2 | loop fusion | bytes 144 | tf_op jit(solution)/shard_map/cos | solution.py:459
  0.7 0.6 %pad_maximum_fusion.trig_ref = f32[2,12]{1,0:T(2,128)} fusion(f32[1,12]{1,0:T(1,128)S(1)} %get-tuple-element.12, f32[1,12]{1,0:T(1,128)S(1)} %get-tuple-element.11), kind=kLoop, calls=%fused_computation | loop fusion | flops 24 | bytes 192 | tf_op jit(solution)/shard_map/stack | solution.py:459
  1.3 15.2 %shard_map.73 = (f32[4,22,48,128]{3,2,1,0:T(8,128)}, f32[2,18,48,128]{3,2,1,0:T(8,128)}) custom-call(f32[4,16,32,128]{3,2,1,0:T(8,128)} %bitcast.13, f32[16,32,128]{2,1,0:T(8,128)} %bitcast.15, f32[16,32,128]{2,1,0:T(8,128)} %bitcast.16), custom_call_target="tpu_custom_call" | custom-call | tf_op jit(solution)/shard_map/pallas_call | solution.py:159
  16.5 24.9 %shard_map.74 = (f32[4,18,40,128]{3,2,1,0:T(8,128)}, f32[4,16,32,128]{3,2,1,0:T(8,128)}, f32[8,4,8,128]{3,2,1,0:T(8,128)}, f32[8,4,4,128]{3,2,1,0:T(4,128)}) custom-call(f32[4,22,48,128]{3,2,1,0:T(8,128)} %get-tuple-element.8.fields_ref, f32[2,18,48,128]{3,2,1,0:T(8,128)} %get-tuple-element.9.coefs_ref, s32[12]{0:T(128)} %bitcast.18, s32[12]{0:T(128)} %bitcast.19, ...), custom_call_target="tpu_custom_call" | custom-call | tf_op jit(solution)/shard_map/pallas_call | solution.py:402
  41.4 2.3 %copy.10 = f32[4,1,16,32,128]{4,3,2,1,0:T(8,128)} copy(f32[4,1,16,32,128]{4,3,2,1,0:T(8,128)} %bitcast.14) | data formatting | bytes 2097152

commit v10 on v8

--- a/solution.py
+++ b/solution.py
@@ -151,7 +151,7 @@
 
 
 def halo_exchange(fields, thermal, viscous, width):
-    lane_pad = 8
+    lane_pad = 12
     height, breadth, radial_len = fields.shape[1], fields.shape[2], fields.shape[3]
     margins = ((width, lane_pad), (1, lane_pad))
     vmem = pl.BlockSpec(memory_space=pltpu.VMEM)
@@ -459,7 +459,7 @@
     trig = jnp.stack([jnp.cos(angles), jnp.sin(angles)])
     frac = donor_offset.reshape(2, -1)
     extended, fresh, row_buf, col_buf = stepped(
-        fields_pad, coefs_pad, 3, 8, lead, donor_row.reshape(-1), donor_column.reshape(-1),
+        fields_pad, coefs_pad, 3, 12, lead, donor_row.reshape(-1), donor_column.reshape(-1),
         frac, trig, row_share,
     )
     return fresh[:, None]

time: 42.7 us -> 43 us (level)
  no operation moved by 1% of the time
where the time goes in v10:
time: 43 us; the launch traced here: 42.8 us
  Pallas kernels  39.3 us (91%)
  local copies, waits for them, and re-layouts  2.96 us (7%)
  other arithmetic  0.58 us (1%)
    pallas_call x1, Pallas kernels, stepped(): pl.pallas_call(functools.partial(step_kernel, row_pad, col_pad), out_shap...  24.3 us
    pallas_call x1, Pallas kernels, halo_exchange(): pl.pallas_call(functools.partial(halo_kernel, width, margins), out_shape=...  15 us
    unnamed x1, local copies, waits for them, and re-layouts  2.26 us

profile of v10, /device:TPU:6, one launch (start us, length us, event | category | flops | bytes accessed | tf_op | source)
XLA Modules:
  0.0 42.8 jit_solution(6385183114700261224)
XLA Ops:
  0.0 0.7 %cosine_bitcast_fusion = (f32[1,12]{1,0:T(1,128)S(1)}, f32[1,12]{1,0:T(1,128)S(1)}) fusion(f32[1,1,1,12]{3,2,1,0:T(1,128)} %param.13), kind=kLoop, calls=%fused_computation.2 | loop fusion | bytes 144 | tf_op jit(solution)/shard_map/cos | solution.py:459
  0.7 0.6 %pad_maximum_fusion.trig_ref = f32[2,12]{1,0:T(2,128)} fusion(f32[1,12]{1,0:T(1,128)S(1)} %get-tuple-element.12, f32[1,12]{1,0:T(1,128)S(1)} %get-tuple-element.11), kind=kLoop, calls=%fused_computation | loop fusion | flops 24 | bytes 192 | tf_op jit(solution)/shard_map/stack | solution.py:459
  1.3 15.0 %shard_map.73 = (f32[4,22,56,128]{3,2,1,0:T(8,128)}, f32[2,18,56,128]{3,2,1,0:T(8,128)}) custom-call(f32[4,16,32,128]{3,2,1,0:T(8,128)} %bitcast.13, f32[16,32,128]{2,1,0:T(8,128)} %bitcast.15, f32[16,32,128]{2,1,0:T(8,128)} %bitcast.16), custom_call_target="tpu_custom_call" | custom-call | tf_op jit(solution)/shard_map/pallas_call | solution.py:159
  16.2 24.3 %shard_map.74 = (f32[4,18,40,128]{3,2,1,0:T(8,128)}, f32[4,16,32,128]{3,2,1,0:T(8,128)}, f32[8,4,8,128]{3,2,1,0:T(8,128)}, f32[8,4,4,128]{3,2,1,0:T(4,128)}) custom-call(f32[4,22,56,128]{3,2,1,0:T(8,128)} %get-tuple-element.8.fields_ref, f32[2,18,56,128]{3,2,1,0:T(8,128)} %get-tuple-element.9.coefs_ref, s32[12]{0:T(128)} %bitcast.18, s32[12]{0:T(128)} %bitcast.19, ...), custom_call_target="tpu_custom_call" | custom-call | tf_op jit(solution)/shard_map/pallas_call | solution.py:402
  40.6 2.3 %copy.10 = f32[4,1,16,32,128]{4,3,2,1,0:T(8,128)} copy(f32[4,1,16,32,128]{4,3,2,1,0:T(8,128)} %bitcast.14) | data formatting | bytes 2097152

commit v11 on v8

--- a/solution.py
+++ b/solution.py
@@ -200,7 +200,8 @@
 
 def step_kernel(
     row_pad, col_pad, fields_ref, coefs_ref, rows_ref, cols_ref, frac_ref, trig_ref,
-    out_ref, final_ref, row_out, col_out, row_send, col_send, send_sem, row_sem, col_sem,
+    out_ref, final_hbm, row_out, col_out, row_send, col_send, block_sem,
+    send_sem, row_sem, col_sem,
 ):
     panel = lax.axis_index("panel")
     colat = lax.axis_index("colat")
@@ -284,8 +285,10 @@
         return carry
 
     lax.fori_loop(0, ext_rows, body, 0)
-    for field in range(4):
-        final_ref[field] = out_ref[field, pl.ds(1, height), pl.ds(lead, breadth), :]
+    whole = pltpu.make_async_copy(
+        out_ref.at[:, pl.ds(1, height), pl.ds(lead, breadth), :], final_hbm, block_sem.at[0]
+    )
+    whole.start()
 
     slots = rows_ref.shape[0]
     column = lax.broadcasted_iota(jnp.int32, (span, radial_len), 0)
@@ -353,6 +356,7 @@
             ).wait_recv()
 
     col_share = col_out.shape[2]
+    whole.wait()
 
     def put_columns(first, second):
         for slot in range(2 * col_types):
@@ -360,7 +364,7 @@
             base = (slot % col_types) * col_share
             for field in range(4):
                 for offset in range(col_share):
-                    final_ref[field, base + offset, pl.ds(column, 1), :] = (
+                    out_ref[field, 1 + base + offset, pl.ds(lead + column, 1), :] = (
                         col_out[slot, field, pl.ds(offset, 1), :]
                     )
 
@@ -369,7 +373,7 @@
             line = first if slot < row_types else second
             base = (slot % row_types) * row_share
             for field in range(4):
-                final_ref[field, line, pl.ds(base, row_share), :] = row_out[slot, field]
+                out_ref[field, 1 + line, pl.ds(lead + base, row_share), :] = row_out[slot, field]
 
     @pl.when(lon == 0)
     def _():
@@ -386,6 +390,31 @@
     @pl.when(colat == colat_count - 1)
     def _():
         put_rows(height - 1, height - 2)
+
+    def patch(rows, cols):
+        part = pltpu.make_async_copy(
+            out_ref.at[:, pl.ds(1 + rows[0], rows[1]), pl.ds(lead + cols[0], cols[1]), :],
+            final_hbm.at[:, pl.ds(rows[0], rows[1]), pl.ds(cols[0], cols[1]), :],
+            block_sem.at[1],
+        )
+        part.start()
+        part.wait()
+
+    @pl.when(lon == 0)
+    def _():
+        patch((0, height), (0, 2))
+
+    @pl.when(lon == lon_count - 1)
+    def _():
+        patch((0, height), (breadth - 2, 2))
+
+    @pl.when(colat == 0)
+    def _():
+        patch((0, 2), (0, breadth))
+
+    @pl.when(colat == colat_count - 1)
+    def _():
+        patch((height - 2, 2), (0, breadth))
 
 
 def stepped(fields_pad, coefs_pad, row_pad, col_pad, lead, rows, cols, frac, trig, row_share):
@@ -408,10 +437,11 @@
             jax.ShapeDtypeStruct((2 * col_types, 4, slots - row_share, radial_len), dtype),
         ),
         in_specs=[vmem, vmem, smem, smem, smem, smem],
-        out_specs=(vmem, vmem, vmem, vmem),
+        out_specs=(vmem, pl.BlockSpec(memory_space=pl.ANY), vmem, vmem),
         scratch_shapes=[
             pltpu.VMEM((4, row_share, radial_len), dtype),
             pltpu.VMEM((4, slots - row_share, radial_len), dtype),
+            pltpu.SemaphoreType.DMA((2,)),
             pltpu.SemaphoreType.DMA((2,)),
             pltpu.SemaphoreType.DMA((2 * row_types,)),
             pltpu.SemaphoreType.DMA((2 * col_types,)),

time: 42.7 us -> 43 us (level)
  no operation moved by 1% of the time
where the time goes in v11:
time: 43 us; the launch traced here: 42.8 us
  Pallas kernels  39.2 us (91%)
  local copies, waits for them, and re-layouts  2.96 us (7%)
  other arithmetic  0.58 us (1%)
    pallas_call x1, Pallas kernels, stepped(): pl.pallas_call(functools.partial(step_kernel, row_pad, col_pad), out_shap...  24.4 us
    pallas_call x1, Pallas kernels, halo_exchange(): pl.pallas_call(functools.partial(halo_kernel, width, margins), out_shape=...  14.8 us
    unnamed x1, local copies, waits for them, and re-layouts  2.26 us

profile of v11, /device:TPU:6, one launch (start us, length us, event | category | flops | bytes accessed | tf_op | source)
XLA Modules:
  0.0 42.8 jit_solution(10950233196169248845)
XLA Ops:
  0.0 0.7 %cosine_bitcast_fusion = (f32[1,12]{1,0:T(1,128)S(1)}, f32[1,12]{1,0:T(1,128)S(1)}) fusion(f32[1,1,1,12]{3,2,1,0:T(1,128)} %param.13), kind=kLoop, calls=%fused_computation.2 | loop fusion | bytes 144 | tf_op jit(solution)/shard_map/cos | solution.py:489
  0.7 0.6 %pad_maximum_fusion.trig_ref = f32[2,12]{1,0:T(2,128)} fusion(f32[1,12]{1,0:T(1,128)S(1)} %get-tuple-element.12, f32[1,12]{1,0:T(1,128)S(1)} %get-tuple-element.11), kind=kLoop, calls=%fused_computation | loop fusion | flops 24 | bytes 192 | tf_op jit(solution)/shard_map/stack | solution.py:489
  1.3 14.8 %shard_map.73 = (f32[4,22,48,128]{3,2,1,0:T(8,128)}, f32[2,18,48,128]{3,2,1,0:T(8,128)}) custom-call(f32[4,16,32,128]{3,2,1,0:T(8,128)} %bitcast.13, f32[16,32,128]{2,1,0:T(8,128)} %bitcast.15, f32[16,32,128]{2,1,0:T(8,128)} %bitcast.16), custom_call_target="tpu_custom_call" | custom-call | tf_op jit(solution)/shard_map/pallas_call | solution.py:159
  16.1 24.4 %shard_map.74 = (f32[4,18,40,128]{3,2,1,0:T(8,128)}, f32[4,16,32,128]{3,2,1,0:T(8,128)}, f32[8,4,8,128]{3,2,1,0:T(8,128)}, f32[8,4,4,128]{3,2,1,0:T(4,128)}) custom-call(f32[4,22,48,128]{3,2,1,0:T(8,128)} %get-tuple-element.8.fields_ref, f32[2,18,48,128]{3,2,1,0:T(8,128)} %get-tuple-element.9.coefs_ref, s32[12]{0:T(128)} %bitcast.18, s32[12]{0:T(128)} %bitcast.19, ...), custom_call_target="tpu_custom_call" | custom-call | tf_op jit(solution)/shard_map/pallas_call | solution.py:431
  40.5 2.3 %copy.10 = f32[4,1,16,32,128]{4,3,2,1,0:T(8,128)} copy(f32[4,1,16,32,128]{4,3,2,1,0:T(8,128)} %bitcast.14) | data formatting | bytes 2097152

commit v12 on v8

--- a/solution.py
+++ b/solution.py
@@ -53,6 +53,15 @@
     if step > 0:
         return offset + length, width
     return offset, length
+
+
+def part_rank(step, part):
+    sides = abs(step[0]) + abs(step[1])
+    if part == 0 and step[1] == 0:
+        return 0
+    if part == 0 and sides == 1:
+        return 1
+    return 2 + part + sides
 
 
 def halo_kernel(width, margins, fields_in, thermal_in, viscous_in, fields_out, coefs_out, send_sem, recv_sem):
@@ -133,12 +142,15 @@
             )
 
     pl.semaphore_wait(barrier, expected)
-    for index, step in enumerate(DIRECTIONS):
-
-        @pl.when(present(step))
+    by_size = sorted(
+        ((index, part) for index in range(count) for part in range(3)),
+        key=lambda item: (part_rank(DIRECTIONS[item[0]], item[1]), item[0], item[1]),
+    )
+    for index, part in by_size:
+
+        @pl.when(present(DIRECTIONS[index]))
         def _():
-            for part in range(3):
-                outgoing(index, part).start()
+            outgoing(index, part).start()
 
     for index, step in enumerate(DIRECTIONS):
 

time: 42.7 us -> 42.9 us (level)
    pallas_call x1, Pallas kernels: 14.8 us -> 15.5 us  [halo_exchange(): pl.pallas_call(functools.partial(halo_kernel, width, margins), out_shape=...]
    pallas_call x1, Pallas kernels: 24.1 us -> 23.6 us  [stepped(): pl.pallas_call(functools.partial(step_kernel, row_pad, col_pad), out_shap...]
where the time goes in v12:
time: 42.9 us; the launch traced here: 42.7 us
  Pallas kernels  39.1 us (91%)
  local copies, waits for them, and re-layouts  2.96 us (7%)
  other arithmetic  0.58 us (1%)
    pallas_call x1, Pallas kernels, stepped(): pl.pallas_call(functools.partial(step_kernel, row_pad, col_pad), out_shap...  23.6 us
    pallas_call x1, Pallas kernels, halo_exchange(): pl.pallas_call(functools.partial(halo_kernel, width, margins), out_shape=...  15.5 us
    unnamed x1, local copies, waits for them, and re-layouts  2.26 us

profile of v12, /device:TPU:6, one launch (start us, length us, event | category | flops | bytes accessed | tf_op | source)
XLA Modules:
  0.0 42.7 jit_solution(9781049109912123028)
XLA Ops:
  0.0 0.7 %cosine_bitcast_fusion = (f32[1,12]{1,0:T(1,128)S(1)}, f32[1,12]{1,0:T(1,128)S(1)}) fusion(f32[1,1,1,12]{3,2,1,0:T(1,128)} %param.13), kind=kLoop, calls=%fused_computation.2 | loop fusion | bytes 144 | tf_op jit(solution)/shard_map/cos | solution.py:471
  0.7 0.6 %pad_maximum_fusion.trig_ref = f32[2,12]{1,0:T(2,128)} fusion(f32[1,12]{1,0:T(1,128)S(1)} %get-tuple-element.12, f32[1,12]{1,0:T(1,128)S(1)} %get-tuple-element.11), kind=kLoop, calls=%fused_computation | loop fusion | flops 24 | bytes 192 | tf_op jit(solution)/shard_map/stack | solution.py:471
  1.3 15.5 %shard_map.73 = (f32[4,22,48,128]{3,2,1,0:T(8,128)}, f32[2,18,48,128]{3,2,1,0:T(8,128)}) custom-call(f32[4,16,32,128]{3,2,1,0:T(8,128)} %bitcast.13, f32[16,32,128]{2,1,0:T(8,128)} %bitcast.15, f32[16,32,128]{2,1,0:T(8,128)} %bitcast.16), custom_call_target="tpu_custom_call" | custom-call | tf_op jit(solution)/shard_map/pallas_call | solution.py:171
  16.8 23.6 %shard_map.74 = (f32[4,18,40,128]{3,2,1,0:T(8,128)}, f32[4,16,32,128]{3,2,1,0:T(8,128)}, f32[8,4,8,128]{3,2,1,0:T(8,128)}, f32[8,4,4,128]{3,2,1,0:T(4,128)}) custom-call(f32[4,22,48,128]{3,2,1,0:T(8,128)} %get-tuple-element.8.fields_ref, f32[2,18,48,128]{3,2,1,0:T(8,128)} %get-tuple-element.9.coefs_ref, s32[12]{0:T(128)} %bitcast.18, s32[12]{0:T(128)} %bitcast.19, ...), custom_call_target="tpu_custom_call" | custom-call | tf_op jit(solution)/shard_map/pallas_call | solution.py:414
  40.4 2.3 %copy.10 = f32[4,1,16,32,128]{4,3,2,1,0:T(8,128)} copy(f32[4,1,16,32,128]{4,3,2,1,0:T(8,128)} %bitcast.14) | data formatting | bytes 2097152

commit v13 on v8

--- a/solution.py
+++ b/solution.py
@@ -284,8 +284,6 @@
         return carry
 
     lax.fori_loop(0, ext_rows, body, 0)
-    for field in range(4):
-        final_ref[field] = out_ref[field, pl.ds(1, height), pl.ds(lead, breadth), :]
 
     slots = rows_ref.shape[0]
     column = lax.broadcasted_iota(jnp.int32, (span, radial_len), 0)
@@ -333,6 +331,8 @@
     )
     row_copy.start()
     col_copy.start()
+    for field in range(4):
+        final_ref[field] = out_ref[field, pl.ds(1, height), pl.ds(lead, breadth), :]
     row_copy.wait_send()
     col_copy.wait_send()
 

time: 42.7 us -> 42.7 us (level)
  no operation moved by 1% of the time
where the time goes in v13:
time: 42.7 us; the launch traced here: 42.4 us
  Pallas kernels  38.9 us (91%)
  local copies, waits for them, and re-layouts  2.96 us (7%)
  other arithmetic  0.58 us (1%)
    pallas_call x1, Pallas kernels, stepped(): pl.pallas_call(functools.partial(step_kernel, row_pad, col_pad), out_shap...  24.1 us
    pallas_call x1, Pallas kernels, halo_exchange(): pl.pallas_call(functools.partial(halo_kernel, width, margins), out_shape=...  14.8 us
    unnamed x1, local copies, waits for them, and re-layouts  2.26 us

profile of v13, /device:TPU:6, one launch (start us, length us, event | category | flops | bytes accessed | tf_op | source)
XLA Modules:
  0.0 42.4 jit_solution(8741228542027285609)
XLA Ops:
  0.0 0.7 %cosine_bitcast_fusion = (f32[1,12]{1,0:T(1,128)S(1)}, f32[1,12]{1,0:T(1,128)S(1)}) fusion(f32[1,1,1,12]{3,2,1,0:T(1,128)} %param.13), kind=kLoop, calls=%fused_computation.2 | loop fusion | bytes 144 | tf_op jit(solution)/shard_map/cos | solution.py:459
  0.7 0.6 %pad_maximum_fusion.trig_ref = f32[2,12]{1,0:T(2,128)} fusion(f32[1,12]{1,0:T(1,128)S(1)} %get-tuple-element.12, f32[1,12]{1,0:T(1,128)S(1)} %get-tuple-element.11), kind=kLoop, calls=%fused_computation | loop fusion | flops 24 | bytes 192 | tf_op jit(solution)/shard_map/stack | solution.py:459
  1.3 14.8 %shard_map.73 = (f32[4,22,48,128]{3,2,1,0:T(8,128)}, f32[2,18,48,128]{3,2,1,0:T(8,128)}) custom-call(f32[4,16,32,128]{3,2,1,0:T(8,128)} %bitcast.13, f32[16,32,128]{2,1,0:T(8,128)} %bitcast.15, f32[16,32,128]{2,1,0:T(8,128)} %bitcast.16), custom_call_target="tpu_custom_call" | custom-call | tf_op jit(solution)/shard_map/pallas_call | solution.py:159
  16.1 24.1 %shard_map.74 = (f32[4,18,40,128]{3,2,1,0:T(8,128)}, f32[4,16,32,128]{3,2,1,0:T(8,128)}, f32[8,4,8,128]{3,2,1,0:T(8,128)}, f32[8,4,4,128]{3,2,1,0:T(4,128)}) custom-call(f32[4,22,48,128]{3,2,1,0:T(8,128)} %get-tuple-element.8.fields_ref, f32[2,18,48,128]{3,2,1,0:T(8,128)} %get-tuple-element.9.coefs_ref, s32[12]{0:T(128)} %bitcast.18, s32[12]{0:T(128)} %bitcast.19, ...), custom_call_target="tpu_custom_call" | custom-call | tf_op jit(solution)/shard_map/pallas_call | solution.py:402
  40.2 2.3 %copy.10 = f32[4,1,16,32,128]{4,3,2,1,0:T(8,128)} copy(f32[4,1,16,32,128]{4,3,2,1,0:T(8,128)} %bitcast.14) | data formatting | bytes 2097152
